TPU v7x, 128 devices: a whole 4x4x4 slice. The times are simulated.
128 devices in a mesh: row: 8 (over y, core), col: 16 (over z, x).
Axes of the slice: x: 4, y: 4, z: 4, core: 2. Of those that a mesh axis runs over, the one named last changes fastest.
Arguments:
- wavefunction: bfloat16 [32, 16, 256, 256], P('row', 'col'), may hold values from -6 to 6
- env_left: bfloat16 [16, 32, 2, 256, 256], P('col', 'row'), may hold values from -0.25 to 0.25
- left_src: int32 [16, 32, 2], P('col', 'row'), may hold values from 0 to 3
- two_site: bfloat16 [16, 16, 16], P('col'), may hold values from -1.5 to 1.5
- env_right: bfloat16 [16, 32, 256, 256], P('col', 'row'), may hold values from -0.09375 to 0.09375
- right_loc: int32 [32, 16], P('row', 'col'), may hold values from 0 to 3
- left_size: int32 [32], P('row'), may hold values from 128 to 256
- right_size: int32 [32], P('row'), may hold values from 128 to 256
Outputs:
- applied: bfloat16 [32, 16, 256, 256], P('row', 'col')
All inputs are finite; a program needn't handle non-finite values.
Results may differ from a plain program's by a relative error of at most 0.018.
Values may be sent and summed in bfloat16 or wider, within the bound.
No kernel may reach another device: no remote copies, remote signals or barrier semaphores. Data moves between devices by JAX's collectives and lax.ppermute only.
A program may use at most 128 MiB of HBM per device.

v0:
```python
import jax
import jax.numpy as jnp
from jax import lax
from jax.sharding import PartitionSpec as P


def per_device(
    wavefunction, env_left, left_src, two_site, env_right, right_loc, left_size, right_size
):
    whole, whole_loc = (
        lax.all_gather(wavefunction, "col", axis=1, tiled=True),
        lax.all_gather(right_loc, "col", axis=1, tiled=True),
    )
    local_tiles = wavefunction.shape[0]
    tile_width = wavefunction.shape[3]
    mixed_rows = []
    for position in range(local_tiles):
        blocks = whole[left_src[0, position]]
        left_part = jnp.einsum(
            "kxy,ksyz->sxz", env_left[0, position], blocks, preferred_element_type=jnp.float32
        ).astype(jnp.bfloat16)
        mixed_rows.append(
            jnp.einsum(
                "ts,sxz->txz", two_site[0], left_part, preferred_element_type=jnp.float32
            ).astype(jnp.bfloat16)
        )
    mixed = jnp.stack(mixed_rows)
    col_iota = lax.broadcasted_iota(jnp.int32, (1, 1, tile_width), 2)
    received, recv_loc = (
        lax.all_to_all(mixed, "row", split_axis=1, concat_axis=0, tiled=True),
        lax.all_to_all(whole_loc, "row", split_axis=1, concat_axis=0, tiled=True),
    )
    pieces = []
    for column in range(received.shape[1]):
        chosen = env_right[0][recv_loc[:, column]]
        product = jnp.einsum(
            "axy,azy->axz", received[:, column], chosen, preferred_element_type=jnp.float32
        )
        col_limit = right_size[recv_loc[:, column]]
        inside = col_iota < col_limit[:, None, None]
        pieces.append(jnp.where(inside, product, 0.0).astype(jnp.bfloat16))
    term = lax.all_to_all(jnp.stack(pieces, axis=1), "row", split_axis=0, concat_axis=1, tiled=True)
    summed = lax.psum_scatter(
        term.astype(jnp.float32).astype(jnp.bfloat16), "col", scatter_dimension=1, tiled=True
    ).astype(jnp.float32)
    row_iota = lax.broadcasted_iota(jnp.int32, summed.shape, 2)
    inside_rows = row_iota < left_size[:, None, None, None]
    return jnp.where(inside_rows, summed, 0.0).astype(jnp.bfloat16)


def solution(mesh):
    placed = (
        P("row", "col", None, None),
        P("col", "row", None, None, None),
        P("col", "row", None),
        P("col", None, None),
        P("col", "row", None, None),
        P("row", "col"),
        P("row"),
        P("row"),
    )
    return jax.shard_map(
        per_device,
        mesh=mesh,
        in_specs=placed,
        out_specs=P("row", "col", None, None),
        check_vma=False,
    )
```

profile of v0, /device:TPU:0, one launch (start us, length us, event | category | flops | bytes accessed | tf_op | source)
XLA Modules:
  0.0 595.9 jit_solution(1501007717909477833)
XLA Ops:
  6.5 0.0 all-gather.3.cloned.1.call-start
  6.5 0.7 all-gather.3.cloned.1.call-update
  7.3 22.0 %all-gather = s32[16,1,4]{2,1,0:T(1,128)S(1)} all-gather(s32[1,1,4]{2,1,0:T(1,128)} %bitcast.158), channel_id=1, replica_groups=mesh['row'=8,'col'=16] {'col'}, dimensions={0}, use_global_device_ids=true | all-gather | bytes 272 | tf_op jit(solution)/shard_map/all_gather | solution.py:12
  29.2 0.1 copy.30
  29.3 0.7 copy.31
  30.0 4.5 all-to-all-start
  34.5 1.0 slice_reduce_fusion.3
  35.6 47.3 %all-gather.3.cloned.1.call-done = bf16[4,16,256,256]{3,2,1,0:T(8,128)(2,1)} async-done(((bf16[4,1,256,256]{3,2,1,0:T(8,128)(2,1)}), bf16[4,16,256,256]{3,2,1,0:T(8,128)(2,1)}) %all-gather.3.cloned.1.call-update) | async-done | bytes 8388624 | tf_op jit(solution)/shard_map/all_gather | solution.py:11
  82.9 6.0 fusion.62
  88.9 2.9 gather_fusion.6
  91.8 4.2 gather_fusion.7
  96.0 4.2 gather_fusion.4
  100.2 4.2 gather_fusion.5
  104.4 4.2 gather_fusion.2
  108.6 4.2 gather_fusion.3
  112.8 4.2 gather_fusion.8
  117.0 4.2 gather_fusion.9
  121.2 2.4 copy.39
  123.6 4.1 copy.40
  127.7 4.2 fusion.34
  131.9 3.3 copy.41
  135.3 4.0 copy.36
  139.2 4.0 copy.37
  143.2 4.9 fusion.31
  148.1 4.6 copy.38
  152.7 2.1 convert_bitcast_fusion.1
  154.8 2.0 convert_bitcast_fusion.2
  156.8 3.9 copy.33
  160.7 2.4 copy.34
  163.1 4.9 fusion.28
  168.0 3.3 copy.35
  171.3 2.0 convert_bitcast_fusion.3
  173.3 4.1 copy.42
  177.4 2.4 copy.43
  179.8 4.9 fusion.37
  184.7 3.3 copy.44
  188.0 0.7 convert_bitcast_fusion
  188.7 0.9 copy-done.5
  189.6 0.6 copy-done.6
  190.3 5.7 pad_maximum_fusion
  196.0 9.6 %copy.45 = bf16[4,16,256,256]{3,2,0,1:T(8,128)(2,1)} copy(bf16[4,16,256,256]{3,1,2,0:T(8,128)(2,1)} %pad_maximum_fusion) | data formatting | bytes 16777216 | tf_op jit(solution)/shard_map/stack | solution.py:27
  205.6 0.0 all-to-all-done
  205.6 5.1 all-to-all-start.1
  210.7 0.0 all-reduce.3.cloned.1.call-start
  210.7 0.6 fusion.63
  211.4 0.1 all_to_all.43
  211.5 2.8 gather_fusion
  214.3 2.8 gather_fusion.1
  217.1 2.5 compare_select_fusion.9
  219.6 0.1 iota_compare_fusion.1
  219.6 85.7 %all-to-all-done.1 = bf16[4,16,256,256]{3,2,0,1:T(8,128)(2,1)} async-done(((bf16[4,16,256,256]{3,2,0,1:T(8,128)(2,1)}), bf16[4,16,256,256]{3,2,0,1:T(8,128)(2,1)}, u32[]{:S(2)}, u32[]{:S(2)}) %all-to-all-start.1) | async-done | bytes 8388640 | tf_op jit(solution)/shard_map/all_to_all | solution.py:30
  305.3 7.8 %copy.46 = bf16[4,8,2,256,256]{4,3,0,1,2:T(8,128)(2,1)} copy(bf16[4,8,2,256,256]{4,3,0,2,1:T(8,128)(2,1)} %bitcast.44) | data formatting | bytes 16777216 | tf_op jit(solution)/shard_map/all_to_all | solution.py:30
  313.1 5.8 fusion
  318.9 1.5 copy-done.7
  320.4 3.3 fusion.1
  323.7 6.2 %pad_maximum_fusion.1 = bf16[32,2,256,256]{3,2,0,1:T(8,128)(2,1)} fusion(bf16[32,1,256,256]{3,2,0,1:T(8,128)(2,1)} %fusion.1, bf16[32,1,256,256]{3,2,0,1:T(8,128)(2,1)S(1)} %copy-done.9), kind=kLoop, calls=%fused_computation.11 | loop fusion | flops 4194304 | bytes 16777216 | tf_op jit(solution)/shard_map/stack | solution.py:42
  329.9 7.6 %copy.47 = bf16[32,2,256,256]{3,2,1,0:T(8,128)(2,1)} copy(bf16[32,2,256,256]{3,2,0,1:T(8,128)(2,1)} %pad_maximum_fusion.1) | data formatting | bytes 16777216 | tf_op jit(solution)/shard_map/stack | solution.py:42
  337.5 101.6 %all_to_all.55 = bf16[32,2,256,256]{3,2,1,0:T(8,128)(2,1)} all-to-all(bf16[32,2,256,256]{3,2,1,0:T(8,128)(2,1)} %copy.47), channel_id=1, replica_groups=mesh['row'=8,'col'=16] {'row'}, dimensions={0} | all-to-all | bytes 16777216 | tf_op jit(solution)/shard_map/all_to_all | solution.py:42
  439.1 7.6 %copy.48 = bf16[4,8,2,256,256]{4,3,2,1,0:T(8,128)(2,1)} copy(bf16[4,8,2,256,256]{4,3,2,0,1:T(8,128)(2,1)} %bitcast.153) | data formatting | bytes 16777216 | tf_op jit(solution)/shard_map/all_to_all | solution.py:42
  446.8 0.0 all-reduce.3.cloned.1.call-update
  446.8 0.6 copy-done.14
  447.4 0.6 dynamic-slice
  448.0 138.4 %all-reduce.3.cloned.1.call-done = bf16[4,16,256,256]{3,2,1,0:T(8,128)(2,1)} async-done(((bf16[4,16,256,256]{3,2,1,0:T(8,128)(2,1)}), bf16[4,16,256,256]{3,2,1,0:T(8,128)(2,1)}) %all-reduce.3.cloned.1.call-update) | async-done | bytes 8388624
  586.4 2.7 select_convert_fusion.2
  (35 shorter events, 0.1 us)
Async XLA Ops:
  6.5 205.0 %copy-start = (bf16[1,4,256,256]{3,2,1,0:T(8,128)(2,1)S(1)}, bf16[1,4,256,256]{3,2,1,0:T(8,128)(2,1)}, u32[]{:S(2)}) copy-start(bf16[1,4,256,256]{3,2,1,0:T(8,128)(2,1)} %param.12) | copy-start | bytes 1572868
  6.5 76.4 %all-gather.3.cloned.1.call-start = ((), (), s32[]{:S(2)}) async-start(), calls=%async_computation.3 | async-start | bytes 8912896 | tf_op jit(solution)/shard_map/all_gather | solution.py:11
  30.0 175.6 %all-to-all-start = ((s32[4,8,2]{0,2,1:T(2,128)}), s32[4,8,2]{0,2,1:T(2,128)S(1)}, u32[]{:S(2)}, u32[]{:S(2)}) async-start(s32[4,8,2]{0,2,1:T(2,128)} %bitcast.3), calls=%async_computation | async-start | bytes 16384 | tf_op jit(solution)/shard_map/all_to_all | solution.py:31
  123.6 4.1 copy-start.10
  148.1 4.6 copy-start.11
  152.7 2.1 copy-start.1
  154.7 6.0 %copy-start.4 = (bf16[2,16,128,256]{3,2,1,0:T(8,128)(2,1)S(1)}, bf16[2,16,128,256]{3,2,1,0:T(8,128)(2,1)}, u32[]{:S(2)}) copy-start(bf16[2,16,128,256]{3,2,1,0:T(8,128)(2,1)} %gather_fusion.3) | copy-start | bytes 6291460
  173.3 4.1 copy-start.3
  188.0 1.6 copy-start.5
  188.0 2.2 copy-start.6
  205.6 5.1 copy-start.12
  205.6 99.7 %all-to-all-start.1 = ((bf16[4,16,256,256]{3,2,0,1:T(8,128)(2,1)}), bf16[4,16,256,256]{3,2,0,1:T(8,128)(2,1)}, u32[]{:S(2)}, u32[]{:S(2)}) async-start(bf16[4,16,256,256]{3,2,0,1:T(8,128)(2,1)} %copy.45), calls=%async_computation.1 | async-start | bytes 16777216 | tf_op jit(solution)/shard_map/all_to_all | solution.py:30
  210.7 375.7 %all-reduce.3.cloned.1.call-start = ((), (), s32[]{:S(2)}) async-start(), calls=%async_computation.4 | async-start | bytes 16777216
  305.3 7.8 %copy-start.8 = (bf16[32,256,256]{2,1,0:T(8,128)(2,1)S(1)}, bf16[32,256,256]{2,1,0:T(8,128)(2,1)}, u32[]{:S(2)}) copy-start(bf16[32,256,256]{2,1,0:T(8,128)(2,1)} %gather_fusion) | copy-start | bytes 12582916
  313.1 5.8 copy-start.2
  313.1 7.3 %copy-start.7 = (bf16[32,256,256]{2,1,0:T(8,128)(2,1)S(1)}, bf16[32,256,256]{2,1,0:T(8,128)(2,1)}, u32[]{:S(2)}) copy-start(bf16[32,256,256]{2,1,0:T(8,128)(2,1)} %gather_fusion.1) | copy-start | bytes 12582916
  320.4 3.3 copy-start.9
  446.7 0.7 copy-start.14
  446.8 139.7 %copy-start.13 = (s32[4]{0:T(128)S(1)}, s32[4]{0:T(128)}, u32[]{:S(2)}) copy-start(s32[4]{0:T(128)} %param.14) | copy-start | bytes 52
Sparse Core Ops, SparseCore 0:
  9.5 73.3 all-gather.2
  446.9 139.4 all-reduce.2
where the time goes:
time: 598 us; the launch traced here: 596 us
  waiting for transfers between devices  272 us (45%)
  local copies, waits for them, and re-layouts  125 us (21%)
  blocking collectives  124 us (21%)
  matrix products  34.7 us (6%)
  other arithmetic  17.2 us (3%)
  between operations  13.6 us (2%)
  starting transfers between devices  9.58 us (2%)
    unnamed x3, waiting for transfers between devices  139 us
    all_to_all x1, blocking collectives, per_device(): lax.all_to_all(jnp.stack(pieces, axis=1), 'row', split_axis=0, concat_axi...  102 us
    all_to_all x1, waiting for transfers between devices, per_device(): lax.all_to_all(mixed, 'row', split_axis=1, concat_axis=0, tiled=True)  85.7 us
    gather x17, local copies, waits for them, and re-layouts, per_device(): blocks = whole[left_src[0, position]]  65.5 us
    all_gather x1, waiting for transfers between devices, per_device(): lax.all_gather(wavefunction, 'col', axis=1, tiled=True)  47.3 us
    all_gather x1, blocking collectives, per_device(): lax.all_gather(right_loc, 'col', axis=1, tiled=True)  22 us
    dot_general x4, matrix products, per_device(): jnp.einsum('kxy,ksyz->sxz', env_left[0, position], blocks, preferred_elem...  18.8 us
    convert_element_type x4, local copies, waits for them, and re-layouts, per_device(): left_part = jnp.einsum('kxy,ksyz->sxz', env_left[0, position], blocks, pr...  14.6 us
  transfers between devices with their start and end apart: 4, of which 3 were waited for; matrix products, arithmetic and copies ran while one was open for 22% of the time, Pallas kernels for 0%

commit v1 on v0

v1 whole, which is shorter than its diff:
```python
import functools

import jax
import jax.numpy as jnp
from jax import lax
from jax.experimental import pallas as pl
from jax.experimental.pallas import tpu as pltpu
from jax.sharding import PartitionSpec as P

BAND = 16


def apply_kernel(src_ref, loc_ref, x_ref, left_ref, mix_ref, right_ref, out_ref, part, mixed):
    a = pl.program_id(0)
    states, _, tile, _ = x_ref.shape
    per_group = states // right_ref.shape[0]
    for s in range(states):
        total = jnp.dot(
            left_ref[0, 0], x_ref[s, src_ref[a, 0]], preferred_element_type=jnp.float32
        )
        total += jnp.dot(
            left_ref[0, 1], x_ref[s, src_ref[a, 1]], preferred_element_type=jnp.float32
        )
        part[s] = total.astype(jnp.bfloat16)
    for band in range(tile // BAND):
        rows = pl.ds(band * BAND, BAND)
        stacked = part[:, rows, :].reshape(states * BAND, tile)
        product = jnp.dot(mix_ref[...], stacked, preferred_element_type=jnp.float32)
        mixed[:, rows, :] = product.astype(jnp.bfloat16).reshape(states, BAND, tile)
    for t in range(states):
        product = lax.dot_general(
            mixed[t],
            right_ref[t // per_group, loc_ref[a, t]],
            (((1,), (1,)), ((), ())),
            preferred_element_type=jnp.float32,
        )
        out_ref[t, 0] = product.astype(jnp.bfloat16)


def apply_terms(src, loc, x, left, mix, right):
    states, tiles, tile, _ = x.shape
    whole = lambda shape: pl.BlockSpec(
        shape, lambda a, *_: (0,) * len(shape), pipeline_mode=pl.Buffered(1)
    )
    return pl.pallas_call(
        apply_kernel,
        out_shape=jax.ShapeDtypeStruct((states, tiles, tile, tile), jnp.bfloat16),
        grid_spec=pltpu.PrefetchScalarGridSpec(
            num_scalar_prefetch=2,
            grid=(tiles,),
            in_specs=[
                whole(x.shape),
                pl.BlockSpec((1,) + left.shape[1:], lambda a, *_: (a, 0, 0, 0)),
                whole(mix.shape),
                whole(right.shape),
            ],
            out_specs=pl.BlockSpec((states, 1, tile, tile), lambda a, *_: (0, a, 0, 0)),
            scratch_shapes=[
                pltpu.VMEM((states, tile, tile), jnp.bfloat16),
                pltpu.VMEM((states, tile, tile), jnp.bfloat16),
            ],
        ),
        compiler_params=pltpu.CompilerParams(vmem_limit_bytes=50 << 20),
        name="apply_terms",
    )(src, loc, x, left, mix, right)


def per_device(
    wavefunction, env_left, left_src, two_site, env_right, right_loc, left_size, right_size
):
    tile = wavefunction.shape[3]
    whole = lax.all_gather(wavefunction[:, 0], "col", axis=0, tiled=False)
    row = lax.broadcasted_iota(jnp.int32, (1, tile, 1), 1)
    right = jnp.where(row < right_size[:, None, None], env_right[0], 0).astype(jnp.bfloat16)
    right = lax.all_gather(right, "row", axis=0, tiled=False)
    loc = lax.all_gather(right_loc, "col", axis=1, tiled=True)
    mix = jnp.kron(two_site[0], jnp.eye(BAND, dtype=jnp.bfloat16))
    terms = apply_terms(left_src[0], loc, whole, env_left[0], mix, right)
    summed = lax.psum_scatter(terms, "col", scatter_dimension=0, tiled=False)
    inside = row < left_size[:, None, None]
    return jnp.where(inside, summed, 0).astype(jnp.bfloat16)[:, None]


def solution(mesh):
    placed = (
        P("row", "col", None, None),
        P("col", "row", None, None, None),
        P("col", "row", None),
        P("col", None, None),
        P("col", "row", None, None),
        P("row", "col"),
        P("row"),
        P("row"),
    )
    return jax.shard_map(
        per_device,
        mesh=mesh,
        in_specs=placed,
        out_specs=P("row", "col", None, None),
        check_vma=False,
    )
```

time: 598 us -> 228 us (0.38)
  local copies, waits for them, and re-layouts: 125 us -> 3.69 us
  waiting for transfers between devices: 272 us -> 167 us
  blocking collectives: 124 us -> 22 us
  matrix products: 34.7 us -> 0 us
  Pallas kernels: 0 us -> 16.3 us
  other arithmetic: 17.2 us -> 5.71 us
  starting transfers between devices: 9.58 us -> 0.08 us
    all_to_all x1 -> x0, blocking collectives: 102 us -> none  [per_device(): lax.all_to_all(jnp.stack(pieces, axis=1), 'row', split_axis=0, concat_axi...]
    all_to_all x2 -> x0, waiting for transfers between devices: 85.7 us -> none  [the longest x1 85.7 us: per_device(): lax.all_to_all(mixed, 'row', split_axis=1, concat_axis=0, tiled=True)]
    gather x20 -> x0, local copies, waits for them, and re-layouts: 71.7 us -> none  [the longest x17 65.5 us: per_device(): blocks = whole[left_src[0, position]]]
    unnamed x3 -> x4, waiting for transfers between devices: 139 us -> 84.9 us
    all_gather x1 -> x2, waiting for transfers between devices: 47.3 us -> 82.3 us  [the longest x1 73 us: per_device(): whole = lax.all_gather(wavefunction[:, 0], 'col', axis=0, tiled=False)]
    dot_general x10 -> x0, matrix products: 34.7 us -> none  [the longest x4 18.8 us: per_device(): jnp.einsum('kxy,ksyz->sxz', env_left[0, position], blocks, preferred_elem...]
    another operation x2 -> x0, local copies, waits for them, and re-layouts: 17.2 us -> none  [the longest x1 9.63 us: per_device(): mixed = jnp.stack(mixed_rows)]
    pallas_call x0 -> x1, Pallas kernels: none -> 16.3 us  [apply_terms(): pl.pallas_call(apply_kernel, out_shape=jax.ShapeDtypeStruct((states, tile...]
  transfers between devices with their start and end apart: 4 -> 3, of which waited for: 3 -> 3; matrix products, arithmetic and copies ran while one was open for 22% -> 1% of each run, Pallas kernels for 0% -> 0%
where the time goes in v1:
time: 228 us
  waiting for transfers between devices  167 us (73%)
  blocking collectives  22 us (10%)
  Pallas kernels  16.3 us (7%)
  between operations  13.1 us (6%)
  other arithmetic  5.71 us (3%)
  local copies, waits for them, and re-layouts  3.69 us (2%)
    unnamed x4, waiting for transfers between devices  84.9 us
    all_gather x1, waiting for transfers between devices, per_device(): whole = lax.all_gather(wavefunction[:, 0], 'col', axis=0, tiled=False)  73 us
    all_gather x1, blocking collectives, per_device(): loc = lax.all_gather(right_loc, 'col', axis=1, tiled=True)  22 us
    pallas_call x1, Pallas kernels, apply_terms(): pl.pallas_call(apply_kernel, out_shape=jax.ShapeDtypeStruct((states, tile...  16.3 us
    all_gather x1, waiting for transfers between devices, per_device(): right = lax.all_gather(right, 'row', axis=0, tiled=False)  9.29 us
  transfers between devices with their start and end apart: 3, of which 3 were waited for; matrix products, arithmetic and copies ran while one was open for 1% of the time, Pallas kernels for 0%

profile of v1, /device:TPU:0, one launch (start us, length us, event | category | flops | bytes accessed | tf_op | source)
XLA Modules:
  0.0 228.0 jit_solution(13911786066514824237)
XLA Ops:
  6.5 0.0 all-gather.5.cloned.1.call-start
  6.5 0.7 iota_compare_fusion.1
  7.3 2.0 broadcast_select_fusion
  9.3 0.0 all-gather.5.cloned.1.call-update
  9.3 0.0 all-gather.7.cloned.1.call-start
  9.4 0.7 all-gather.7.cloned.1.call-update
  10.1 0.0 reduce-scatter.4.cloned.1.call-start
  10.1 0.8 broadcast_multiply_fusion
  11.0 1.0 mul.30.mix_ref
  12.0 22.0 %all-gather.1 = s32[16,1,4]{2,1,0:T(1,128)S(1)} all-gather(s32[1,1,4]{2,1,0:T(1,128)} %bitcast.22), channel_id=1, replica_groups=mesh['row'=8,'col'=16] {'col'}, dimensions={0}, use_global_device_ids=true | all-gather | bytes 272 | tf_op jit(solution)/shard_map/all_gather | solution.py:76
  33.9 0.1 copy.12
  34.0 0.8 copy.13.src_ref
  34.8 9.3 %all-gather.5.cloned.1.call-done.right_ref = bf16[8,4,256,256]{3,2,1,0:T(8,128)(2,1)} async-done(((bf16[1,4,256,256]{3,2,1,0:T(8,128)(2,1)}), bf16[8,4,256,256]{3,2,1,0:T(8,128)(2,1)}) %all-gather.5.cloned.1.call-update) | async-done | bytes 4194320 | tf_op jit(solution)/shard_map/all_gather | solution.py:75
  44.1 73.0 %all-gather.7.cloned.1.call-done = bf16[64,1,256,256]{3,2,1,0:T(8,128)(2,1)} async-done(((bf16[4,1,256,256]{3,2,1,0:T(8,128)(2,1)}), bf16[64,1,256,256]{3,2,1,0:T(8,128)(2,1)}) %all-gather.7.cloned.1.call-update) | async-done | bytes 8388624 | tf_op jit(solution)/shard_map/all_gather | solution.py:72
  117.0 0.0 copy-start
  117.0 1.2 copy-done
  118.3 16.3 %apply_terms.1 = bf16[16,4,256,256]{3,2,1,0:T(8,128)(2,1)} custom-call(s32[4,2]{1,0:T(4,128)S(1)} %copy.13.src_ref, s32[4,16]{1,0:T(4,128)S(1)} %bitcast.18, bf16[16,4,256,256]{3,2,1,0:T(8,128)(2,1)} %bitcast.19, bf16[4,2,256,256]{3,2,1,0:T(8,128)(2,1)S(1)} %bitcast.17, bf16[256,256]{1,0:T(8,128)(2,1)S(1)} %mul.30.mix_ref, ...), custom_call_target="tpu_custom_call" | custom-call | tf_op jit(solution)/shard_map/apply_terms/pallas_call | solution.py:45
  134.5 0.0 copy-start.1
  134.6 0.0 reduce-scatter.4.cloned.1.call-update
  134.6 0.6 copy-done.1
  135.2 0.1 iota_compare_fusion.2
  135.3 84.2 %reduce-scatter.4.cloned.1.call-done = bf16[1,4,256,256]{3,2,1,0:T(8,128)(2,1)} async-done(((bf16[16,4,256,256]{3,2,1,0:T(8,128)(2,1)}), bf16[1,4,256,256]{3,2,1,0:T(8,128)(2,1)}) %reduce-scatter.4.cloned.1.call-update) | async-done | bytes 524304
  219.5 2.0 fusion
  (1 shorter events, 0.0 us)
Async XLA Ops:
  6.5 37.5 %all-gather.5.cloned.1.call-start = ((), (), s32[]{:S(2)}) async-start(), calls=%async_computation.1 | async-start | bytes 4718592 | tf_op jit(solution)/shard_map/all_gather | solution.py:75
  9.3 107.7 %all-gather.7.cloned.1.call-start = ((), (), s32[]{:S(2)}) async-start(), calls=%async_computation.2 | async-start | bytes 8912896 | tf_op jit(solution)/shard_map/all_gather | solution.py:72
  10.1 209.4 %reduce-scatter.4.cloned.1.call-start = ((), (), s32[]{:S(2)}) async-start(), calls=%async_computation.3 | async-start | bytes 8912896
  117.0 1.2 copy-start
  134.5 0.7 copy-start.1
Sparse Core Ops, SparseCore 0:
  9.4 34.5 all-gather.4
  46.2 70.7 all-gather.6
  134.7 84.7 reduce-scatter.3

commit v2 on v0

v2 whole, which is shorter than its diff:
```python
import jax
import jax.numpy as jnp
from jax import lax
from jax.experimental import pallas as pl
from jax.experimental.pallas import tpu as pltpu
from jax.sharding import PartitionSpec as P

BAND = 16
RING = 4
OFFSETS = (0, -1, 1, 2)


def shift(value, dz, dx):
    pairs = []
    for device in range(RING * RING):
        z, x = device // RING, device % RING
        pairs.append((device, (z + dz) % RING * RING + (x + dx) % RING))
    return lax.ppermute(value, "col", pairs)


def along(axis, step):
    return (step, 0) if axis == "z" else (0, step)


def ring_gather(block, axis):
    half = block.shape[0] // 2
    low = shift(block, *along(axis, 1))
    high = shift(block, *along(axis, -1))
    far_low = shift(low[:half], *along(axis, 1))
    far_high = shift(high[half:], *along(axis, -1))
    return block, low, high, far_low, far_high


def add(*parts):
    total = parts[0].astype(jnp.float32)
    for part in parts[1:]:
        total += part.astype(jnp.float32)
    return total.astype(jnp.bfloat16)


def ring_reduce(own, low, high, far_low, far_high, axis):
    half = far_low.shape[0]
    up = shift(far_low, *along(axis, 1))
    down = shift(far_high, *along(axis, -1))
    high = jnp.concatenate([add(high[:half], up), high[half:]])
    low = jnp.concatenate([low[:half], add(low[half:], down)])
    return add(own, shift(high, *along(axis, 1)), shift(low, *along(axis, -1)))


def apply_kernel(src_ref, pick_ref, *refs):
    pieces, (left_ref, mix_ref, right_ref), refs = refs[:10], refs[10:13], refs[13:]
    outs, (x_ref, part, mixed, sem) = refs[:10], refs[10:]
    tile = left_ref.shape[-1]
    states = RING * RING

    copies = []
    for number in range(10):
        first, piece = number < 5, number % 5
        tiles = pl.ds(0 if first else 2, 2)
        inner = pl.ds(0 if piece < 4 else 2, 2 if piece >= 3 else 4)
        outer = min(piece, 3)
        place = (outer, inner) if first else (inner, outer)
        copies.append(
            pltpu.make_async_copy(pieces[number], x_ref.at[place + (tiles,)], sem.at[number])
        )
    for copy in copies:
        copy.start()
    for copy in copies:
        copy.wait()

    def product_for(a):
        for s in range(states):
            i, k = s // RING, s % RING
            total = jnp.dot(
                left_ref[a, 0], x_ref[i, k, src_ref[a, 0]], preferred_element_type=jnp.float32
            )
            total += jnp.dot(
                left_ref[a, 1], x_ref[i, k, src_ref[a, 1]], preferred_element_type=jnp.float32
            )
            part[s] = total.astype(jnp.bfloat16)
        for band in range(tile // BAND):
            rows = pl.ds(band * BAND, BAND)
            stacked = part[:, rows, :].reshape(states * BAND, tile)
            product = jnp.dot(mix_ref[...], stacked, preferred_element_type=jnp.float32)
            mixed[:, rows, :] = product.astype(jnp.bfloat16).reshape(states, BAND, tile)

    def store_for(a, first):
        outs_half = outs[:5] if first else outs[5:]
        for t in range(states):
            i, k = t // RING, t % RING
            outer, inner = (i, k) if first else (k, i)
            product = lax.dot_general(
                mixed[t],
                right_ref[pick_ref[a, t]],
                (((1,), (1,)), ((), ())),
                preferred_element_type=jnp.float32,
            ).astype(jnp.bfloat16)
            slot = a if first else a - 2
            if outer < 3:
                outs_half[outer][inner, slot] = product
            else:
                outs_half[3 + inner // 2][inner % 2, slot] = product

    for half in range(2):

        def body(step, carry):
            a = step + 2 * half
            product_for(a)
            store_for(a, half == 0)
            return carry

        lax.fori_loop(0, 2, body, 0)


def apply_terms(src, pick, pieces, left, mix, right):
    tile = left.shape[-1]
    out = lambda n: jax.ShapeDtypeStruct((n, 2, tile, tile), jnp.bfloat16)
    anywhere = pl.BlockSpec(memory_space=pl.ANY)
    vmem = pl.BlockSpec(memory_space=pltpu.VMEM)
    smem = pl.BlockSpec(memory_space=pltpu.SMEM)
    return pl.pallas_call(
        apply_kernel,
        out_shape=[out(RING)] * 3 + [out(2)] * 2 + [out(RING)] * 3 + [out(2)] * 2,
        in_specs=[smem, smem] + [anywhere] * 10 + [vmem] * 3,
        out_specs=[vmem] * 10,
        scratch_shapes=[
            pltpu.VMEM((RING, RING, 4, tile, tile), jnp.bfloat16),
            pltpu.VMEM((RING * RING, tile, tile), jnp.bfloat16),
            pltpu.VMEM((RING * RING, tile, tile), jnp.bfloat16),
            pltpu.SemaphoreType.DMA((10,)),
        ],
        compiler_params=pltpu.CompilerParams(vmem_limit_bytes=50 << 20),
        name="apply_terms",
    )(src, pick, *pieces, left, mix, right)


def per_device(
    wavefunction, env_left, left_src, two_site, env_right, right_loc, left_size, right_size
):
    tile = wavefunction.shape[3]
    states = two_site.shape[1]
    tiles = wavefunction.shape[0]
    z, x = lax.axis_index("col") // RING, lax.axis_index("col") % RING
    offsets = jnp.asarray(OFFSETS, jnp.int32)
    order = (
        ((z + offsets) % RING)[:, None] * RING + ((x + offsets) % RING)[None, :]
    ).reshape(states)

    row = lax.broadcasted_iota(jnp.int32, (1, tile, 1), 1)
    right = jnp.where(row < right_size[:, None, None], env_right[0], 0).astype(jnp.bfloat16)
    right = lax.all_gather(right, "row", axis=0, tiled=True)

    shard = wavefunction[:, 0]
    first = ring_gather(shard[:2], "x")
    second = ring_gather(shard[2:], "z")
    first = ring_gather(jnp.concatenate(first), "z")
    second = ring_gather(jnp.concatenate(second), "x")
    pieces = [p.reshape(-1, 2, tile, tile) for p in first + second]

    loc = lax.all_to_all(
        jnp.broadcast_to(right_loc[:, 0][None], (states, tiles)), "col", 0, 0, tiled=True
    )
    pick = ((order // 2 * 4)[:, None] + loc[order]).T
    mix = two_site[0][order][:, order]
    mix = jnp.kron(mix, jnp.eye(BAND, dtype=jnp.bfloat16))

    outs = apply_terms(left_src[0], pick, pieces, env_left[0], mix, right)
    own, low, high, far_low, far_high = outs[:5]
    sum_first = ring_reduce(own, low, high, far_low, far_high, "z")
    own, low, high, far_low, far_high = outs[5:]
    sum_second = ring_reduce(own, low, high, far_low, far_high, "x")

    def last(sums, axis):
        split = lambda v: v.reshape(2 * 2, tile // 2, tile)
        far = split(sums[3])
        return ring_reduce(
            split(sums[0]), split(sums[1]), split(sums[2]), far[:2], far[2:], axis
        ).reshape(2, tile, tile)

    summed = jnp.concatenate([last(sum_first, "x"), last(sum_second, "z")])
    inside = row < left_size[:, None, None]
    return jnp.where(inside, summed, 0).astype(jnp.bfloat16)[:, None]


def solution(mesh):
    placed = (
        P("row", "col", None, None),
        P("col", "row", None, None, None),
        P("col", "row", None),
        P("col", None, None),
        P("col", "row", None, None),
        P("row", "col"),
        P("row"),
        P("row"),
    )
    return jax.shard_map(
        per_device,
        mesh=mesh,
        in_specs=placed,
        out_specs=P("row", "col", None, None),
        check_vma=False,
    )
```

time: 598 us -> 160 us (0.27)
  waiting for transfers between devices: 272 us -> 46.6 us
  blocking collectives: 124 us -> 0 us
  local copies, waits for them, and re-layouts: 125 us -> 19.3 us
  starting transfers between devices: 9.58 us -> 55.6 us
  matrix products: 34.7 us -> 0 us
  Pallas kernels: 0 us -> 18 us
  other arithmetic: 17.2 us -> 6.36 us
    unnamed x3 -> x1, waiting for transfers between devices: 139 us -> 0.02 us
    all_to_all x1 -> x0, blocking collectives: 102 us -> none  [per_device(): lax.all_to_all(jnp.stack(pieces, axis=1), 'row', split_axis=0, concat_axi...]
    all_to_all x2 -> x1, waiting for transfers between devices: 85.7 us -> 0.01 us  [per_device(): lax.all_to_all(jnp.broadcast_to(right_loc[:, 0][None], (states, tiles)),...]
    gather x20 -> x6, local copies, waits for them, and re-layouts: 71.7 us -> 1.96 us  [the longest x4 1.32 us: per_device(): mix = two_site[0][order][:, order]]
    ppermute x0 -> x32, starting transfers between devices: none -> 52 us  [shift(): return lax.ppermute(value, 'col', pairs)]
    all_gather x1, waiting for transfers between devices: 47.3 us -> 0.01 us  [per_device(): right = lax.all_gather(right, 'row', axis=0, tiled=True)]
    ppermute x0 -> x32, waiting for transfers between devices: none -> 46.6 us  [shift(): return lax.ppermute(value, 'col', pairs)]
    dot_general x10 -> x0, matrix products: 34.7 us -> none  [the longest x4 18.8 us: per_device(): jnp.einsum('kxy,ksyz->sxz', env_left[0, position], blocks, preferred_elem...]
  transfers between devices with their start and end apart: 4 -> 34, of which waited for: 3 -> 12; matrix products, arithmetic and copies ran while one was open for 22% -> 13% of each run, Pallas kernels for 0% -> 0%
where the time goes in v2:
time: 160 us
  starting transfers between devices  55.6 us (35%)
  waiting for transfers between devices  46.6 us (29%)
  local copies, waits for them, and re-layouts  19.3 us (12%)
  Pallas kernels  18 us (11%)
  between operations  13.9 us (9%)
  other arithmetic  6.36 us (4%)
    ppermute x32, starting transfers between devices, shift(): return lax.ppermute(value, 'col', pairs)  52 us
    ppermute x32, waiting for transfers between devices, shift(): return lax.ppermute(value, 'col', pairs)  46.6 us
    pallas_call x1, Pallas kernels, apply_terms(): pl.pallas_call(apply_kernel, out_shape=[out(RING)] * 3 + [out(2)] * 2 + [...  18 us
    unnamed x37, local copies, waits for them, and re-layouts  6.1 us
    all_to_all x1, starting transfers between devices, per_device(): lax.all_to_all(jnp.broadcast_to(right_loc[:, 0][None], (states, tiles)),...  3.6 us
  transfers between devices with their start and end apart: 34, of which 12 were waited for; matrix products, arithmetic and copies ran while one was open for 13% of the time, Pallas kernels for 0%

profile of v2, /device:TPU:0, one launch (start us, length us, event | category | flops | bytes accessed | tf_op | source)
XLA Modules:
  0.0 159.7 jit_solution(10131719905883567186)
XLA Ops:
  6.5 0.8 iota_compare_fusion.1
  7.3 2.0 %bitcast_select_fusion = bf16[4,256,256]{2,1,0:T(8,128)(2,1)} fusion(bf16[1,4,256,256]{3,2,1,0:T(8,128)(2,1)} %param.13, pred[4,256]{1,0:T(4,128)(4,1)S(1)} %iota_compare_fusion.1), kind=kLoop, calls=%fused_computation.20 | loop fusion | flops 262144 | bytes 1049600 | tf_op jit(solution)/shard_map/jit(_where)/select_n | solution.py:150
  9.4 1.1 slice_bitcast_fusion
  10.5 2.1 %collective-permute-start.8 = (bf16[2,256,256]{2,1,0:T(8,128)(2,1)S(1)}, bf16[2,256,256]{2,1,0:T(8,128)(2,1)S(1)}, u32[]{:S(2)}, u32[]{:S(2)}) collective-permute-start(bf16[2,256,256]{2,1,0:T(8,128)(2,1)S(1)} %get-tuple-element.37), channel_id=1, source_target_pairs={{0,4},{1,5},{2,6},{3,7},{4,8},{5,9},{6,10},{7,11},{8,12},{9,13},{1... | collective-permute-start | bytes 786440 | tf_op jit(solution)/shard_map/ppermute | solution.py:18
  12.5 2.2 %collective-permute-start.9 = (bf16[2,256,256]{2,1,0:T(8,128)(2,1)S(1)}, bf16[2,256,256]{2,1,0:T(8,128)(2,1)S(1)}, u32[]{:S(2)}, u32[]{:S(2)}) collective-permute-start(bf16[2,256,256]{2,1,0:T(8,128)(2,1)S(1)} %get-tuple-element.37), channel_id=1, source_target_pairs={{0,12},{1,13},{2,14},{3,15},{4,0},{5,1},{6,2},{7,3},{8,4},{9,5},{1... | collective-permute-start | bytes 786440 | tf_op jit(solution)/shard_map/ppermute | solution.py:18
  14.7 1.5 collective-permute-start
  16.2 1.7 %collective-permute-start.1 = (bf16[2,256,256]{2,1,0:T(8,128)(2,1)S(1)}, bf16[2,256,256]{2,1,0:T(8,128)(2,1)S(1)}, u32[]{:S(2)}, u32[]{:S(2)}) collective-permute-start(bf16[2,256,256]{2,1,0:T(8,128)(2,1)S(1)} %get-tuple-element.38), channel_id=1, source_target_pairs={{0,3},{1,0},{2,1},{3,2},{4,7},{5,4},{6,5},{7,6},{8,11},{9,8},{10,9... | collective-permute-start | bytes 786440 | tf_op jit(solution)/shard_map/ppermute | solution.py:18
  18.0 0.8 constant_dynamic-update-slice_fusion.9
  18.8 2.1 %collective-permute-done.8 = bf16[2,256,256]{2,1,0:T(8,128)(2,1)S(1)} collective-permute-done((bf16[2,256,256]{2,1,0:T(8,128)(2,1)S(1)}, bf16[2,256,256]{2,1,0:T(8,128)(2,1)S(1)}, u32[]{:S(2)}, u32[]{:S(2)}) %collective-permute-start.8) | collective-permute-done | bytes 262176 | tf_op jit(solution)/shard_map/ppermute | solution.py:18
  21.1 3.3 %collective-permute-start.11 = (bf16[1,256,256]{2,1,0:T(8,128)(2,1)S(1)}, bf16[1,256,256]{2,1,0:T(8,128)(2,1)S(1)}, u32[]{:S(2)}, u32[]{:S(2)}) collective-permute-start(bf16[1,256,256]{2,1,0:T(8,128)(2,1)S(1)} %slice.201), channel_id=1, source_target_pairs={{0,12},{1,13},{2,14},{3,15},{4,0},{5,1},{6,2},{7,3},{8,4},{9,5},{1... | collective-permute-start | bytes 393224 | tf_op jit(solution)/shard_map/ppermute | solution.py:18
  24.4 1.6 collective-permute-start.2
  26.0 1.8 %collective-permute-start.3 = (bf16[1,256,256]{2,1,0:T(8,128)(2,1)S(1)}, bf16[1,256,256]{2,1,0:T(8,128)(2,1)S(1)}, u32[]{:S(2)}, u32[]{:S(2)}) collective-permute-start(bf16[1,256,256]{2,1,0:T(8,128)(2,1)S(1)} %slice.197), channel_id=1, source_target_pairs={{0,3},{1,0},{2,1},{3,2},{4,7},{5,4},{6,5},{7,6},{8,11},{9,8},{10,9... | collective-permute-start | bytes 393224 | tf_op jit(solution)/shard_map/ppermute | solution.py:18
  27.8 0.7 constant_dynamic-update-slice_fusion.8
  28.5 0.7 constant_dynamic-update-slice_fusion.7
  29.2 0.7 constant_dynamic-update-slice_fusion.3
  30.0 0.7 constant_dynamic-update-slice_fusion.2
  30.7 0.7 constant_dynamic-update-slice_fusion.6
  31.3 0.7 constant_dynamic-update-slice_fusion.5
  32.0 0.3 collective-permute-start.12
  32.3 3.0 %collective-permute-start.13 = (bf16[8,256,256]{2,1,0:T(8,128)(2,1)}, bf16[8,256,256]{2,1,0:T(8,128)(2,1)S(1)}, u32[]{:S(2)}, u32[]{:S(2)}) collective-permute-start(bf16[8,256,256]{2,1,0:T(8,128)(2,1)} %constant_dynamic-update-slice_fusion.5), channel_id=1, source_target_pairs={{0,3},{1,0},{2,1},{3,2},{4,7},{5,4},{6,5},{7,6},{8,11},{9,8},{10,9... | collective-permute-start | bytes 3145736 | tf_op jit(solution)/shard_map/ppermute | solution.py:18
  35.2 0.7 constant_dynamic-update-slice_fusion.1
  35.9 0.7 constant_dynamic-update-slice_fusion
  36.5 1.0 collective-permute-start.5
  37.6 1.0 collective-permute-start.4
  38.6 0.6 broadcast_in_dim.42
  39.2 3.6 %all-to-all-start = ((s32[16,1,4]{2,1,0:T(1,128)}), s32[16,1,4]{2,1,0:T(1,128)S(1)}, u32[]{:S(2)}, u32[]{:S(2)}) async-start(s32[16,1,4]{2,1,0:T(1,128)} %broadcast_in_dim.42), calls=%async_computation | async-start | bytes 16384 | tf_op jit(solution)/shard_map/all_to_all | solution.py:160
  43.1 13.6 %collective-permute-done.12 = bf16[8,256,256]{2,1,0:T(8,128)(2,1)S(1)} collective-permute-done((bf16[8,256,256]{2,1,0:T(8,128)(2,1)}, bf16[8,256,256]{2,1,0:T(8,128)(2,1)S(1)}, u32[]{:S(2)}, u32[]{:S(2)}) %collective-permute-start.12) | collective-permute-done | bytes 1048608 | tf_op jit(solution)/shard_map/ppermute | solution.py:18
  56.7 1.0 copy-done.1
  57.7 0.8 slice.202
  58.5 0.9 slice.203
  59.4 3.2 %collective-permute-start.15 = (bf16[4,256,256]{2,1,0:T(8,128)(2,1)}, bf16[4,256,256]{2,1,0:T(8,128)(2,1)}, u32[]{:S(2)}, u32[]{:S(2)}) collective-permute-start(bf16[4,256,256]{2,1,0:T(8,128)(2,1)} %slice.203), channel_id=1, source_target_pairs={{0,3},{1,0},{2,1},{3,2},{4,7},{5,4},{6,5},{7,6},{8,11},{9,8},{10,9... | collective-permute-start | bytes 1572872 | tf_op jit(solution)/shard_map/ppermute | solution.py:18
  62.7 0.9 slice.199
  63.6 0.6 collective-permute-start.7
  64.2 1.9 %slice.198 = bf16[4,256,256]{2,1,0:T(8,128)(2,1)} slice(bf16[8,256,256]{2,1,0:T(8,128)(2,1)} %collective-permute-done.4), slice={[0:4], [0:256], [0:256]} | slice | bytes 1048576 | tf_op jit(solution)/shard_map/slice | solution.py:29
  66.1 1.4 collective-permute-start.6
  67.5 0.6 gather_fusion.1
  68.1 0.6 gather_fusion.2
  69.0 1.0 mul.40.refs_11_
  70.1 0.6 gather_fusion
  70.7 0.3 collective-permute-done.14
  71.4 3.0 %collective-permute-done.7 = bf16[4,256,256]{2,1,0:T(8,128)(2,1)S(1)} collective-permute-done((bf16[4,256,256]{2,1,0:T(8,128)(2,1)}, bf16[4,256,256]{2,1,0:T(8,128)(2,1)S(1)}, u32[]{:S(2)}, u32[]{:S(2)}) %collective-permute-start.7) | collective-permute-done | bytes 524320 | tf_op jit(solution)/shard_map/ppermute | solution.py:18
  74.3 3.1 %collective-permute-done.6 = bf16[4,256,256]{2,1,0:T(8,128)(2,1)S(1)} collective-permute-done((bf16[4,256,256]{2,1,0:T(8,128)(2,1)}, bf16[4,256,256]{2,1,0:T(8,128)(2,1)S(1)}, u32[]{:S(2)}, u32[]{:S(2)}) %collective-permute-start.6) | collective-permute-done | bytes 524320 | tf_op jit(solution)/shard_map/ppermute | solution.py:18
  77.4 18.0 %apply_terms.1 = (bf16[4,2,256,256]{3,2,1,0:T(8,128)(2,1)}, bf16[4,2,256,256]{3,2,1,0:T(8,128)(2,1)}, bf16[4,2,256,256]{3,2,1,0:T(8,128)(2,1)}, bf16[2,2,256,256...) custom-call(s32[4,2]{1,0:T(4,128)S(1)} %copy.20.src_ref, ...), custom_call_target="tpu_custom_call" | custom-call | tf_op jit(solution)/shard_map/apply_terms/pallas_call | solution.py:121
  95.5 0.6 collective-permute-start.16
  96.1 2.7 %collective-permute-start.18 = (bf16[2,2,256,256]{3,2,1,0:T(8,128)(2,1)S(1)}, bf16[2,2,256,256]{3,2,1,0:T(8,128)(2,1)S(1)}, u32[]{:S(2)}, u32[]{:S(2)}) collective-permute-start(bf16[2,2,256,256]{3,2,1,0:T(8,128)(2,1)S(1)} %get-tuple-element.19), channel_id=1, source_target_pairs={{0,12},{1,13},{2,14},{3,15},{4,0},{5,1},{6,2},{7,3},{8,4},{9,5},{1... | collective-permute-start | bytes 1572872 | tf_op jit(solution)/shard_map/ppermute | solution.py:18
  98.8 1.2 slice.161
  99.9 1.1 slice.162
  101.1 3.3 %collective-permute-start.26 = (bf16[2,2,256,256]{3,2,1,0:T(8,128)(2,1)S(1)}, bf16[2,2,256,256]{3,2,1,0:T(8,128)(2,1)S(1)}, u32[]{:S(2)}, u32[]{:S(2)}) collective-permute-start(bf16[2,2,256,256]{3,2,1,0:T(8,128)(2,1)S(1)} %get-tuple-element.24), channel_id=1, source_target_pairs={{0,3},{1,0},{2,1},{3,2},{4,7},{5,4},{6,5},{7,6},{8,11},{9,8},{10,9... | collective-permute-start | bytes 1572872 | tf_op jit(solution)/shard_map/ppermute | solution.py:18
  104.5 3.2 %collective-permute-done.16 = bf16[2,2,256,256]{3,2,1,0:T(8,128)(2,1)S(1)} collective-permute-done((bf16[2,2,256,256]{3,2,1,0:T(8,128)(2,1)S(1)}, bf16[2,2,256,256]{3,2,1,0:T(8,128)(2,1)S(1)}, u32[]{:S(2)}, u32[]{:S(2)}) %collective-permute-start.16) | collective-permute-done | bytes 524320 | tf_op jit(solution)/shard_map/ppermute | solution.py:18
  108.3 3.3 %collective-permute-start.19 = (bf16[4,2,256,256]{3,2,1,0:T(8,128)(2,1)S(1)}, bf16[4,2,256,256]{3,2,1,0:T(8,128)(2,1)S(1)}, u32[]{:S(2)}, u32[]{:S(2)}) collective-permute-start(bf16[4,2,256,256]{3,2,1,0:T(8,128)(2,1)S(1)} %pad_maximum_fusion.1), channel_id=1, source_target_pairs={{0,12},{1,13},{2,14},{3,15},{4,0},{5,1},{6,2},{7,3},{8,4},{9,5},{1... | collective-permute-start | bytes 3145736 | tf_op jit(solution)/shard_map/ppermute | solution.py:18
  111.5 2.0 %collective-permute-done.24 = bf16[2,2,256,256]{3,2,1,0:T(8,128)(2,1)S(1)} collective-permute-done((bf16[2,2,256,256]{3,2,1,0:T(8,128)(2,1)S(1)}, bf16[2,2,256,256]{3,2,1,0:T(8,128)(2,1)S(1)}, u32[]{:S(2)}, u32[]{:S(2)}) %collective-permute-start.24) | collective-permute-done | bytes 524320 | tf_op jit(solution)/shard_map/ppermute | solution.py:18
  114.1 3.3 %collective-permute-start.27 = (bf16[4,2,256,256]{3,2,1,0:T(8,128)(2,1)S(1)}, bf16[4,2,256,256]{3,2,1,0:T(8,128)(2,1)S(1)}, u32[]{:S(2)}, u32[]{:S(2)}) collective-permute-start(bf16[4,2,256,256]{3,2,1,0:T(8,128)(2,1)S(1)} %pad_maximum_fusion.3), channel_id=1, source_target_pairs={{0,3},{1,0},{2,1},{3,2},{4,7},{5,4},{6,5},{7,6},{8,11},{9,8},{10,9... | collective-permute-start | bytes 3145736 | tf_op jit(solution)/shard_map/ppermute | solution.py:18
  117.4 11.0 %collective-permute-done.17 = bf16[4,2,256,256]{3,2,1,0:T(8,128)(2,1)S(1)} collective-permute-done((bf16[4,2,256,256]{3,2,1,0:T(8,128)(2,1)S(1)}, bf16[4,2,256,256]{3,2,1,0:T(8,128)(2,1)S(1)}, u32[]{:S(2)}, u32[]{:S(2)}) %collective-permute-start.17) | collective-permute-done | bytes 1048608 | tf_op jit(solution)/shard_map/ppermute | solution.py:18
  128.4 0.5 add_convert_fusion.1
  129.0 3.2 %collective-permute-start.22 = (bf16[2,128,256]{2,1,0:T(8,128)(2,1)S(1)}, bf16[2,128,256]{2,1,0:T(8,128)(2,1)S(1)}, u32[]{:S(2)}, u32[]{:S(2)}) collective-permute-start(bf16[2,128,256]{2,1,0:T(8,128)(2,1)S(1)} %bitcast.76), channel_id=1, source_target_pairs={{0,3},{1,0},{2,1},{3,2},{4,7},{5,4},{6,5},{7,6},{8,11},{9,8},{10,9... | collective-permute-start | bytes 393224 | tf_op jit(solution)/shard_map/ppermute | solution.py:18
  132.2 3.9 %collective-permute-done.25 = bf16[4,2,256,256]{3,2,1,0:T(8,128)(2,1)S(1)} collective-permute-done((bf16[4,2,256,256]{3,2,1,0:T(8,128)(2,1)S(1)}, bf16[4,2,256,256]{3,2,1,0:T(8,128)(2,1)S(1)}, u32[]{:S(2)}, u32[]{:S(2)}) %collective-permute-start.25) | collective-permute-done | bytes 1048608 | tf_op jit(solution)/shard_map/ppermute | solution.py:18
  136.2 0.4 add_convert_fusion
  136.6 0.3 collective-permute-start.28
  137.0 3.2 %collective-permute-start.30 = (bf16[2,128,256]{2,1,0:T(8,128)(2,1)S(1)}, bf16[2,128,256]{2,1,0:T(8,128)(2,1)S(1)}, u32[]{:S(2)}, u32[]{:S(2)}) collective-permute-start(bf16[2,128,256]{2,1,0:T(8,128)(2,1)S(1)} %bitcast.75), channel_id=1, source_target_pairs={{0,12},{1,13},{2,14},{3,15},{4,0},{5,1},{6,2},{7,3},{8,4},{9,5},{1... | collective-permute-start | bytes 393224 | tf_op jit(solution)/shard_map/ppermute | solution.py:18
  140.4 3.6 %collective-permute-start.23 = (bf16[4,128,256]{2,1,0:T(8,128)(2,1)S(1)}, bf16[4,128,256]{2,1,0:T(8,128)(2,1)S(1)}, u32[]{:S(2)}, u32[]{:S(2)}) collective-permute-start(bf16[4,128,256]{2,1,0:T(8,128)(2,1)S(1)} %pad_maximum_fusion.5), channel_id=1, source_target_pairs={{0,3},{1,0},{2,1},{3,2},{4,7},{5,4},{6,5},{7,6},{8,11},{9,8},{10,9... | collective-permute-start | bytes 786440 | tf_op jit(solution)/shard_map/ppermute | solution.py:18
  144.3 3.3 %collective-permute-start.31 = (bf16[4,128,256]{2,1,0:T(8,128)(2,1)S(1)}, bf16[4,128,256]{2,1,0:T(8,128)(2,1)S(1)}, u32[]{:S(2)}, u32[]{:S(2)}) collective-permute-start(bf16[4,128,256]{2,1,0:T(8,128)(2,1)S(1)} %pad_maximum_fusion.7), channel_id=1, source_target_pairs={{0,12},{1,13},{2,14},{3,15},{4,0},{5,1},{6,2},{7,3},{8,4},{9,5},{1... | collective-permute-start | bytes 786440 | tf_op jit(solution)/shard_map/ppermute | solution.py:18
  147.7 0.5 collective-permute-done.21
  148.3 3.4 %collective-permute-done.29 = bf16[4,128,256]{2,1,0:T(8,128)(2,1)S(1)} collective-permute-done((bf16[4,128,256]{2,1,0:T(8,128)(2,1)S(1)}, bf16[4,128,256]{2,1,0:T(8,128)(2,1)S(1)}, u32[]{:S(2)}, u32[]{:S(2)}) %collective-permute-start.29) | collective-permute-done | bytes 262176 | tf_op jit(solution)/shard_map/ppermute | solution.py:18
  151.9 1.0 maximum_select_fusion
  (105 shorter events, 3.4 us)
Async XLA Ops:
  6.5 60.9 %copy-start = (bf16[1,16,16]{2,1,0:T(8,128)(2,1)S(1)}, bf16[1,16,16]{2,1,0:T(8,128)(2,1)}, u32[]{:S(2)}) copy-start(bf16[1,16,16]{2,1,0:T(8,128)(2,1)} %param.12) | copy-start | bytes 1540
  6.5 11.4 %copy-start.4 = (bf16[4,1,256,256]{3,2,1,0:T(8,128)(2,1)S(1)}, bf16[4,1,256,256]{3,2,1,0:T(8,128)(2,1)}, u32[]{:S(2)}) copy-start(bf16[4,1,256,256]{3,2,1,0:T(8,128)(2,1)} %param.9) | copy-start | bytes 1572868
  6.5 70.9 %all-gather.2.cloned.1.call-start = ((), (), s32[]{:S(2)}) async-start(), calls=%async_computation.1 | async-start | bytes 4718592 | tf_op jit(solution)/shard_map/all_gather | solution.py:151
  10.5 10.5 %collective-permute-start.8 = (bf16[2,256,256]{2,1,0:T(8,128)(2,1)S(1)}, bf16[2,256,256]{2,1,0:T(8,128)(2,1)S(1)}, u32[]{:S(2)}, u32[]{:S(2)}) collective-permute-start(bf16[2,256,256]{2,1,0:T(8,128)(2,1)S(1)} %get-tuple-element.37), channel_id=1, source_target_pairs={{0,4},{1,5},{2,6},{3,7},{4,8},{5,9},{6,10},{7,11},{8,12},{9,13},{1... | collective-permute-start | bytes 786440 | tf_op jit(solution)/shard_map/ppermute | solution.py:18
  12.5 8.5 %collective-permute-start.9 = (bf16[2,256,256]{2,1,0:T(8,128)(2,1)S(1)}, bf16[2,256,256]{2,1,0:T(8,128)(2,1)S(1)}, u32[]{:S(2)}, u32[]{:S(2)}) collective-permute-start(bf16[2,256,256]{2,1,0:T(8,128)(2,1)S(1)} %get-tuple-element.37), channel_id=1, source_target_pairs={{0,12},{1,13},{2,14},{3,15},{4,0},{5,1},{6,2},{7,3},{8,4},{9,5},{1... | collective-permute-start | bytes 786440 | tf_op jit(solution)/shard_map/ppermute | solution.py:18
  14.7 9.6 %collective-permute-start = (bf16[2,256,256]{2,1,0:T(8,128)(2,1)S(1)}, bf16[2,256,256]{2,1,0:T(8,128)(2,1)S(1)}, u32[]{:S(2)}, u32[]{:S(2)}) collective-permute-start(bf16[2,256,256]{2,1,0:T(8,128)(2,1)S(1)} %get-tuple-element.38), channel_id=1, source_target_pairs={{0,1},{1,2},{2,3},{3,0},{4,5},{5,6},{6,7},{7,4},{8,9},{9,10},{10,1... | collective-permute-start | bytes 786440 | tf_op jit(solution)/shard_map/ppermute | solution.py:18
  16.2 9.7 %collective-permute-start.1 = (bf16[2,256,256]{2,1,0:T(8,128)(2,1)S(1)}, bf16[2,256,256]{2,1,0:T(8,128)(2,1)S(1)}, u32[]{:S(2)}, u32[]{:S(2)}) collective-permute-start(bf16[2,256,256]{2,1,0:T(8,128)(2,1)S(1)} %get-tuple-element.38), channel_id=1, source_target_pairs={{0,3},{1,0},{2,1},{3,2},{4,7},{5,4},{6,5},{7,6},{8,11},{9,8},{10,9... | collective-permute-start | bytes 786440 | tf_op jit(solution)/shard_map/ppermute | solution.py:18
  18.8 19.7 %copy-start.12 = (s32[4,1]{0,1:T(1,128)S(1)}, s32[4,1]{0,1:T(1,128)}, u32[]{:S(2)}) copy-start(s32[4,1]{0,1:T(1,128)} %param.14) | copy-start | bytes 52
  18.8 24.0 %copy-start.13 = (s32[4]{0:T(128)S(1)}, s32[4]{0:T(128)}, u32[]{:S(2)}) copy-start(s32[4]{0:T(128)} %constant.64.clone) | copy-start | bytes 52
  21.0 9.7 %collective-permute-start.10 = (bf16[1,256,256]{2,1,0:T(8,128)(2,1)S(1)}, bf16[1,256,256]{2,1,0:T(8,128)(2,1)S(1)}, u32[]{:S(2)}, u32[]{:S(2)}) collective-permute-start(bf16[1,256,256]{2,1,0:T(8,128)(2,1)S(1)} %slice.200), channel_id=1, source_target_pairs={{0,4},{1,5},{2,6},{3,7},{4,8},{5,9},{6,10},{7,11},{8,12},{9,13},{1... | collective-permute-start | bytes 393224 | tf_op jit(solution)/shard_map/ppermute | solution.py:18
  21.1 10.2 %collective-permute-start.11 = (bf16[1,256,256]{2,1,0:T(8,128)(2,1)S(1)}, bf16[1,256,256]{2,1,0:T(8,128)(2,1)S(1)}, u32[]{:S(2)}, u32[]{:S(2)}) collective-permute-start(bf16[1,256,256]{2,1,0:T(8,128)(2,1)S(1)} %slice.201), channel_id=1, source_target_pairs={{0,12},{1,13},{2,14},{3,15},{4,0},{5,1},{6,2},{7,3},{8,4},{9,5},{1... | collective-permute-start | bytes 393224 | tf_op jit(solution)/shard_map/ppermute | solution.py:18
  24.4 10.8 %collective-permute-start.2 = (bf16[1,256,256]{2,1,0:T(8,128)(2,1)S(1)}, bf16[1,256,256]{2,1,0:T(8,128)(2,1)S(1)}, u32[]{:S(2)}, u32[]{:S(2)}) collective-permute-start(bf16[1,256,256]{2,1,0:T(8,128)(2,1)S(1)} %slice.196), channel_id=1, source_target_pairs={{0,1},{1,2},{2,3},{3,0},{4,5},{5,6},{6,7},{7,4},{8,9},{9,10},{10,1... | collective-permute-start | bytes 393224 | tf_op jit(solution)/shard_map/ppermute | solution.py:18
  26.0 9.9 %collective-permute-start.3 = (bf16[1,256,256]{2,1,0:T(8,128)(2,1)S(1)}, bf16[1,256,256]{2,1,0:T(8,128)(2,1)S(1)}, u32[]{:S(2)}, u32[]{:S(2)}) collective-permute-start(bf16[1,256,256]{2,1,0:T(8,128)(2,1)S(1)} %slice.197), channel_id=1, source_target_pairs={{0,3},{1,0},{2,1},{3,2},{4,7},{5,4},{6,5},{7,6},{8,11},{9,8},{10,9... | collective-permute-start | bytes 393224 | tf_op jit(solution)/shard_map/ppermute | solution.py:18
  32.0 24.7 %collective-permute-start.12 = (bf16[8,256,256]{2,1,0:T(8,128)(2,1)}, bf16[8,256,256]{2,1,0:T(8,128)(2,1)S(1)}, u32[]{:S(2)}, u32[]{:S(2)}) collective-permute-start(bf16[8,256,256]{2,1,0:T(8,128)(2,1)} %constant_dynamic-update-slice_fusion.5), channel_id=1, source_target_pairs={{0,1},{1,2},{2,3},{3,0},{4,5},{5,6},{6,7},{7,4},{8,9},{9,10},{10,1... | collective-permute-start | bytes 3145736 | tf_op jit(solution)/shard_map/ppermute | solution.py:18
  32.3 26.3 %collective-permute-start.13 = (bf16[8,256,256]{2,1,0:T(8,128)(2,1)}, bf16[8,256,256]{2,1,0:T(8,128)(2,1)S(1)}, u32[]{:S(2)}, u32[]{:S(2)}) collective-permute-start(bf16[8,256,256]{2,1,0:T(8,128)(2,1)} %constant_dynamic-update-slice_fusion.5), channel_id=1, source_target_pairs={{0,3},{1,0},{2,1},{3,2},{4,7},{5,4},{6,5},{7,6},{8,11},{9,8},{10,9... | collective-permute-start | bytes 3145736 | tf_op jit(solution)/shard_map/ppermute | solution.py:18
  36.5 26.1 %collective-permute-start.5 = (bf16[8,256,256]{2,1,0:T(8,128)(2,1)}, bf16[8,256,256]{2,1,0:T(8,128)(2,1)S(1)}, u32[]{:S(2)}, u32[]{:S(2)}) collective-permute-start(bf16[8,256,256]{2,1,0:T(8,128)(2,1)} %constant_dynamic-update-slice_fusion), channel_id=1, source_target_pairs={{0,12},{1,13},{2,14},{3,15},{4,0},{5,1},{6,2},{7,3},{8,4},{9,5},{1... | collective-permute-start | bytes 3145736 | tf_op jit(solution)/shard_map/ppermute | solution.py:18
  37.6 26.6 %collective-permute-start.4 = (bf16[8,256,256]{2,1,0:T(8,128)(2,1)}, bf16[8,256,256]{2,1,0:T(8,128)(2,1)}, u32[]{:S(2)}, u32[]{:S(2)}) collective-permute-start(bf16[8,256,256]{2,1,0:T(8,128)(2,1)} %constant_dynamic-update-slice_fusion), channel_id=1, source_target_pairs={{0,4},{1,5},{2,6},{3,7},{4,8},{5,9},{6,10},{7,11},{8,12},{9,13},{1... | collective-permute-start | bytes 3145736 | tf_op jit(solution)/shard_map/ppermute | solution.py:18
  39.2 30.9 %all-to-all-start = ((s32[16,1,4]{2,1,0:T(1,128)}), s32[16,1,4]{2,1,0:T(1,128)S(1)}, u32[]{:S(2)}, u32[]{:S(2)}) async-start(s32[16,1,4]{2,1,0:T(1,128)} %broadcast_in_dim.42), calls=%async_computation | async-start | bytes 16384 | tf_op jit(solution)/shard_map/all_to_all | solution.py:160
  56.7 1.0 copy-start.1
  58.5 12.6 %collective-permute-start.14 = (bf16[4,256,256]{2,1,0:T(8,128)(2,1)}, bf16[4,256,256]{2,1,0:T(8,128)(2,1)S(1)}, u32[]{:S(2)}, u32[]{:S(2)}) collective-permute-start(bf16[4,256,256]{2,1,0:T(8,128)(2,1)} %slice.202), channel_id=1, source_target_pairs={{0,1},{1,2},{2,3},{3,0},{4,5},{5,6},{6,7},{7,4},{8,9},{9,10},{10,1... | collective-permute-start | bytes 1572872 | tf_op jit(solution)/shard_map/ppermute | solution.py:18
  58.5 4.1 %copy-start.2 = (bf16[8,256,256]{2,1,0:T(8,128)(2,1)}, bf16[8,256,256]{2,1,0:T(8,128)(2,1)S(1)}, u32[]{:S(2)}) copy-start(bf16[8,256,256]{2,1,0:T(8,128)(2,1)S(1)} %collective-permute-done.13) | copy-start | bytes 3145732
  59.4 10.5 %copy-start.11 = (s32[1,4,2]{1,2,0:T(2,128)S(1)}, s32[1,4,2]{1,2,0:T(2,128)}, u32[]{:S(2)}) copy-start(s32[1,4,2]{1,2,0:T(2,128)} %param.11) | copy-start | bytes 100
  59.4 11.9 %collective-permute-start.15 = (bf16[4,256,256]{2,1,0:T(8,128)(2,1)}, bf16[4,256,256]{2,1,0:T(8,128)(2,1)}, u32[]{:S(2)}, u32[]{:S(2)}) collective-permute-start(bf16[4,256,256]{2,1,0:T(8,128)(2,1)} %slice.203), channel_id=1, source_target_pairs={{0,3},{1,0},{2,1},{3,2},{4,7},{5,4},{6,5},{7,6},{8,11},{9,8},{10,9... | collective-permute-start | bytes 1572872 | tf_op jit(solution)/shard_map/ppermute | solution.py:18
  62.7 6.0 %copy-start.3 = (bf16[8,256,256]{2,1,0:T(8,128)(2,1)}, bf16[8,256,256]{2,1,0:T(8,128)(2,1)S(1)}, u32[]{:S(2)}) copy-start(bf16[8,256,256]{2,1,0:T(8,128)(2,1)S(1)} %collective-permute-done.5) | copy-start | bytes 3145732
  63.6 10.8 %collective-permute-start.7 = (bf16[4,256,256]{2,1,0:T(8,128)(2,1)}, bf16[4,256,256]{2,1,0:T(8,128)(2,1)S(1)}, u32[]{:S(2)}, u32[]{:S(2)}) collective-permute-start(bf16[4,256,256]{2,1,0:T(8,128)(2,1)} %slice.199), channel_id=1, source_target_pairs={{0,12},{1,13},{2,14},{3,15},{4,0},{5,1},{6,2},{7,3},{8,4},{9,5},{1... | collective-permute-start | bytes 1572872 | tf_op jit(solution)/shard_map/ppermute | solution.py:18
  66.1 11.4 %collective-permute-start.6 = (bf16[4,256,256]{2,1,0:T(8,128)(2,1)}, bf16[4,256,256]{2,1,0:T(8,128)(2,1)S(1)}, u32[]{:S(2)}, u32[]{:S(2)}) collective-permute-start(bf16[4,256,256]{2,1,0:T(8,128)(2,1)} %slice.198), channel_id=1, source_target_pairs={{0,4},{1,5},{2,6},{3,7},{4,8},{5,9},{6,10},{7,11},{8,12},{9,13},{1... | collective-permute-start | bytes 1572872 | tf_op jit(solution)/shard_map/ppermute | solution.py:18
  95.4 5.7 %copy-start.6 = (bf16[4,2,256,256]{3,2,1,0:T(8,128)(2,1)S(1)}, bf16[4,2,256,256]{3,2,1,0:T(8,128)(2,1)}, u32[]{:S(2)}) copy-start(bf16[4,2,256,256]{3,2,1,0:T(8,128)(2,1)} %get-tuple-element.21) | copy-start | bytes 3145732
  95.4 9.0 %copy-start.5 = (bf16[4,2,256,256]{3,2,1,0:T(8,128)(2,1)S(1)}, bf16[4,2,256,256]{3,2,1,0:T(8,128)(2,1)}, u32[]{:S(2)}) copy-start(bf16[4,2,256,256]{3,2,1,0:T(8,128)(2,1)} %get-tuple-element.23) | copy-start | bytes 3145732
  95.5 12.2 %collective-permute-start.16 = (bf16[2,2,256,256]{3,2,1,0:T(8,128)(2,1)S(1)}, bf16[2,2,256,256]{3,2,1,0:T(8,128)(2,1)S(1)}, u32[]{:S(2)}, u32[]{:S(2)}) collective-permute-start(bf16[2,2,256,256]{3,2,1,0:T(8,128)(2,1)S(1)} %get-tuple-element.17), channel_id=1, source_target_pairs={{0,4},{1,5},{2,6},{3,7},{4,8},{5,9},{6,10},{7,11},{8,12},{9,13},{1... | collective-permute-start | bytes 1572872 | tf_op jit(solution)/shard_map/ppermute | solution.py:18
  96.1 12.0 %collective-permute-start.18 = (bf16[2,2,256,256]{3,2,1,0:T(8,128)(2,1)S(1)}, bf16[2,2,256,256]{3,2,1,0:T(8,128)(2,1)S(1)}, u32[]{:S(2)}, u32[]{:S(2)}) collective-permute-start(bf16[2,2,256,256]{3,2,1,0:T(8,128)(2,1)S(1)} %get-tuple-element.19), channel_id=1, source_target_pairs={{0,12},{1,13},{2,14},{3,15},{4,0},{5,1},{6,2},{7,3},{8,4},{9,5},{1... | collective-permute-start | bytes 1572872 | tf_op jit(solution)/shard_map/ppermute | solution.py:18
  98.8 8.9 %copy-start.8 = (bf16[4,2,256,256]{3,2,1,0:T(8,128)(2,1)S(1)}, bf16[4,2,256,256]{3,2,1,0:T(8,128)(2,1)}, u32[]{:S(2)}) copy-start(bf16[4,2,256,256]{3,2,1,0:T(8,128)(2,1)} %get-tuple-element.16) | copy-start | bytes 3145732
  101.0 12.5 %collective-permute-start.24 = (bf16[2,2,256,256]{3,2,1,0:T(8,128)(2,1)S(1)}, bf16[2,2,256,256]{3,2,1,0:T(8,128)(2,1)S(1)}, u32[]{:S(2)}, u32[]{:S(2)}) collective-permute-start(bf16[2,2,256,256]{3,2,1,0:T(8,128)(2,1)S(1)} %get-tuple-element.22), channel_id=1, source_target_pairs={{0,1},{1,2},{2,3},{3,0},{4,5},{5,6},{6,7},{7,4},{8,9},{9,10},{10,1... | collective-permute-start | bytes 1572872 | tf_op jit(solution)/shard_map/ppermute | solution.py:18
  101.1 12.7 %collective-permute-start.26 = (bf16[2,2,256,256]{3,2,1,0:T(8,128)(2,1)S(1)}, bf16[2,2,256,256]{3,2,1,0:T(8,128)(2,1)S(1)}, u32[]{:S(2)}, u32[]{:S(2)}) collective-permute-start(bf16[2,2,256,256]{3,2,1,0:T(8,128)(2,1)S(1)} %get-tuple-element.24), channel_id=1, source_target_pairs={{0,3},{1,0},{2,1},{3,2},{4,7},{5,4},{6,5},{7,6},{8,11},{9,8},{10,9... | collective-permute-start | bytes 1572872 | tf_op jit(solution)/shard_map/ppermute | solution.py:18
  104.5 3.6 %copy-start.7 = (bf16[4,2,256,256]{3,2,1,0:T(8,128)(2,1)S(1)}, bf16[4,2,256,256]{3,2,1,0:T(8,128)(2,1)}, u32[]{:S(2)}) copy-start(bf16[4,2,256,256]{3,2,1,0:T(8,128)(2,1)} %get-tuple-element.18) | copy-start | bytes 3145732
  107.9 20.4 %collective-permute-start.17 = (bf16[4,2,256,256]{3,2,1,0:T(8,128)(2,1)S(1)}, bf16[4,2,256,256]{3,2,1,0:T(8,128)(2,1)S(1)}, u32[]{:S(2)}, u32[]{:S(2)}) collective-permute-start(bf16[4,2,256,256]{3,2,1,0:T(8,128)(2,1)S(1)} %pad_maximum_fusion), channel_id=1, source_target_pairs={{0,4},{1,5},{2,6},{3,7},{4,8},{5,9},{6,10},{7,11},{8,12},{9,13},{1... | collective-permute-start | bytes 3145736 | tf_op jit(solution)/shard_map/ppermute | solution.py:18
  108.3 20.1 %collective-permute-start.19 = (bf16[4,2,256,256]{3,2,1,0:T(8,128)(2,1)S(1)}, bf16[4,2,256,256]{3,2,1,0:T(8,128)(2,1)S(1)}, u32[]{:S(2)}, u32[]{:S(2)}) collective-permute-start(bf16[4,2,256,256]{3,2,1,0:T(8,128)(2,1)S(1)} %pad_maximum_fusion.1), channel_id=1, source_target_pairs={{0,12},{1,13},{2,14},{3,15},{4,0},{5,1},{6,2},{7,3},{8,4},{9,5},{1... | collective-permute-start | bytes 3145736 | tf_op jit(solution)/shard_map/ppermute | solution.py:18
  113.7 14.6 %copy-start.10 = (bf16[4,2,256,256]{3,2,1,0:T(8,128)(2,1)S(1)}, bf16[4,2,256,256]{3,2,1,0:T(8,128)(2,1)}, u32[]{:S(2)}) copy-start(bf16[4,2,256,256]{3,2,1,0:T(8,128)(2,1)} %get-tuple-element.15) | copy-start | bytes 3145732
  113.8 22.4 %collective-permute-start.25 = (bf16[4,2,256,256]{3,2,1,0:T(8,128)(2,1)S(1)}, bf16[4,2,256,256]{3,2,1,0:T(8,128)(2,1)S(1)}, u32[]{:S(2)}, u32[]{:S(2)}) collective-permute-start(bf16[4,2,256,256]{3,2,1,0:T(8,128)(2,1)S(1)} %pad_maximum_fusion.2), channel_id=1, source_target_pairs={{0,1},{1,2},{2,3},{3,0},{4,5},{5,6},{6,7},{7,4},{8,9},{9,10},{10,1... | collective-permute-start | bytes 3145736 | tf_op jit(solution)/shard_map/ppermute | solution.py:18
  114.1 22.1 %collective-permute-start.27 = (bf16[4,2,256,256]{3,2,1,0:T(8,128)(2,1)S(1)}, bf16[4,2,256,256]{3,2,1,0:T(8,128)(2,1)S(1)}, u32[]{:S(2)}, u32[]{:S(2)}) collective-permute-start(bf16[4,2,256,256]{3,2,1,0:T(8,128)(2,1)S(1)} %pad_maximum_fusion.3), channel_id=1, source_target_pairs={{0,3},{1,0},{2,1},{3,2},{4,7},{5,4},{6,5},{7,6},{8,11},{9,8},{10,9... | collective-permute-start | bytes 3145736 | tf_op jit(solution)/shard_map/ppermute | solution.py:18
  128.4 7.8 %copy-start.9 = (bf16[4,2,256,256]{3,2,1,0:T(8,128)(2,1)S(1)}, bf16[4,2,256,256]{3,2,1,0:T(8,128)(2,1)}, u32[]{:S(2)}) copy-start(bf16[4,2,256,256]{3,2,1,0:T(8,128)(2,1)} %get-tuple-element.20) | copy-start | bytes 3145732
  128.9 11.3 %collective-permute-start.20 = (bf16[2,128,256]{2,1,0:T(8,128)(2,1)S(1)}, bf16[2,128,256]{2,1,0:T(8,128)(2,1)S(1)}, u32[]{:S(2)}, u32[]{:S(2)}) collective-permute-start(bf16[2,128,256]{2,1,0:T(8,128)(2,1)S(1)} %bitcast.78), channel_id=1, source_target_pairs={{0,1},{1,2},{2,3},{3,0},{4,5},{5,6},{6,7},{7,4},{8,9},{9,10},{10,1... | collective-permute-start | bytes 393224 | tf_op jit(solution)/shard_map/ppermute | solution.py:18
  129.0 11.3 %collective-permute-start.22 = (bf16[2,128,256]{2,1,0:T(8,128)(2,1)S(1)}, bf16[2,128,256]{2,1,0:T(8,128)(2,1)S(1)}, u32[]{:S(2)}, u32[]{:S(2)}) collective-permute-start(bf16[2,128,256]{2,1,0:T(8,128)(2,1)S(1)} %bitcast.76), channel_id=1, source_target_pairs={{0,3},{1,0},{2,1},{3,2},{4,7},{5,4},{6,5},{7,6},{8,11},{9,8},{10,9... | collective-permute-start | bytes 393224 | tf_op jit(solution)/shard_map/ppermute | solution.py:18
  136.6 10.9 %copy-start.14 = (s32[4]{0:T(128)S(1)}, s32[4]{0:T(128)}, u32[]{:S(2)}) copy-start(s32[4]{0:T(128)} %param.15) | copy-start | bytes 52
  136.6 7.4 %collective-permute-start.28 = (bf16[2,128,256]{2,1,0:T(8,128)(2,1)S(1)}, bf16[2,128,256]{2,1,0:T(8,128)(2,1)S(1)}, u32[]{:S(2)}, u32[]{:S(2)}) collective-permute-start(bf16[2,128,256]{2,1,0:T(8,128)(2,1)S(1)} %bitcast.77), channel_id=1, source_target_pairs={{0,4},{1,5},{2,6},{3,7},{4,8},{5,9},{6,10},{7,11},{8,12},{9,13},{1... | collective-permute-start | bytes 393224 | tf_op jit(solution)/shard_map/ppermute | solution.py:18
  137.0 7.3 %collective-permute-start.30 = (bf16[2,128,256]{2,1,0:T(8,128)(2,1)S(1)}, bf16[2,128,256]{2,1,0:T(8,128)(2,1)S(1)}, u32[]{:S(2)}, u32[]{:S(2)}) collective-permute-start(bf16[2,128,256]{2,1,0:T(8,128)(2,1)S(1)} %bitcast.75), channel_id=1, source_target_pairs={{0,12},{1,13},{2,14},{3,15},{4,0},{5,1},{6,2},{7,3},{8,4},{9,5},{1... | collective-permute-start | bytes 393224 | tf_op jit(solution)/shard_map/ppermute | solution.py:18
  140.2 8.0 %collective-permute-start.21 = (bf16[4,128,256]{2,1,0:T(8,128)(2,1)S(1)}, bf16[4,128,256]{2,1,0:T(8,128)(2,1)S(1)}, u32[]{:S(2)}, u32[]{:S(2)}) collective-permute-start(bf16[4,128,256]{2,1,0:T(8,128)(2,1)S(1)} %pad_maximum_fusion.4), channel_id=1, source_target_pairs={{0,1},{1,2},{2,3},{3,0},{4,5},{5,6},{6,7},{7,4},{8,9},{9,10},{10,1... | collective-permute-start | bytes 786440 | tf_op jit(solution)/shard_map/ppermute | solution.py:18
  140.4 7.8 %collective-permute-start.23 = (bf16[4,128,256]{2,1,0:T(8,128)(2,1)S(1)}, bf16[4,128,256]{2,1,0:T(8,128)(2,1)S(1)}, u32[]{:S(2)}, u32[]{:S(2)}) collective-permute-start(bf16[4,128,256]{2,1,0:T(8,128)(2,1)S(1)} %pad_maximum_fusion.5), channel_id=1, source_target_pairs={{0,3},{1,0},{2,1},{3,2},{4,7},{5,4},{6,5},{7,6},{8,11},{9,8},{10,9... | collective-permute-start | bytes 786440 | tf_op jit(solution)/shard_map/ppermute | solution.py:18
  144.1 7.7 %collective-permute-start.29 = (bf16[4,128,256]{2,1,0:T(8,128)(2,1)S(1)}, bf16[4,128,256]{2,1,0:T(8,128)(2,1)S(1)}, u32[]{:S(2)}, u32[]{:S(2)}) collective-permute-start(bf16[4,128,256]{2,1,0:T(8,128)(2,1)S(1)} %pad_maximum_fusion.6), channel_id=1, source_target_pairs={{0,4},{1,5},{2,6},{3,7},{4,8},{5,9},{6,10},{7,11},{8,12},{9,13},{1... | collective-permute-start | bytes 786440 | tf_op jit(solution)/shard_map/ppermute | solution.py:18
  144.3 7.5 %collective-permute-start.31 = (bf16[4,128,256]{2,1,0:T(8,128)(2,1)S(1)}, bf16[4,128,256]{2,1,0:T(8,128)(2,1)S(1)}, u32[]{:S(2)}, u32[]{:S(2)}) collective-permute-start(bf16[4,128,256]{2,1,0:T(8,128)(2,1)S(1)} %pad_maximum_fusion.7), channel_id=1, source_target_pairs={{0,12},{1,13},{2,14},{3,15},{4,0},{5,1},{6,2},{7,3},{8,4},{9,5},{1... | collective-permute-start | bytes 786440 | tf_op jit(solution)/shard_map/ppermute | solution.py:18
Sparse Core Ops, SparseCore 0:
  9.5 34.5 all-gather.1

commit v3 on v0

v3 whole, which is shorter than its diff:
```python
import functools

import jax
import jax.numpy as jnp
from jax import lax
from jax.experimental import pallas as pl
from jax.experimental.pallas import tpu as pltpu
from jax.sharding import PartitionSpec as P

BAND = 16
RING = 4
STATES = RING * RING
OFFSETS = (0, -1, 1, 2)
LIMIT = 40 << 20


def shift(value, axis, step):
    pairs = []
    for device in range(STATES):
        z, x = device // RING, device % RING
        if axis == "z":
            z = (z + step) % RING
        else:
            x = (x + step) % RING
        pairs.append((device, z * RING + x))
    return lax.ppermute(value, "col", pairs)


def gather_near(block, axis):
    low = shift(block, axis, 1)
    high = shift(block, axis, -1)
    far = shift(block, axis, 2)
    return jnp.stack([block, low]), jnp.stack([high, far])


def gather_ring(first, second, axis):
    low_first = shift(first, axis, 1)
    high_second = shift(second, axis, -1)
    high_first = shift(first, axis, -1)
    low_second = shift(second, axis, 1)
    far_first = shift(low_first, axis, 1)
    far_second = shift(high_second, axis, -1)
    return (low_first, low_second), (high_first, high_second), (far_first, far_second)


def add(*parts):
    total = parts[0].astype(jnp.float32)
    for part in parts[1:]:
        total += part.astype(jnp.float32)
    return total.astype(jnp.bfloat16)


def left_product(left_ref, src_ref, a, pair):
    total = None
    for k in range(2):
        j = src_ref[a, k]
        both = jnp.concatenate([pair[0, j], pair[1, j]], axis=1)
        product = jnp.dot(left_ref[k], both, preferred_element_type=jnp.float32)
        total = product if total is None else total + product
    return total.astype(jnp.bfloat16)


def left_kernel(count, src_ref, left_ref, *refs):
    pairs, outs = refs[:count], refs[count:]

    def body(a, carry):
        for pair, out in zip(pairs, outs):
            out[a] = left_product(left_ref.at[a], src_ref, a, pair)
        return carry

    lax.fori_loop(0, left_ref.shape[0], body, 0)


def left_parts(src, left, pairs):
    tiles, _, tile, _ = left.shape
    smem = pl.BlockSpec(memory_space=pltpu.SMEM)
    vmem = pl.BlockSpec(memory_space=pltpu.VMEM)
    count = len(pairs)
    return pl.pallas_call(
        functools.partial(left_kernel, count),
        out_shape=[jax.ShapeDtypeStruct((tiles, tile, tile), jnp.bfloat16)] * count,
        in_specs=[smem] + [vmem] * (count + 1),
        out_specs=[vmem] * count,
        compiler_params=pltpu.CompilerParams(vmem_limit_bytes=20 << 20),
        cost_estimate=pl.CostEstimate(
            flops=count * tiles * 2 * 2 * tile**3,
            bytes_accessed=count * tiles * tile * tile * 4,
            transcendentals=0,
        ),
        name="left_parts",
    )(src, left, *pairs)


def right_product(block, right, pick):
    return lax.dot_general(
        block, right[pick], (((1,), (1,)), ((), ())), preferred_element_type=jnp.float32
    ).astype(jnp.bfloat16)


def mix_kernel(src_ref, pick_ref, left_ref, mix_ref, right_hbm, *refs):
    far, near, refs = refs[:4], refs[4:16], refs[16:]
    mixed_ref, far_outs, (own, right, sem) = refs[0], refs[1:5], refs[5:]
    a = pl.program_id(0)
    tile = left_ref.shape[-1]
    fetch = pltpu.make_async_copy(right_hbm, right, sem)

    @pl.when(a == 0)
    def _():
        fetch.start()

    for number in range(4):
        own[number] = left_product(left_ref.at[0], src_ref, a, far[number])

    def slab(half, ring, inner, rows):
        lanes = pl.ds(inner % 2 * (tile // 2), tile // 2)
        if ring == 3:
            return own[half * 2 + inner // 2, rows, lanes]
        return near[(half * 3 + ring) * 2 + inner // 2][0, rows, lanes]

    for band in range(tile // BAND):
        rows = pl.ds(band * BAND, BAND)
        slabs = []
        for s in range(STATES):
            i, k = s // RING, s % RING
            slabs.append(jnp.concatenate([slab(0, i, k, rows), slab(1, k, i, rows)], axis=1))
        product = jnp.dot(
            mix_ref[...], jnp.concatenate(slabs), preferred_element_type=jnp.float32
        )
        mixed_ref[0, :, rows, :] = product.astype(jnp.bfloat16).reshape(STATES, BAND, tile)

    @pl.when(a == 0)
    def _():
        fetch.wait()

    for half in range(2):

        @pl.when(a // 2 == half)
        def _():
            for inner in range(RING):
                t = 3 * RING + inner if half == 0 else inner * RING + 3
                far_outs[half * 2 + inner // 2][inner % 2, 0] = right_product(
                    mixed_ref[0, t], right, pick_ref[a, t]
                )


def term_kernel(pick_ref, mixed_ref, right, *outs):
    a = pl.program_id(0)
    for half in range(2):

        @pl.when(a // 2 == half)
        def _():
            for ring in (2, 1, 0):
                for inner in range(RING):
                    t = ring * RING + inner if half == 0 else inner * RING + ring
                    product = right_product(mixed_ref[0, t], right, pick_ref[a, t])
                    if ring:
                        outs[half * 8 + (ring - 1) * 2 + inner // 2][inner % 2, 0] = product
                    else:
                        outs[half * 8 + 4 + inner][0] = product


def half_slot(half):
    return lambda a: jnp.minimum(a, 1) if half == 0 else jnp.maximum(a - 2, 0)


def whole(shape):
    return pl.BlockSpec(shape, lambda a: (0,) * len(shape), pipeline_mode=pl.Buffered(1))


def pair_spec(half, tile):
    slot = half_slot(half)
    return pl.BlockSpec((2, 1, tile, tile), lambda a: (0, slot(a), 0, 0))


def mixed_and_far(src, pick, left, mix, right, far, near):
    tiles, _, tile, _ = left.shape
    smem = pl.BlockSpec(memory_space=pltpu.SMEM)
    pair = jax.ShapeDtypeStruct((2, tiles // 2, tile, tile), jnp.bfloat16)
    return pl.pallas_call(
        mix_kernel,
        grid=(tiles,),
        out_shape=[jax.ShapeDtypeStruct((tiles, STATES, tile, tile), jnp.bfloat16)] + [pair] * 4,
        in_specs=[
            smem,
            smem,
            pl.BlockSpec((1, 2, tile, tile), lambda a: (a, 0, 0, 0)),
            whole(mix.shape),
            pl.BlockSpec(memory_space=pl.ANY),
        ]
        + [whole(far[0].shape)] * 4
        + [pl.BlockSpec((1, tile, tile), lambda a: (a, 0, 0))] * 12,
        out_specs=[pl.BlockSpec((1, STATES, tile, tile), lambda a: (a, 0, 0, 0))]
        + [pair_spec(half, tile) for half in (0, 0, 1, 1)],
        scratch_shapes=[
            pltpu.VMEM((4, tile, tile), jnp.bfloat16),
            pltpu.VMEM(right.shape, jnp.bfloat16),
            pltpu.SemaphoreType.DMA,
        ],
        compiler_params=pltpu.CompilerParams(vmem_limit_bytes=LIMIT),
        name="mixed_and_far",
    )(src, pick, left, mix, right, *far, *near)


def near_terms(pick, mixed, right):
    tiles, _, tile, _ = mixed.shape
    smem = pl.BlockSpec(memory_space=pltpu.SMEM)
    pair = jax.ShapeDtypeStruct((2, tiles // 2, tile, tile), jnp.bfloat16)
    single = jax.ShapeDtypeStruct((tiles // 2, tile, tile), jnp.bfloat16)

    def single_spec(half):
        slot = half_slot(half)
        return pl.BlockSpec((1, tile, tile), lambda a: (slot(a), 0, 0))

    return pl.pallas_call(
        term_kernel,
        grid=(tiles,),
        out_shape=([pair] * 4 + [single] * 4) * 2,
        in_specs=[
            smem,
            pl.BlockSpec((1, STATES, tile, tile), lambda a: (a, 0, 0, 0)),
            whole(right.shape),
        ],
        out_specs=[
            spec
            for half in (0, 1)
            for spec in [pair_spec(half, tile)] * 4 + [single_spec(half)] * 4
        ],
        compiler_params=pltpu.CompilerParams(vmem_limit_bytes=LIMIT),
        cost_estimate=pl.CostEstimate(
            flops=tiles * 12 * 2 * tile**3,
            bytes_accessed=tiles * 32 * 2 * tile * tile,
            transcendentals=0,
        ),
        name="near_terms",
    )(pick, mixed, right)


def ring_sums(far, near, axis):
    low_first, low_second, high_first, high_second = near[:4]
    own = near[4:]
    up = shift(far[0], axis, 1)
    down = shift(far[1], axis, -1)
    from_low_second = shift(high_second, axis, 1)
    from_high_first = shift(low_first, axis, -1)
    from_low_first = shift(add(high_first, up), axis, 1)
    from_high_second = shift(add(low_second, down), axis, -1)
    first = [add(own[n], from_high_first[n], from_low_first[n]) for n in range(2)]
    second = [add(own[2 + n], from_low_second[n], from_high_second[n]) for n in range(2)]
    return first + second


def last_sum(blocks, axis):
    own, low, high, far = blocks
    return (
        own,
        shift(far, axis, 2),
        shift(high, axis, 1),
        shift(low, axis, -1),
    )


def per_device(
    wavefunction, env_left, left_src, two_site, env_right, right_loc, left_size, right_size
):
    tile = wavefunction.shape[3]
    tiles = wavefunction.shape[0]
    z, x = lax.axis_index("col") // RING, lax.axis_index("col") % RING
    offsets = jnp.asarray(OFFSETS, jnp.int32)
    order = (
        ((z + offsets) % RING)[:, None] * RING + ((x + offsets) % RING)[None, :]
    ).reshape(STATES)

    shard = wavefunction[:, 0]
    own_a = gather_near(shard[:, :, : tile // 2], "x")
    own_b = gather_near(shard[:, :, tile // 2 :], "z")
    ring_a = gather_ring(*own_a, "z")
    ring_b = gather_ring(*own_b, "x")

    row = lax.broadcasted_iota(jnp.int32, (1, tile, 1), 1)
    right = jnp.where(row < right_size[:, None, None], env_right[0], 0).astype(jnp.bfloat16)
    right = lax.all_gather(right, "row", axis=0, tiled=True)
    loc = lax.all_to_all(
        jnp.broadcast_to(right_loc[:, 0][None], (STATES, tiles)), "col", 0, 0, tiled=True
    )
    pick = ((order // 2 * 4)[:, None] + loc[order]).T
    mix = two_site[0][order][:, order]
    mix = jnp.kron(mix, jnp.eye(BAND, dtype=jnp.bfloat16))

    src, left = left_src[0], env_left[0]
    parts_own = left_parts(src, left, own_a + own_b)
    parts_near = left_parts(src, left, ring_a[0] + ring_a[1] + ring_b[0] + ring_b[1])
    near = parts_own[:2] + parts_near[:4] + parts_own[2:] + parts_near[4:]
    mixed, *far = mixed_and_far(src, pick, left, mix, right, ring_a[2] + ring_b[2], near)
    outs = near_terms(pick, mixed, right)

    sums_a = ring_sums(far[:2], outs[:8], "z")
    sums_b = ring_sums(far[2:], outs[8:], "x")
    parts_a = last_sum(sums_a, "x")
    parts_b = last_sum(sums_b, "z")
    summed = jnp.concatenate([add(*parts_a), add(*parts_b)])
    inside = row < left_size[:, None, None]
    return jnp.where(inside, summed, 0).astype(jnp.bfloat16)[:, None]


def solution(mesh):
    placed = (
        P("row", "col", None, None),
        P("col", "row", None, None, None),
        P("col", "row", None),
        P("col", None, None),
        P("col", "row", None, None),
        P("row", "col"),
        P("row"),
        P("row"),
    )
    return jax.shard_map(
        per_device,
        mesh=mesh,
        in_specs=placed,
        out_specs=P("row", "col", None, None),
        check_vma=False,
    )
```

time: 598 us -> 189 us (0.32)
  waiting for transfers between devices: 272 us -> 51 us
  blocking collectives: 124 us -> 0 us
  local copies, waits for them, and re-layouts: 125 us -> 33.9 us
  starting transfers between devices: 9.58 us -> 56.6 us
  matrix products: 34.7 us -> 0 us
  Pallas kernels: 0 us -> 23.3 us
  other arithmetic: 17.2 us -> 9.42 us
    unnamed x3 -> x1, waiting for transfers between devices: 139 us -> 0.02 us
    all_to_all x1 -> x0, blocking collectives: 102 us -> none  [per_device(): lax.all_to_all(jnp.stack(pieces, axis=1), 'row', split_axis=0, concat_axi...]
    all_to_all x2 -> x1, waiting for transfers between devices: 85.7 us -> 0.01 us  [per_device(): lax.all_to_all(jnp.broadcast_to(right_loc[:, 0][None], (STATES, tiles)),...]
    gather x20 -> x6, local copies, waits for them, and re-layouts: 71.7 us -> 1.96 us  [the longest x4 1.32 us: per_device(): mix = two_site[0][order][:, order]]
    ppermute x0 -> x36, waiting for transfers between devices: none -> 50.9 us  [shift(): return lax.ppermute(value, 'col', pairs)]
    ppermute x0 -> x36, starting transfers between devices: none -> 49.9 us  [shift(): return lax.ppermute(value, 'col', pairs)]
    all_gather x1, waiting for transfers between devices: 47.3 us -> 0.02 us  [per_device(): right = lax.all_gather(right, 'row', axis=0, tiled=True)]
    dot_general x10 -> x0, matrix products: 34.7 us -> none  [the longest x4 18.8 us: per_device(): jnp.einsum('kxy,ksyz->sxz', env_left[0, position], blocks, preferred_elem...]
  transfers between devices with their start and end apart: 4 -> 38, of which waited for: 3 -> 13; matrix products, arithmetic and copies ran while one was open for 22% -> 7% of each run, Pallas kernels for 0% -> 7%
where the time goes in v3:
time: 189 us; the launch traced here: 188 us
  starting transfers between devices  56.6 us (30%)
  waiting for transfers between devices  51 us (27%)
  local copies, waits for them, and re-layouts  33.9 us (18%)
  Pallas kernels  23.3 us (12%)
  between operations  13.7 us (7%)
  other arithmetic  9.42 us (5%)
    ppermute x36, waiting for transfers between devices, shift(): return lax.ppermute(value, 'col', pairs)  50.9 us
    ppermute x36, starting transfers between devices, shift(): return lax.ppermute(value, 'col', pairs)  49.9 us
    unnamed x74, local copies, waits for them, and re-layouts  26.1 us
    pallas_call x1, Pallas kernels, mixed_and_far(): pl.pallas_call(mix_kernel, grid=(tiles,), out_shape=[jax.ShapeDtypeStruct...  9.99 us
    pallas_call x2, Pallas kernels, left_parts(): pl.pallas_call(functools.partial(left_kernel, count), out_shape=[jax.Shap...  7.69 us
    all_to_all x1, starting transfers between devices, per_device(): lax.all_to_all(jnp.broadcast_to(right_loc[:, 0][None], (STATES, tiles)),...  6.7 us
    pallas_call x1, Pallas kernels, near_terms(): pl.pallas_call(term_kernel, grid=(tiles,), out_shape=([pair] * 4 + [singl...  5.65 us
  transfers between devices with their start and end apart: 38, of which 13 were waited for; matrix products, arithmetic and copies ran while one was open for 7% of the time, Pallas kernels for 7%

profile of v3, /device:TPU:0, one launch (start us, length us, event | category | flops | bytes accessed | tf_op | source)
XLA Modules:
  0.0 187.9 jit_solution(829258322825104788)
XLA Ops:
  7.4 2.0 %bitcast_select_fusion = bf16[4,256,256]{2,1,0:T(8,128)(2,1)} fusion(bf16[1,4,256,256]{3,2,1,0:T(8,128)(2,1)} %param.13, pred[4,256]{1,0:T(4,128)(4,1)S(1)} %iota_compare_fusion.1), kind=kLoop, calls=%fused_computation.37 | loop fusion | flops 262144 | bytes 1049600 | tf_op jit(solution)/shard_map/jit(_where)/select_n | solution.py:280
  9.4 2.1 %slice_bitcast_fusion.16 = (bf16[1,4,256,128]{3,2,1,0:T(8,128)(2,1)S(1)}, bf16[1,4,256,128]{3,2,1,0:T(8,128)(2,1)}, bf16[4,256,128]{2,1,0:T(8,128)(2,1)}, bf16[4,256,128]{2,1,0:T(8,128)(2,1)S(1)}) fusion(bf16[4,256,256]{2,1,0:T(8,128)(2,1)} %bitcast.116), kind=kLoop, calls=%fused_computation.82 | loop fusion | bytes 1572864 | tf_op jit(solution)/shard_map/stack | solution.py:33
  11.5 4.1 %collective-permute-start.10 = (bf16[4,256,128]{2,1,0:T(8,128)(2,1)}, bf16[4,256,128]{2,1,0:T(8,128)(2,1)S(1)}, u32[]{:S(2)}, u32[]{:S(2)}) collective-permute-start(bf16[4,256,128]{2,1,0:T(8,128)(2,1)} %get-tuple-element.77), channel_id=1, source_target_pairs={{0,12},{1,13},{2,14},{3,15},{4,0},{5,1},{6,2},{7,3},{8,4},{9,5},{1... | collective-permute-start | bytes 786440 | tf_op jit(solution)/shard_map/ppermute | solution.py:26
  15.6 2.8 %collective-permute-start.3 = (bf16[4,256,128]{2,1,0:T(8,128)(2,1)S(1)}, bf16[4,256,128]{2,1,0:T(8,128)(2,1)S(1)}, u32[]{:S(2)}, u32[]{:S(2)}) collective-permute-start(bf16[4,256,128]{2,1,0:T(8,128)(2,1)S(1)} %get-tuple-element.78), channel_id=1, source_target_pairs={{0,3},{1,0},{2,1},{3,2},{4,7},{5,4},{6,5},{7,6},{8,11},{9,8},{10,9... | collective-permute-start | bytes 786440 | tf_op jit(solution)/shard_map/ppermute | solution.py:26
  19.2 0.9 collective-permute-start
  20.1 1.3 broadcast_in_dim.42
  21.3 6.7 %all-to-all-start = ((s32[16,1,4]{2,1,0:T(1,128)}), s32[16,1,4]{2,1,0:T(1,128)S(1)}, u32[]{:S(2)}, u32[]{:S(2)}) async-start(s32[16,1,4]{2,1,0:T(1,128)} %broadcast_in_dim.42), calls=%async_computation | async-start | bytes 16384 | tf_op jit(solution)/shard_map/all_to_all | solution.py:282
  28.9 1.9 %collective-permute-start.7 = (bf16[4,256,128]{2,1,0:T(8,128)(2,1)}, bf16[4,256,128]{2,1,0:T(8,128)(2,1)S(1)}, u32[]{:S(2)}, u32[]{:S(2)}) collective-permute-start(bf16[4,256,128]{2,1,0:T(8,128)(2,1)} %get-tuple-element.77), channel_id=1, source_target_pairs={{0,4},{1,5},{2,6},{3,7},{4,8},{5,9},{6,10},{7,11},{8,12},{9,13},{1... | collective-permute-start | bytes 786440 | tf_op jit(solution)/shard_map/ppermute | solution.py:26
  30.8 2.7 %collective-permute-start.12 = (bf16[2,4,256,128]{3,2,1,0:T(8,128)(2,1)S(1)}, bf16[2,4,256,128]{3,2,1,0:T(8,128)(2,1)}, u32[]{:S(2)}, u32[]{:S(2)}) collective-permute-start(bf16[2,4,256,128]{3,2,1,0:T(8,128)(2,1)S(1)} %pad_maximum_fusion.3.refs_3_), channel_id=1, source_target_pairs={{0,3},{1,0},{2,1},{3,2},{4,7},{5,4},{6,5},{7,6},{8,11},{9,8},{10,9... | collective-permute-start | bytes 1572872 | tf_op jit(solution)/shard_map/ppermute | solution.py:26
  33.6 1.8 collective-permute-start.5
  35.8 1.1 pad_maximum_fusion.refs_0_
  37.0 2.3 %collective-permute-start.1 = (bf16[2,4,256,128]{3,2,1,0:T(8,128)(2,1)S(1)}, bf16[2,4,256,128]{3,2,1,0:T(8,128)(2,1)}, u32[]{:S(2)}, u32[]{:S(2)}) collective-permute-start(bf16[2,4,256,128]{3,2,1,0:T(8,128)(2,1)S(1)} %pad_maximum_fusion.refs_0_), channel_id=1, source_target_pairs={{0,4},{1,5},{2,6},{3,7},{4,8},{5,9},{6,10},{7,11},{8,12},{9,13},{1... | collective-permute-start | bytes 1572872 | tf_op jit(solution)/shard_map/ppermute | solution.py:26
  40.1 2.4 %collective-permute-done.12.refs_7_ = bf16[2,4,256,128]{3,2,1,0:T(8,128)(2,1)} collective-permute-done((bf16[2,4,256,128]{3,2,1,0:T(8,128)(2,1)S(1)}, bf16[2,4,256,128]{3,2,1,0:T(8,128)(2,1)}, u32[]{:S(2)}, u32[]{:S(2)}) %collective-permute-start.12) | collective-permute-done | bytes 524320 | tf_op jit(solution)/shard_map/ppermute | solution.py:26
  42.5 1.8 collective-permute-start.15
  44.3 3.7 %collective-permute-done.5.refs_3_ = bf16[2,4,256,128]{3,2,1,0:T(8,128)(2,1)} collective-permute-done((bf16[2,4,256,128]{3,2,1,0:T(8,128)(2,1)S(1)}, bf16[2,4,256,128]{3,2,1,0:T(8,128)(2,1)}, u32[]{:S(2)}, u32[]{:S(2)}) %collective-permute-start.5) | collective-permute-done | bytes 524320 | tf_op jit(solution)/shard_map/ppermute | solution.py:26
  49.4 1.1 broadcast_multiply_fusion
  50.6 1.1 collective-permute-done.14.refs_1_
  51.6 2.2 %collective-permute-start.17 = (bf16[2,4,256,128]{3,2,1,0:T(8,128)(2,1)}, bf16[2,4,256,128]{3,2,1,0:T(8,128)(2,1)}, u32[]{:S(2)}, u32[]{:S(2)}) collective-permute-start(bf16[2,4,256,128]{3,2,1,0:T(8,128)(2,1)} %pad_maximum_fusion.2.refs_2_), channel_id=1, source_target_pairs={{0,3},{1,0},{2,1},{3,2},{4,7},{5,4},{6,5},{7,6},{8,11},{9,8},{10,9... | collective-permute-start | bytes 1572872 | tf_op jit(solution)/shard_map/ppermute | solution.py:26
  53.8 2.2 %mul.40.mix_ref = bf16[256,256]{1,0:T(8,128)(2,1)S(1)} reshape(bf16[16,16,16,16]{3,2,1,0:T(8,128)(2,1)} %broadcast_multiply_fusion) | data formatting | bytes 262144 | tf_op jit(solution)/shard_map/jit(kron)/mul | solution.py:287
  56.8 0.9 collective-permute-start.13
  57.7 1.6 collective-permute-done.1.refs_0_
  59.3 1.9 collective-permute-start.6
  61.3 1.7 collective-permute-start.9
  63.0 1.0 copy-done.28
  64.1 1.0 copy-done.30
  65.1 1.0 copy-done.32
  66.2 2.8 %left_parts.2 = (bf16[4,256,256]{2,1,0:T(8,128)(2,1)S(1)}, bf16[4,256,256]{2,1,0:T(8,128)(2,1)S(1)}, bf16[4,256,256]{2,1,0:T(8,128)(2,1)S(1)}, bf16[4,256,256]{2,1,0:T(8,128)(2,1)S(1)}) custom-call(s32[4,2]{1,0:T(4,128)S(1)} %copy.25.src_ref, bf16[4,2,256,256]{3,2,1,0:T(8,128)(2,1)S(1)} %bitcast.112, bf16[2,4,256,128]{3,2,1,0:T(8,128)(2,1)S(1)} %copy-done.32, ...), custom_call_target="tpu_custom_call" | custom-call | flops 1073741824 | bytes 4194304 | tf_op jit(solution)/shard_map/left_parts/pallas_call | solution.py:79
  71.4 1.2 copy-done.34
  72.6 4.9 %left_parts.3 = (bf16[4,256,256]{2,1,0:T(8,128)(2,1)S(1)}, bf16[4,256,256]{2,1,0:T(8,128)(2,1)S(1)}, bf16[4,256,256]{2,1,0:T(8,128)(2,1)S(1)}, bf16[4,256,256]{2...) custom-call(s32[4,2]{1,0:T(4,128)S(1)} %copy.25.src_ref, ...), custom_call_target="tpu_custom_call" | custom-call | flops 2147483648 | bytes 8388608 | tf_op jit(solution)/shard_map/left_parts/pallas_call | solution.py:79
  84.1 1.2 copy-done.4
  85.3 1.3 copy-done.6
  86.6 1.0 copy-done.8
  87.6 1.0 copy-done.10
  88.6 1.0 copy-done.12
  89.7 1.0 copy-done.14
  90.7 1.0 copy-done.16
  91.8 1.0 copy-done.18
  92.8 1.0 copy-done.20
  93.9 1.0 copy-done.22
  94.9 1.0 copy-done.24
  95.9 1.0 copy-done.26
  97.0 10.0 %mixed_and_far.1 = (bf16[4,16,256,256]{3,2,1,0:T(8,128)(2,1)}, bf16[2,2,256,256]{3,2,1,0:T(8,128)(2,1)S(1)}, bf16[2,2,256,256]{3,2,1,0:T(8,128)(2,1)S(1)}, bf16[...) custom-call(s32[4,2]{1,0:T(4,128)S(1)} %copy.25.src_ref, s32[4,16]{1,0:T(4,128)S(1)} %add_bitcast_fusion.pick_ref, ...), custom_call_target="tpu_custom_call" | custom-call | tf_op jit(solution)/shard_map/mixed_and_far/pallas_call | solution.py:179
  107.0 2.8 %collective-permute-start.22 = (bf16[2,2,256,256]{3,2,1,0:T(8,128)(2,1)S(1)}, bf16[2,2,256,256]{3,2,1,0:T(8,128)(2,1)S(1)}, u32[]{:S(2)}, u32[]{:S(2)}) collective-permute-start(bf16[2,2,256,256]{3,2,1,0:T(8,128)(2,1)S(1)} %get-tuple-element.58), channel_id=1, source_target_pairs={{0,12},{1,13},{2,14},{3,15},{4,0},{5,1},{6,2},{7,3},{8,4},{9,5},{1... | collective-permute-start | bytes 1572872 | tf_op jit(solution)/shard_map/ppermute | solution.py:26
  109.9 5.7 %near_terms.1 = (bf16[2,2,256,256]{3,2,1,0:T(8,128)(2,1)S(1)}, bf16[2,2,256,256]{3,2,1,0:T(8,128)(2,1)S(1)}, bf16[2,2,256,256]{3,2,1,0:T(8,128)(2,1)S(1)}, bf16[...) custom-call(s32[4,16]{1,0:T(4,128)S(1)} %add_bitcast_fusion.pick_ref, ...), custom_call_target="tpu_custom_call" | custom-call | flops 1610612736 | bytes 16777216 | tf_op jit(solution)/shard_map/near_terms/pallas_call | solution.py:214
  115.6 3.3 %collective-permute-start.18 = (bf16[2,2,256,256]{3,2,1,0:T(8,128)(2,1)S(1)}, bf16[2,2,256,256]{3,2,1,0:T(8,128)(2,1)S(1)}, u32[]{:S(2)}, u32[]{:S(2)}) collective-permute-start(bf16[2,2,256,256]{3,2,1,0:T(8,128)(2,1)S(1)} %get-tuple-element.52), channel_id=1, source_target_pairs={{0,12},{1,13},{2,14},{3,15},{4,0},{5,1},{6,2},{7,3},{8,4},{9,5},{1... | collective-permute-start | bytes 1572872 | tf_op jit(solution)/shard_map/ppermute | solution.py:26
  118.9 2.1 %collective-permute-start.31 = (bf16[2,2,256,256]{3,2,1,0:T(8,128)(2,1)S(1)}, bf16[2,2,256,256]{3,2,1,0:T(8,128)(2,1)S(1)}, u32[]{:S(2)}, u32[]{:S(2)}) collective-permute-start(bf16[2,2,256,256]{3,2,1,0:T(8,128)(2,1)S(1)} %get-tuple-element.68), channel_id=1, source_target_pairs={{0,3},{1,0},{2,1},{3,2},{4,7},{5,4},{6,5},{7,6},{8,11},{9,8},{10,9... | collective-permute-start | bytes 1572872 | tf_op jit(solution)/shard_map/ppermute | solution.py:26
  121.0 1.6 collective-permute-start.30
  122.7 3.2 %collective-permute-done.19 = bf16[2,2,256,256]{3,2,1,0:T(8,128)(2,1)S(1)} collective-permute-done((bf16[2,2,256,256]{3,2,1,0:T(8,128)(2,1)S(1)}, bf16[2,2,256,256]{3,2,1,0:T(8,128)(2,1)S(1)}, u32[]{:S(2)}, u32[]{:S(2)}) %collective-permute-start.19) | collective-permute-done | bytes 524320 | tf_op jit(solution)/shard_map/ppermute | solution.py:26
  125.9 1.5 collective-permute-start.28
  127.5 1.2 collective-permute-done.31
  128.7 1.7 collective-permute-start.23
  130.5 2.6 %collective-permute-done.21 = bf16[2,2,256,256]{3,2,1,0:T(8,128)(2,1)S(1)} collective-permute-done((bf16[2,2,256,256]{3,2,1,0:T(8,128)(2,1)S(1)}, bf16[2,2,256,256]{3,2,1,0:T(8,128)(2,1)S(1)}, u32[]{:S(2)}, u32[]{:S(2)}) %collective-permute-start.21) | collective-permute-done | bytes 524320 | tf_op jit(solution)/shard_map/ppermute | solution.py:26
  133.1 10.9 %collective-permute-done.28 = bf16[2,2,256,256]{3,2,1,0:T(8,128)(2,1)S(1)} collective-permute-done((bf16[2,2,256,256]{3,2,1,0:T(8,128)(2,1)S(1)}, bf16[2,2,256,256]{3,2,1,0:T(8,128)(2,1)S(1)}, u32[]{:S(2)}, u32[]{:S(2)}) %collective-permute-start.28) | collective-permute-done | bytes 524320 | tf_op jit(solution)/shard_map/ppermute | solution.py:26
  144.2 2.1 %collective-permute-start.29 = (bf16[2,2,256,256]{3,2,1,0:T(8,128)(2,1)S(1)}, bf16[2,2,256,256]{3,2,1,0:T(8,128)(2,1)S(1)}, u32[]{:S(2)}, u32[]{:S(2)}) collective-permute-start(bf16[2,2,256,256]{3,2,1,0:T(8,128)(2,1)S(1)} %add_convert_fusion.1), channel_id=1, source_target_pairs={{0,1},{1,2},{2,3},{3,0},{4,5},{5,6},{6,7},{7,4},{8,9},{9,10},{10,1... | collective-permute-start | bytes 1572872 | tf_op jit(solution)/shard_map/ppermute | solution.py:26
  146.6 2.1 %collective-permute-start.24 = (bf16[2,256,256]{2,1,0:T(8,128)(2,1)S(1)}, bf16[2,256,256]{2,1,0:T(8,128)(2,1)S(1)}, u32[]{:S(2)}, u32[]{:S(2)}) collective-permute-start(bf16[2,256,256]{2,1,0:T(8,128)(2,1)S(1)} %get-tuple-element.71), channel_id=1, source_target_pairs={{0,2},{1,3},{2,0},{3,1},{4,6},{5,7},{6,4},{7,5},{8,10},{9,11},{10,... | collective-permute-start | bytes 786440 | tf_op jit(solution)/shard_map/ppermute | solution.py:26
  148.9 10.0 %collective-permute-done.32 = bf16[2,2,256,256]{3,2,1,0:T(8,128)(2,1)S(1)} collective-permute-done((bf16[2,2,256,256]{3,2,1,0:T(8,128)(2,1)S(1)}, bf16[2,2,256,256]{3,2,1,0:T(8,128)(2,1)S(1)}, u32[]{:S(2)}, u32[]{:S(2)}) %collective-permute-start.32) | collective-permute-done | bytes 524320 | tf_op jit(solution)/shard_map/ppermute | solution.py:26
  158.9 1.6 collective-permute-start.26
  160.7 8.5 %collective-permute-done.27 = bf16[2,2,256,256]{3,2,1,0:T(8,128)(2,1)S(1)} collective-permute-done((bf16[2,2,256,256]{3,2,1,0:T(8,128)(2,1)S(1)}, bf16[2,2,256,256]{3,2,1,0:T(8,128)(2,1)S(1)}, u32[]{:S(2)}, u32[]{:S(2)}) %collective-permute-start.27) | collective-permute-done | bytes 524320 | tf_op jit(solution)/shard_map/ppermute | solution.py:26
  169.2 1.4 collective-permute-start.33
  170.7 3.3 %collective-permute-start.35 = (bf16[2,256,256]{2,1,0:T(8,128)(2,1)S(1)}, bf16[2,256,256]{2,1,0:T(8,128)(2,1)S(1)}, u32[]{:S(2)}, u32[]{:S(2)}) collective-permute-start(bf16[2,256,256]{2,1,0:T(8,128)(2,1)S(1)} %fusion.1), channel_id=1, source_target_pairs={{0,12},{1,13},{2,14},{3,15},{4,0},{5,1},{6,2},{7,3},{8,4},{9,5},{1... | collective-permute-start | bytes 786440 | tf_op jit(solution)/shard_map/ppermute | solution.py:26
  174.0 0.9 collective-permute-done.26
  175.1 2.1 %collective-permute-done.33 = bf16[2,256,256]{2,1,0:T(8,128)(2,1)S(1)} collective-permute-done((bf16[2,256,256]{2,1,0:T(8,128)(2,1)S(1)}, bf16[2,256,256]{2,1,0:T(8,128)(2,1)S(1)}, u32[]{:S(2)}, u32[]{:S(2)}) %collective-permute-start.33) | collective-permute-done | bytes 262176 | tf_op jit(solution)/shard_map/ppermute | solution.py:26
  177.2 2.7 %collective-permute-done.34 = bf16[2,256,256]{2,1,0:T(8,128)(2,1)S(1)} collective-permute-done((bf16[2,256,256]{2,1,0:T(8,128)(2,1)S(1)}, bf16[2,256,256]{2,1,0:T(8,128)(2,1)S(1)}, u32[]{:S(2)}, u32[]{:S(2)}) %collective-permute-start.34) | collective-permute-done | bytes 262176 | tf_op jit(solution)/shard_map/ppermute | solution.py:26
  180.1 1.0 fusion
  (129 shorter events, 17.1 us)
Async XLA Ops:
  6.5 41.6 %copy-start = (bf16[1,16,16]{2,1,0:T(8,128)(2,1)S(1)}, bf16[1,16,16]{2,1,0:T(8,128)(2,1)}, u32[]{:S(2)}) copy-start(bf16[1,16,16]{2,1,0:T(8,128)(2,1)} %param.12) | copy-start | bytes 1540
  6.5 49.5 %copy-start.35 = (s32[1,4,2]{1,2,0:T(2,128)S(1)}, s32[1,4,2]{1,2,0:T(2,128)}, u32[]{:S(2)}) copy-start(s32[1,4,2]{1,2,0:T(2,128)} %param.11) | copy-start | bytes 100
  6.5 56.5 %copy-start.2 = (bf16[1,4,2,256,256]{4,3,2,1,0:T(8,128)(2,1)S(1)}, bf16[1,4,2,256,256]{4,3,2,1,0:T(8,128)(2,1)}, u32[]{:S(2)}) copy-start(bf16[1,4,2,256,256]{4,3,2,1,0:T(8,128)(2,1)} %param.10) | copy-start | bytes 3145732
  6.5 77.5 %all-gather.2.cloned.1.call-start = ((), (), s32[]{:S(2)}) async-start(), calls=%async_computation.1 | async-start | bytes 4718592 | tf_op jit(solution)/shard_map/all_gather | solution.py:281
  11.5 17.4 %collective-permute-start.10 = (bf16[4,256,128]{2,1,0:T(8,128)(2,1)}, bf16[4,256,128]{2,1,0:T(8,128)(2,1)S(1)}, u32[]{:S(2)}, u32[]{:S(2)}) collective-permute-start(bf16[4,256,128]{2,1,0:T(8,128)(2,1)} %get-tuple-element.77), channel_id=1, source_target_pairs={{0,12},{1,13},{2,14},{3,15},{4,0},{5,1},{6,2},{7,3},{8,4},{9,5},{1... | collective-permute-start | bytes 786440 | tf_op jit(solution)/shard_map/ppermute | solution.py:26
  15.6 15.2 %collective-permute-start.11 = (bf16[4,256,128]{2,1,0:T(8,128)(2,1)}, bf16[4,256,128]{2,1,0:T(8,128)(2,1)S(1)}, u32[]{:S(2)}, u32[]{:S(2)}) collective-permute-start(bf16[4,256,128]{2,1,0:T(8,128)(2,1)} %get-tuple-element.77), channel_id=1, source_target_pairs={{0,8},{1,9},{2,10},{3,11},{4,12},{5,13},{6,14},{7,15},{8,0},{9,1},... | collective-permute-start | bytes 786440 | tf_op jit(solution)/shard_map/ppermute | solution.py:26
  15.6 18.0 %collective-permute-start.3 = (bf16[4,256,128]{2,1,0:T(8,128)(2,1)S(1)}, bf16[4,256,128]{2,1,0:T(8,128)(2,1)S(1)}, u32[]{:S(2)}, u32[]{:S(2)}) collective-permute-start(bf16[4,256,128]{2,1,0:T(8,128)(2,1)S(1)} %get-tuple-element.78), channel_id=1, source_target_pairs={{0,3},{1,0},{2,1},{3,2},{4,7},{5,4},{6,5},{7,6},{8,11},{9,8},{10,9... | collective-permute-start | bytes 786440 | tf_op jit(solution)/shard_map/ppermute | solution.py:26
  18.4 15.2 %collective-permute-start.4 = (bf16[4,256,128]{2,1,0:T(8,128)(2,1)S(1)}, bf16[4,256,128]{2,1,0:T(8,128)(2,1)S(1)}, u32[]{:S(2)}, u32[]{:S(2)}) collective-permute-start(bf16[4,256,128]{2,1,0:T(8,128)(2,1)S(1)} %get-tuple-element.78), channel_id=1, source_target_pairs={{0,2},{1,3},{2,0},{3,1},{4,6},{5,7},{6,4},{7,5},{8,10},{9,11},{10,... | collective-permute-start | bytes 786440 | tf_op jit(solution)/shard_map/ppermute | solution.py:26
  19.2 16.7 %collective-permute-start = (bf16[4,256,128]{2,1,0:T(8,128)(2,1)S(1)}, bf16[4,256,128]{2,1,0:T(8,128)(2,1)}, u32[]{:S(2)}, u32[]{:S(2)}) collective-permute-start(bf16[4,256,128]{2,1,0:T(8,128)(2,1)S(1)} %get-tuple-element.78), channel_id=1, source_target_pairs={{0,1},{1,2},{2,3},{3,0},{4,5},{5,6},{6,7},{7,4},{8,9},{9,10},{10,1... | collective-permute-start | bytes 786440 | tf_op jit(solution)/shard_map/ppermute | solution.py:26
  21.3 34.8 %all-to-all-start = ((s32[16,1,4]{2,1,0:T(1,128)}), s32[16,1,4]{2,1,0:T(1,128)S(1)}, u32[]{:S(2)}, u32[]{:S(2)}) async-start(s32[16,1,4]{2,1,0:T(1,128)} %broadcast_in_dim.42), calls=%async_computation | async-start | bytes 16384 | tf_op jit(solution)/shard_map/all_to_all | solution.py:282
  28.9 8.1 %collective-permute-start.7 = (bf16[4,256,128]{2,1,0:T(8,128)(2,1)}, bf16[4,256,128]{2,1,0:T(8,128)(2,1)S(1)}, u32[]{:S(2)}, u32[]{:S(2)}) collective-permute-start(bf16[4,256,128]{2,1,0:T(8,128)(2,1)} %get-tuple-element.77), channel_id=1, source_target_pairs={{0,4},{1,5},{2,6},{3,7},{4,8},{5,9},{6,10},{7,11},{8,12},{9,13},{1... | collective-permute-start | bytes 786440 | tf_op jit(solution)/shard_map/ppermute | solution.py:26
  30.8 26.0 %copy-start.27 = (bf16[2,4,256,128]{3,2,1,0:T(8,128)(2,1)}, bf16[2,4,256,128]{3,2,1,0:T(8,128)(2,1)S(1)}, u32[]{:S(2)}) copy-start(bf16[2,4,256,128]{3,2,1,0:T(8,128)(2,1)S(1)} %pad_maximum_fusion.3.refs_3_) | copy-start | bytes 1572868
  30.8 11.7 %collective-permute-start.12 = (bf16[2,4,256,128]{3,2,1,0:T(8,128)(2,1)S(1)}, bf16[2,4,256,128]{3,2,1,0:T(8,128)(2,1)}, u32[]{:S(2)}, u32[]{:S(2)}) collective-permute-start(bf16[2,4,256,128]{3,2,1,0:T(8,128)(2,1)S(1)} %pad_maximum_fusion.3.refs_3_), channel_id=1, source_target_pairs={{0,3},{1,0},{2,1},{3,2},{4,7},{5,4},{6,5},{7,6},{8,11},{9,8},{10,9... | collective-permute-start | bytes 1572872 | tf_op jit(solution)/shard_map/ppermute | solution.py:26
  33.6 24.1 %copy-start.29 = (bf16[2,4,256,128]{3,2,1,0:T(8,128)(2,1)}, bf16[2,4,256,128]{3,2,1,0:T(8,128)(2,1)S(1)}, u32[]{:S(2)}) copy-start(bf16[2,4,256,128]{3,2,1,0:T(8,128)(2,1)S(1)} %pad_maximum_fusion.1.refs_1_) | copy-start | bytes 1572868
  33.6 14.4 %collective-permute-start.5 = (bf16[2,4,256,128]{3,2,1,0:T(8,128)(2,1)S(1)}, bf16[2,4,256,128]{3,2,1,0:T(8,128)(2,1)}, u32[]{:S(2)}, u32[]{:S(2)}) collective-permute-start(bf16[2,4,256,128]{3,2,1,0:T(8,128)(2,1)S(1)} %pad_maximum_fusion.1.refs_1_), channel_id=1, source_target_pairs={{0,12},{1,13},{2,14},{3,15},{4,0},{5,1},{6,2},{7,3},{8,4},{9,5},{1... | collective-permute-start | bytes 1572872 | tf_op jit(solution)/shard_map/ppermute | solution.py:26
  35.5 16.1 %collective-permute-start.14 = (bf16[2,4,256,128]{3,2,1,0:T(8,128)(2,1)S(1)}, bf16[2,4,256,128]{3,2,1,0:T(8,128)(2,1)S(1)}, u32[]{:S(2)}, u32[]{:S(2)}) collective-permute-start(bf16[2,4,256,128]{3,2,1,0:T(8,128)(2,1)S(1)} %pad_maximum_fusion.1.refs_1_), channel_id=1, source_target_pairs={{0,4},{1,5},{2,6},{3,7},{4,8},{5,9},{6,10},{7,11},{8,12},{9,13},{1... | collective-permute-start | bytes 1572872 | tf_op jit(solution)/shard_map/ppermute | solution.py:26
  35.8 21.0 %collective-permute-start.16 = (bf16[2,4,256,128]{3,2,1,0:T(8,128)(2,1)S(1)}, bf16[2,4,256,128]{3,2,1,0:T(8,128)(2,1)}, u32[]{:S(2)}, u32[]{:S(2)}) collective-permute-start(bf16[2,4,256,128]{3,2,1,0:T(8,128)(2,1)S(1)} %pad_maximum_fusion.3.refs_3_), channel_id=1, source_target_pairs={{0,1},{1,2},{2,3},{3,0},{4,5},{5,6},{6,7},{7,4},{8,9},{9,10},{10,1... | collective-permute-start | bytes 1572872 | tf_op jit(solution)/shard_map/ppermute | solution.py:26
  36.9 24.4 %copy-start.31 = (bf16[2,4,256,128]{3,2,1,0:T(8,128)(2,1)}, bf16[2,4,256,128]{3,2,1,0:T(8,128)(2,1)S(1)}, u32[]{:S(2)}) copy-start(bf16[2,4,256,128]{3,2,1,0:T(8,128)(2,1)S(1)} %pad_maximum_fusion.refs_0_) | copy-start | bytes 1572868
  37.0 22.3 %collective-permute-start.1 = (bf16[2,4,256,128]{3,2,1,0:T(8,128)(2,1)S(1)}, bf16[2,4,256,128]{3,2,1,0:T(8,128)(2,1)}, u32[]{:S(2)}, u32[]{:S(2)}) collective-permute-start(bf16[2,4,256,128]{3,2,1,0:T(8,128)(2,1)S(1)} %pad_maximum_fusion.refs_0_), channel_id=1, source_target_pairs={{0,4},{1,5},{2,6},{3,7},{4,8},{5,9},{6,10},{7,11},{8,12},{9,13},{1... | collective-permute-start | bytes 1572872 | tf_op jit(solution)/shard_map/ppermute | solution.py:26
  42.5 18.8 %collective-permute-start.15 = (bf16[2,4,256,128]{3,2,1,0:T(8,128)(2,1)S(1)}, bf16[2,4,256,128]{3,2,1,0:T(8,128)(2,1)}, u32[]{:S(2)}, u32[]{:S(2)}) collective-permute-start(bf16[2,4,256,128]{3,2,1,0:T(8,128)(2,1)S(1)} %pad_maximum_fusion.refs_0_), channel_id=1, source_target_pairs={{0,12},{1,13},{2,14},{3,15},{4,0},{5,1},{6,2},{7,3},{8,4},{9,5},{1... | collective-permute-start | bytes 1572872 | tf_op jit(solution)/shard_map/ppermute | solution.py:26
  48.0 13.2 %collective-permute-start.8 = (bf16[2,4,256,128]{3,2,1,0:T(8,128)(2,1)}, bf16[2,4,256,128]{3,2,1,0:T(8,128)(2,1)}, u32[]{:S(2)}, u32[]{:S(2)}) collective-permute-start(bf16[2,4,256,128]{3,2,1,0:T(8,128)(2,1)} %pad_maximum_fusion.2.refs_2_), channel_id=1, source_target_pairs={{0,1},{1,2},{2,3},{3,0},{4,5},{5,6},{6,7},{7,4},{8,9},{9,10},{10,1... | collective-permute-start | bytes 1572872 | tf_op jit(solution)/shard_map/ppermute | solution.py:26
  51.6 9.5 %copy-start.33 = (bf16[2,4,256,128]{3,2,1,0:T(8,128)(2,1)}, bf16[2,4,256,128]{3,2,1,0:T(8,128)(2,1)S(1)}, u32[]{:S(2)}) copy-start(bf16[2,4,256,128]{3,2,1,0:T(8,128)(2,1)S(1)} %collective-permute-done.14.refs_1_) | copy-start | bytes 1572868
  51.6 19.8 %collective-permute-start.17 = (bf16[2,4,256,128]{3,2,1,0:T(8,128)(2,1)}, bf16[2,4,256,128]{3,2,1,0:T(8,128)(2,1)}, u32[]{:S(2)}, u32[]{:S(2)}) collective-permute-start(bf16[2,4,256,128]{3,2,1,0:T(8,128)(2,1)} %pad_maximum_fusion.2.refs_2_), channel_id=1, source_target_pairs={{0,3},{1,0},{2,1},{3,2},{4,7},{5,4},{6,5},{7,6},{8,11},{9,8},{10,9... | collective-permute-start | bytes 1572872 | tf_op jit(solution)/shard_map/ppermute | solution.py:26
  56.8 27.2 %collective-permute-start.13 = (bf16[2,4,256,128]{3,2,1,0:T(8,128)(2,1)}, bf16[2,4,256,128]{3,2,1,0:T(8,128)(2,1)S(1)}, u32[]{:S(2)}, u32[]{:S(2)}) collective-permute-start(bf16[2,4,256,128]{3,2,1,0:T(8,128)(2,1)} %collective-permute-done.12.refs_7_), channel_id=1, source_target_pairs={{0,3},{1,0},{2,1},{3,2},{4,7},{5,4},{6,5},{7,6},{8,11},{9,8},{10,9... | collective-permute-start | bytes 1572872 | tf_op jit(solution)/shard_map/ppermute | solution.py:26
  59.3 24.7 %collective-permute-start.6 = (bf16[2,4,256,128]{3,2,1,0:T(8,128)(2,1)}, bf16[2,4,256,128]{3,2,1,0:T(8,128)(2,1)S(1)}, u32[]{:S(2)}, u32[]{:S(2)}) collective-permute-start(bf16[2,4,256,128]{3,2,1,0:T(8,128)(2,1)} %collective-permute-done.5.refs_3_), channel_id=1, source_target_pairs={{0,12},{1,13},{2,14},{3,15},{4,0},{5,1},{6,2},{7,3},{8,4},{9,5},{1... | collective-permute-start | bytes 1572872 | tf_op jit(solution)/shard_map/ppermute | solution.py:26
  61.2 22.9 %collective-permute-start.2 = (bf16[2,4,256,128]{3,2,1,0:T(8,128)(2,1)}, bf16[2,4,256,128]{3,2,1,0:T(8,128)(2,1)S(1)}, u32[]{:S(2)}, u32[]{:S(2)}) collective-permute-start(bf16[2,4,256,128]{3,2,1,0:T(8,128)(2,1)} %collective-permute-done.1.refs_0_), channel_id=1, source_target_pairs={{0,4},{1,5},{2,6},{3,7},{4,8},{5,9},{6,10},{7,11},{8,12},{9,13},{1... | collective-permute-start | bytes 1572872 | tf_op jit(solution)/shard_map/ppermute | solution.py:26
  61.3 22.7 %collective-permute-start.9 = (bf16[2,4,256,128]{3,2,1,0:T(8,128)(2,1)}, bf16[2,4,256,128]{3,2,1,0:T(8,128)(2,1)S(1)}, u32[]{:S(2)}, u32[]{:S(2)}) collective-permute-start(bf16[2,4,256,128]{3,2,1,0:T(8,128)(2,1)} %collective-permute-done.8.refs_4_), channel_id=1, source_target_pairs={{0,1},{1,2},{2,3},{3,0},{4,5},{5,6},{6,7},{7,4},{8,9},{9,10},{10,1... | collective-permute-start | bytes 1572872 | tf_op jit(solution)/shard_map/ppermute | solution.py:26
  63.0 1.0 copy-start.28
  64.1 1.0 copy-start.30
  65.1 1.0 copy-start.32
  71.4 12.6 %copy-start.9 = (bf16[4,256,256]{2,1,0:T(8,128)(2,1)}, bf16[4,256,256]{2,1,0:T(8,128)(2,1)S(1)}, u32[]{:S(2)}) copy-start(bf16[4,256,256]{2,1,0:T(8,128)(2,1)S(1)} %get-tuple-element.45.refs_11_) | copy-start | bytes 1572868
  71.4 1.2 copy-start.34
  72.6 37.2 %copy-start.36 = (s32[4]{0:T(128)S(1)}, s32[4]{0:T(128)}, u32[]{:S(2)}) copy-start(s32[4]{0:T(128)} %param.15) | copy-start | bytes 52
  84.1 25.8 %copy-start.1 = (bf16[32,256,256]{2,1,0:T(8,128)(2,1)S(1)}, bf16[32,256,256]{2,1,0:T(8,128)(2,1)}, u32[]{:S(2)}) copy-start(bf16[32,256,256]{2,1,0:T(8,128)(2,1)} %all-gather.2.cloned.1.call-done.right_hbm.right) | copy-start | bytes 12582916
  84.1 1.2 copy-start.4
  85.3 1.3 copy-start.6
  86.6 1.0 copy-start.8
  87.6 1.0 copy-start.10
  88.6 1.0 copy-start.12
  89.7 1.0 copy-start.14
  90.7 1.0 copy-start.16
  91.8 1.0 copy-start.18
  92.8 1.0 copy-start.20
  93.9 1.0 copy-start.22
  94.9 1.0 copy-start.24
  95.9 1.0 copy-start.26
  107.0 14.0 %collective-permute-start.22 = (bf16[2,2,256,256]{3,2,1,0:T(8,128)(2,1)S(1)}, bf16[2,2,256,256]{3,2,1,0:T(8,128)(2,1)S(1)}, u32[]{:S(2)}, u32[]{:S(2)}) collective-permute-start(bf16[2,2,256,256]{3,2,1,0:T(8,128)(2,1)S(1)} %get-tuple-element.58), channel_id=1, source_target_pairs={{0,12},{1,13},{2,14},{3,15},{4,0},{5,1},{6,2},{7,3},{8,4},{9,5},{1... | collective-permute-start | bytes 1572872 | tf_op jit(solution)/shard_map/ppermute | solution.py:26
  109.8 16.1 %collective-permute-start.19 = (bf16[2,2,256,256]{3,2,1,0:T(8,128)(2,1)S(1)}, bf16[2,2,256,256]{3,2,1,0:T(8,128)(2,1)S(1)}, u32[]{:S(2)}, u32[]{:S(2)}) collective-permute-start(bf16[2,2,256,256]{3,2,1,0:T(8,128)(2,1)S(1)} %get-tuple-element.54), channel_id=1, source_target_pairs={{0,4},{1,5},{2,6},{3,7},{4,8},{5,9},{6,10},{7,11},{8,12},{9,13},{1... | collective-permute-start | bytes 1572872 | tf_op jit(solution)/shard_map/ppermute | solution.py:26
  115.5 17.6 %collective-permute-start.21 = (bf16[2,2,256,256]{3,2,1,0:T(8,128)(2,1)S(1)}, bf16[2,2,256,256]{3,2,1,0:T(8,128)(2,1)S(1)}, u32[]{:S(2)}, u32[]{:S(2)}) collective-permute-start(bf16[2,2,256,256]{3,2,1,0:T(8,128)(2,1)S(1)} %get-tuple-element.56), channel_id=1, source_target_pairs={{0,4},{1,5},{2,6},{3,7},{4,8},{5,9},{6,10},{7,11},{8,12},{9,13},{1... | collective-permute-start | bytes 1572872 | tf_op jit(solution)/shard_map/ppermute | solution.py:26
  115.6 28.5 %collective-permute-start.18 = (bf16[2,2,256,256]{3,2,1,0:T(8,128)(2,1)S(1)}, bf16[2,2,256,256]{3,2,1,0:T(8,128)(2,1)S(1)}, u32[]{:S(2)}, u32[]{:S(2)}) collective-permute-start(bf16[2,2,256,256]{3,2,1,0:T(8,128)(2,1)S(1)} %get-tuple-element.52), channel_id=1, source_target_pairs={{0,12},{1,13},{2,14},{3,15},{4,0},{5,1},{6,2},{7,3},{8,4},{9,5},{1... | collective-permute-start | bytes 1572872 | tf_op jit(solution)/shard_map/ppermute | solution.py:26
  118.9 9.8 %collective-permute-start.31 = (bf16[2,2,256,256]{3,2,1,0:T(8,128)(2,1)S(1)}, bf16[2,2,256,256]{3,2,1,0:T(8,128)(2,1)S(1)}, u32[]{:S(2)}, u32[]{:S(2)}) collective-permute-start(bf16[2,2,256,256]{3,2,1,0:T(8,128)(2,1)S(1)} %get-tuple-element.68), channel_id=1, source_target_pairs={{0,3},{1,0},{2,1},{3,2},{4,7},{5,4},{6,5},{7,6},{8,11},{9,8},{10,9... | collective-permute-start | bytes 1572872 | tf_op jit(solution)/shard_map/ppermute | solution.py:26
  121.0 27.7 %collective-permute-start.30 = (bf16[2,2,256,256]{3,2,1,0:T(8,128)(2,1)S(1)}, bf16[2,2,256,256]{3,2,1,0:T(8,128)(2,1)S(1)}, u32[]{:S(2)}, u32[]{:S(2)}) collective-permute-start(bf16[2,2,256,256]{3,2,1,0:T(8,128)(2,1)S(1)} %get-tuple-element.66), channel_id=1, source_target_pairs={{0,1},{1,2},{2,3},{3,0},{4,5},{5,6},{6,7},{7,4},{8,9},{9,10},{10,1... | collective-permute-start | bytes 1572872 | tf_op jit(solution)/shard_map/ppermute | solution.py:26
  125.9 18.1 %collective-permute-start.28 = (bf16[2,2,256,256]{3,2,1,0:T(8,128)(2,1)S(1)}, bf16[2,2,256,256]{3,2,1,0:T(8,128)(2,1)S(1)}, u32[]{:S(2)}, u32[]{:S(2)}) collective-permute-start(bf16[2,2,256,256]{3,2,1,0:T(8,128)(2,1)S(1)} %get-tuple-element.64), channel_id=1, source_target_pairs={{0,1},{1,2},{2,3},{3,0},{4,5},{5,6},{6,7},{7,4},{8,9},{9,10},{10,1... | collective-permute-start | bytes 1572872 | tf_op jit(solution)/shard_map/ppermute | solution.py:26
  128.7 15.5 %collective-permute-start.23 = (bf16[2,2,256,256]{3,2,1,0:T(8,128)(2,1)S(1)}, bf16[2,2,256,256]{3,2,1,0:T(8,128)(2,1)S(1)}, u32[]{:S(2)}, u32[]{:S(2)}) collective-permute-start(bf16[2,2,256,256]{3,2,1,0:T(8,128)(2,1)S(1)} %add_convert_fusion.2), channel_id=1, source_target_pairs={{0,12},{1,13},{2,14},{3,15},{4,0},{5,1},{6,2},{7,3},{8,4},{9,5},{1... | collective-permute-start | bytes 1572872 | tf_op jit(solution)/shard_map/ppermute | solution.py:26
  133.1 13.4 %collective-permute-start.20 = (bf16[2,2,256,256]{3,2,1,0:T(8,128)(2,1)S(1)}, bf16[2,2,256,256]{3,2,1,0:T(8,128)(2,1)S(1)}, u32[]{:S(2)}, u32[]{:S(2)}) collective-permute-start(bf16[2,2,256,256]{3,2,1,0:T(8,128)(2,1)S(1)} %add_convert_fusion.3), channel_id=1, source_target_pairs={{0,4},{1,5},{2,6},{3,7},{4,8},{5,9},{6,10},{7,11},{8,12},{9,13},{1... | collective-permute-start | bytes 1572872 | tf_op jit(solution)/shard_map/ppermute | solution.py:26
  144.0 14.9 %collective-permute-start.32 = (bf16[2,2,256,256]{3,2,1,0:T(8,128)(2,1)S(1)}, bf16[2,2,256,256]{3,2,1,0:T(8,128)(2,1)S(1)}, u32[]{:S(2)}, u32[]{:S(2)}) collective-permute-start(bf16[2,2,256,256]{3,2,1,0:T(8,128)(2,1)S(1)} %add_convert_fusion), channel_id=1, source_target_pairs={{0,3},{1,0},{2,1},{3,2},{4,7},{5,4},{6,5},{7,6},{8,11},{9,8},{10,9... | collective-permute-start | bytes 1572872 | tf_op jit(solution)/shard_map/ppermute | solution.py:26
  144.2 25.0 %collective-permute-start.27 = (bf16[2,2,256,256]{3,2,1,0:T(8,128)(2,1)S(1)}, bf16[2,2,256,256]{3,2,1,0:T(8,128)(2,1)S(1)}, u32[]{:S(2)}, u32[]{:S(2)}) collective-permute-start(bf16[2,2,256,256]{3,2,1,0:T(8,128)(2,1)S(1)} %get-tuple-element.62), channel_id=1, source_target_pairs={{0,3},{1,0},{2,1},{3,2},{4,7},{5,4},{6,5},{7,6},{8,11},{9,8},{10,9... | collective-permute-start | bytes 1572872 | tf_op jit(solution)/shard_map/ppermute | solution.py:26
  144.2 26.3 %collective-permute-start.29 = (bf16[2,2,256,256]{3,2,1,0:T(8,128)(2,1)S(1)}, bf16[2,2,256,256]{3,2,1,0:T(8,128)(2,1)S(1)}, u32[]{:S(2)}, u32[]{:S(2)}) collective-permute-start(bf16[2,2,256,256]{3,2,1,0:T(8,128)(2,1)S(1)} %add_convert_fusion.1), channel_id=1, source_target_pairs={{0,1},{1,2},{2,3},{3,0},{4,5},{5,6},{6,7},{7,4},{8,9},{9,10},{10,1... | collective-permute-start | bytes 1572872 | tf_op jit(solution)/shard_map/ppermute | solution.py:26
  146.6 24.1 %collective-permute-start.24 = (bf16[2,256,256]{2,1,0:T(8,128)(2,1)S(1)}, bf16[2,256,256]{2,1,0:T(8,128)(2,1)S(1)}, u32[]{:S(2)}, u32[]{:S(2)}) collective-permute-start(bf16[2,256,256]{2,1,0:T(8,128)(2,1)S(1)} %get-tuple-element.71), channel_id=1, source_target_pairs={{0,2},{1,3},{2,0},{3,1},{4,6},{5,7},{6,4},{7,5},{8,10},{9,11},{10,... | collective-permute-start | bytes 786440 | tf_op jit(solution)/shard_map/ppermute | solution.py:26
  148.7 25.3 %collective-permute-start.25 = (bf16[2,256,256]{2,1,0:T(8,128)(2,1)S(1)}, bf16[2,256,256]{2,1,0:T(8,128)(2,1)S(1)}, u32[]{:S(2)}, u32[]{:S(2)}) collective-permute-start(bf16[2,256,256]{2,1,0:T(8,128)(2,1)S(1)} %get-tuple-element.72), channel_id=1, source_target_pairs={{0,1},{1,2},{2,3},{3,0},{4,5},{5,6},{6,7},{7,4},{8,9},{9,10},{10,1... | collective-permute-start | bytes 786440 | tf_op jit(solution)/shard_map/ppermute | solution.py:26
  158.9 16.0 %collective-permute-start.26 = (bf16[2,256,256]{2,1,0:T(8,128)(2,1)S(1)}, bf16[2,256,256]{2,1,0:T(8,128)(2,1)S(1)}, u32[]{:S(2)}, u32[]{:S(2)}) collective-permute-start(bf16[2,256,256]{2,1,0:T(8,128)(2,1)S(1)} %fusion.5), channel_id=1, source_target_pairs={{0,3},{1,0},{2,1},{3,2},{4,7},{5,4},{6,5},{7,6},{8,11},{9,8},{10,9... | collective-permute-start | bytes 786440 | tf_op jit(solution)/shard_map/ppermute | solution.py:26
  169.2 8.0 %collective-permute-start.33 = (bf16[2,256,256]{2,1,0:T(8,128)(2,1)S(1)}, bf16[2,256,256]{2,1,0:T(8,128)(2,1)S(1)}, u32[]{:S(2)}, u32[]{:S(2)}) collective-permute-start(bf16[2,256,256]{2,1,0:T(8,128)(2,1)S(1)} %get-tuple-element.73), channel_id=1, source_target_pairs={{0,8},{1,9},{2,10},{3,11},{4,12},{5,13},{6,14},{7,15},{8,0},{9,1},... | collective-permute-start | bytes 786440 | tf_op jit(solution)/shard_map/ppermute | solution.py:26
  170.6 9.3 %collective-permute-start.34 = (bf16[2,256,256]{2,1,0:T(8,128)(2,1)S(1)}, bf16[2,256,256]{2,1,0:T(8,128)(2,1)S(1)}, u32[]{:S(2)}, u32[]{:S(2)}) collective-permute-start(bf16[2,256,256]{2,1,0:T(8,128)(2,1)S(1)} %get-tuple-element.74), channel_id=1, source_target_pairs={{0,4},{1,5},{2,6},{3,7},{4,8},{5,9},{6,10},{7,11},{8,12},{9,13},{1... | collective-permute-start | bytes 786440 | tf_op jit(solution)/shard_map/ppermute | solution.py:26
  170.7 9.2 %collective-permute-start.35 = (bf16[2,256,256]{2,1,0:T(8,128)(2,1)S(1)}, bf16[2,256,256]{2,1,0:T(8,128)(2,1)S(1)}, u32[]{:S(2)}, u32[]{:S(2)}) collective-permute-start(bf16[2,256,256]{2,1,0:T(8,128)(2,1)S(1)} %fusion.1), channel_id=1, source_target_pairs={{0,12},{1,13},{2,14},{3,15},{4,0},{5,1},{6,2},{7,3},{8,4},{9,5},{1... | collective-permute-start | bytes 786440 | tf_op jit(solution)/shard_map/ppermute | solution.py:26
  (11 other events, 8.9 us)
Sparse Core Ops, SparseCore 0:
  9.5 34.5 all-gather.1

commit v4 on v0

v4 whole, which is shorter than its diff:
```python
import functools

import jax
import jax.numpy as jnp
from jax import lax
from jax.experimental import pallas as pl
from jax.experimental.pallas import tpu as pltpu
from jax.sharding import PartitionSpec as P

BAND = 16
RING = 4
STATES = RING * RING
CORES = 2
LIMIT = 48 << 20
CALLS = ((0, 2), (1, 3))
AXIS = ((0, 0), (0, 1), (0, 2), (0, 3), (1, 0), (2, 0), (3, 0))
NEAR = ((1, 1), (1, 3), (3, 1), (3, 3))
FAR = ((1, 2), (2, 1), (2, 2), (2, 3), (3, 2))

HBM = pl.BlockSpec(memory_space=pltpu.HBM)
SMEM = pl.BlockSpec(memory_space=pltpu.SMEM)
VMEM = pl.BlockSpec(memory_space=pltpu.VMEM)


def in_hbm(value):
    return pltpu.with_memory_space_constraint(value, pltpu.HBM)


def hop(value, axis, distance=1):
    pairs = []
    for row in range(RING * CORES):
        for col in range(STATES):
            step = distance if row % CORES == 0 else -distance
            y, z, x = row // CORES, col // RING, col % RING
            y, z, x = (
                (v + (step if name == axis else 0)) % RING
                for name, v in (("y", y), ("z", z), ("x", x))
            )
            target = (y * CORES + row % CORES) * STATES + z * RING + x
            pairs.append((row * STATES + col, target))
    return lax.ppermute(value, ("row", "col"), pairs)


def send(value, axis, step):
    pairs = []
    for device in range(STATES):
        z, x = device // RING, device % RING
        if axis == "z":
            z = (z + step) % RING
        else:
            x = (x + step) % RING
        pairs.append((device, z * RING + x))
    return lax.ppermute(value, "col", pairs)


def swap_cores(value):
    return lax.ppermute(value, "row", [(r, r ^ 1) for r in range(RING * CORES)])


def add(*parts):
    total = parts[0].astype(jnp.float32)
    for part in parts[1:]:
        total += part.astype(jnp.float32)
    return total.astype(jnp.bfloat16)


def left_product(left, src_ref, a, block):
    rows = jnp.concatenate([block(src_ref[a, k]) for k in range(2)], axis=0)
    wide = jnp.concatenate([left[a, 0], left[a, 1]], axis=1)
    return jnp.dot(wide, rows, preferred_element_type=jnp.float32).astype(jnp.bfloat16)


def joined(first, second):
    return lambda j: jnp.concatenate([first[j], second[j]], axis=1)


def axis_kernel(src_ref, left_hbm, *refs):
    count = len(AXIS)
    blocks_hbm, out_hbm, (left, blocks, out, sem) = refs[:count], refs[count], refs[count + 1 :]
    get_left = pltpu.make_async_copy(left_hbm, left, sem.at[0])
    gets = [
        pltpu.make_async_copy(blocks_hbm[n], blocks.at[n], sem.at[1 + n]) for n in range(count)
    ]
    puts = [
        pltpu.make_async_copy(out.at[n], out_hbm.at[n], sem.at[1 + count + n])
        for n in range(count)
    ]
    get_left.start()
    for get in gets:
        get.start()
    get_left.wait()
    for n in range(count):
        gets[n].wait()
        for a in range(left.shape[0]):
            out[n, a] = left_product(left, src_ref, a, lambda j: blocks[n, j])
        puts[n].start()
    for put in puts:
        put.wait()


def near_kernel(src_ref, left_hbm, *refs):
    pieces_hbm, out_hbm, (left, pieces, out, sem) = refs[:4], refs[4], refs[5:]
    get_left = pltpu.make_async_copy(left_hbm, left, sem.at[0])
    gets = [pltpu.make_async_copy(pieces_hbm[n], pieces.at[n], sem.at[1 + n]) for n in range(4)]
    puts = [pltpu.make_async_copy(out.at[n], out_hbm.at[n], sem.at[5 + n]) for n in range(4)]
    for get in [get_left] + gets:
        get.start()
    for get in [get_left] + gets:
        get.wait()
    for n, (i, k) in enumerate(NEAR):
        block = joined(pieces.at[i // 2, k - 1], pieces.at[2 + k // 2, i - 1])
        for a in range(left.shape[0]):
            out[n, a] = left_product(left, src_ref, a, block)
        puts[n].start()
    for put in puts:
        put.wait()


def left_parts(kernel, count, src, left, pieces):
    tiles, _, tile, _ = left.shape
    out = (count, tiles, tile, tile)
    return pl.pallas_call(
        kernel,
        out_shape=pltpu.HBM(out, jnp.bfloat16),
        in_specs=[SMEM] + [HBM] * (1 + len(pieces)),
        out_specs=HBM,
        scratch_shapes=[
            pltpu.VMEM(left.shape, jnp.bfloat16),
            pltpu.VMEM((len(pieces),) + pieces[0].shape, jnp.bfloat16),
            pltpu.VMEM(out, jnp.bfloat16),
            pltpu.SemaphoreType.DMA((1 + len(pieces) + count,)),
        ],
        compiler_params=pltpu.CompilerParams(vmem_limit_bytes=LIMIT),
        cost_estimate=pl.CostEstimate(
            flops=count * tiles * 4 * tile**3, bytes_accessed=5 << 20, transcendentals=0
        ),
        name="left_parts",
    )(src, left, *(in_hbm(piece) for piece in pieces))


def mix_matrix(two_site, z, x, flow):
    size = STATES * BAND
    slot = lax.broadcasted_iota(jnp.int32, (size, STATES), 0) // BAND
    lane = lax.broadcasted_iota(jnp.int32, (size, STATES), 1)
    target = ((z + slot // RING) & 3) * RING + ((x + slot % RING) & 3)
    source = jnp.zeros_like(slot)
    for n, (i, k) in enumerate(AXIS + NEAR + FAR):
        state = ((z - flow * i) & 3) * RING + ((x - flow * k) & 3)
        source = jnp.where(slot == n, state, source)
    spread = lambda state: jnp.where(state == lane, 1.0, 0.0).astype(jnp.bfloat16)
    half = jnp.dot(spread(target), two_site, preferred_element_type=jnp.float32)
    full = lax.dot_general(
        half.astype(jnp.bfloat16),
        spread(source),
        (((1,), (1,)), ((), ())),
        preferred_element_type=jnp.float32,
    )
    row = lax.broadcasted_iota(jnp.int32, (size, size), 0)
    col = lax.broadcasted_iota(jnp.int32, (size, size), 1)
    return jnp.where(row % BAND == col % BAND, full, 0.0).astype(jnp.bfloat16)


def term(mixed, right, loc_ref, a, state, spot):
    z, x, y, core, flow = spot
    i, k = state
    t = ((z + i) & 3) * RING + ((x + k) & 3)
    group = t // 2
    other = (group + core) & 1
    back = (flow * (1 - 2 * other) * (y - group // CORES)) & 3
    tile = (other * RING + back) * 4 + loc_ref[t, 0, a]
    return jnp.dot(mixed, right[tile], preferred_element_type=jnp.float32).astype(jnp.bfloat16)


def spot_of():
    c, r = lax.axis_index("col"), lax.axis_index("row")
    core = r % CORES
    return c // RING, c % RING, r // CORES, core, 1 - 2 * core


def slot_state(half, ahead, inner):
    return (ahead, inner) if half == 0 else (inner, ahead)


def apply_kernel(chosen, src_ref, loc_ref, two_site_ref, token_ref, left_hbm, *refs):
    right_hbm, pieces_hbm, near_hbm, refs = refs[:8], refs[8:14], refs[14:16], refs[16:]
    outs, (left, right, first, second, part, mix, mixed, sem) = refs[:-8], refs[-8:]
    tile = left.shape[-1]
    spot = spot_of()
    z, x, _, _, flow = spot
    outs, passed = outs[:-1], outs[-1]
    passed[...] = token_ref[...]

    gets = [pltpu.make_async_copy(left_hbm, left, sem.at[0])]
    for which, pieces in enumerate((first, second)):
        behind, ahead, far = pieces_hbm[3 * which : 3 * which + 3]
        gets += [
            pltpu.make_async_copy(behind.at[1], pieces.at[0, 1], sem.at[1 + 3 * which]),
            pltpu.make_async_copy(ahead.at[1], pieces.at[2, 1], sem.at[2 + 3 * which]),
            pltpu.make_async_copy(far, pieces.at[1], sem.at[3 + 3 * which]),
        ]
    get_right = [
        pltpu.make_async_copy(right_hbm[n], right.at[pl.ds(4 * n, 4)], sem.at[7 + n])
        for n in range(8)
    ]
    get_near = [
        [
            pltpu.make_async_copy(
                near_hbm[0].at[:, a], part.at[place, pl.ds(0, 7)], sem.at[15 + 2 * place]
            ),
            pltpu.make_async_copy(
                near_hbm[1].at[:, a], part.at[place, pl.ds(7, 4)], sem.at[16 + 2 * place]
            ),
        ]
        for place, a in enumerate(chosen)
    ]
    for get in gets + get_near[0] + get_right:
        get.start()
    for later in get_near[1:]:
        for get in later:
            get.start()
    mix[...] = mix_matrix(two_site_ref[0], z, x, flow)
    for get in gets:
        get.wait()

    order = AXIS + NEAR + FAR
    for number, a in enumerate(chosen):
        half = a // 2
        for n, (i, k) in enumerate(FAR):
            block = joined(first.at[i - 1, k - 1], second.at[k - 1, i - 1])
            part[number, len(AXIS) + len(NEAR) + n] = left_product(left, src_ref, a, block)
        for get in get_near[number]:
            get.wait()
        for band in range(tile // BAND):
            rows = pl.ds(band * BAND, BAND)
            stacked = part[number, :, rows, :].reshape(STATES * BAND, tile)
            product = jnp.dot(mix[...], stacked, preferred_element_type=jnp.float32)
            mixed[:, rows, :] = product.astype(jnp.bfloat16).reshape(STATES, BAND, tile)
        if number == 0:
            for get in get_right:
                get.wait()
        for ring in (2, 3, 1, 0):
            for inner in range(RING):
                i, k = slot_state(half, (flow * ring) & 3, (flow * inner) & 3)
                outs[number * RING + ring][inner] = term(
                    mixed[i * RING + k], right, loc_ref, a, (i, k), spot
                )


def apply_terms(chosen, src, loc, two_site, token, left, right, pieces, near):
    tiles, _, tile, _ = left.shape
    count = len(chosen)
    out = jax.ShapeDtypeStruct((RING, tile, tile), jnp.bfloat16)
    side = (RING - 1, RING - 1) + pieces[0].shape[1:]
    return pl.pallas_call(
        functools.partial(apply_kernel, chosen),
        out_shape=[out] * (RING * count) + [jax.ShapeDtypeStruct(token.shape, token.dtype)],
        in_specs=[SMEM, SMEM, VMEM, VMEM] + [HBM] * 17,
        out_specs=[VMEM] * (RING * count + 1),
        scratch_shapes=[
            pltpu.VMEM(left.shape, jnp.bfloat16),
            pltpu.VMEM((32, tile, tile), jnp.bfloat16),
            pltpu.VMEM(side, jnp.bfloat16),
            pltpu.VMEM(side, jnp.bfloat16),
            pltpu.VMEM((count, STATES, tile, tile), jnp.bfloat16),
            pltpu.VMEM((STATES * BAND, STATES * BAND), jnp.bfloat16),
            pltpu.VMEM((STATES, tile, tile), jnp.bfloat16),
            pltpu.SemaphoreType.DMA((15 + 2 * count,)),
        ],
        compiler_params=pltpu.CompilerParams(vmem_limit_bytes=LIMIT),
        cost_estimate=pl.CostEstimate(
            flops=count * 80 * tile**3, bytes_accessed=8 << 20, transcendentals=0
        ),
        name="apply_terms",
    )(src, loc, two_site, token, left, *(in_hbm(v) for v in (*right, *pieces, *near)))


def ring_sum(blocks, axis):
    own, behind, far, ahead = blocks
    straight = hop(ahead, axis, -1)
    return own, straight, hop(add(behind, hop(far, axis, 1)), axis, 1)


def last_sum(tiles, axis):
    blocks = [
        jnp.stack([add(*(part[n] for part in parts)) for parts in tiles]) for n in range(RING)
    ]
    return add(*ring_sum(blocks, axis))


def per_device(
    wavefunction, env_left, left_src, two_site, env_right, right_loc, left_size, right_size
):
    tile = wavefunction.shape[3]
    tiles = wavefunction.shape[0]
    src, left = left_src[0], env_left[0]

    shard, cut = wavefunction[:, 0], tile // 2
    behind_x, behind_z = hop(shard, "x", 1), hop(shard, "z", 1)
    ahead_x, ahead_z = hop(shard, "x", -1), hop(shard, "z", -1)
    far_x, far_z = hop(behind_x, "x", 1), hop(behind_z, "z", 1)

    env_right, right_loc, _ = lax.optimization_barrier((env_right, right_loc, behind_x))
    lane = lax.broadcasted_iota(jnp.int32, (1, 1, tile), 2)
    right = jnp.swapaxes(env_right[0], 1, 2)
    right = [jnp.where(lane < right_size[:, None, None], right, 0).astype(jnp.bfloat16)]
    for _ in range(RING - 1):
        right.append(hop(right[-1], "y"))
    right += [swap_cores(block) for block in right]
    loc = lax.all_to_all(
        jnp.broadcast_to(right_loc[:, 0][None, None], (STATES, 1, tiles)), "col", 0, 0, tiled=True
    )

    axis_blocks = (shard, behind_x, far_x, ahead_x, behind_z, far_z, ahead_z)
    corner_a = jnp.stack([block[:, :, :cut] for block in axis_blocks[1:4]])
    corner_b = jnp.stack([block[:, :, cut:] for block in axis_blocks[4:]])
    behind_a, behind_b = hop(corner_a, "z", 1), hop(corner_b, "x", 1)
    ahead_a, ahead_b = hop(corner_a, "z", -1), hop(corner_b, "x", -1)
    part_axis = left_parts(axis_kernel, len(AXIS), src, left, axis_blocks)
    behind_a, behind_b, part_axis = lax.optimization_barrier((behind_a, behind_b, part_axis))
    far_a, far_b = hop(behind_a, "z", 1), hop(behind_b, "x", 1)
    near = (behind_a, ahead_a, behind_b, ahead_b)
    part_near = left_parts(near_kernel, len(NEAR), src, left, near)

    pieces = (behind_a, ahead_a, far_a, behind_b, ahead_b, far_b)
    token, sums = jnp.zeros((16, 128), jnp.bfloat16), {}
    for chosen in CALLS:
        *outs, token = apply_terms(
            chosen, src, loc, two_site, token, left, right, pieces, (part_axis, part_near)
        )
        token = swap_cores(token)
        for number, a in enumerate(chosen):
            sums[a] = ring_sum(outs[RING * number : RING * (number + 1)], "z" if a < 2 else "x")
    summed = jnp.concatenate(
        [last_sum((sums[0], sums[1]), "x"), last_sum((sums[2], sums[3]), "z")]
    )
    row = lax.broadcasted_iota(jnp.int32, (1, tile, 1), 1)
    inside = row < left_size[:, None, None]
    return jnp.where(inside, summed, 0).astype(jnp.bfloat16)[:, None]


def solution(mesh):
    placed = (
        P("row", "col", None, None),
        P("col", "row", None, None, None),
        P("col", "row", None),
        P("col", None, None),
        P("col", "row", None, None),
        P("row", "col"),
        P("row"),
        P("row"),
    )
    return jax.shard_map(
        per_device,
        mesh=mesh,
        in_specs=placed,
        out_specs=P("row", "col", None, None),
        check_vma=False,
    )
```

time: 598 us -> 148 us (0.25)
  waiting for transfers between devices: 272 us -> 56.6 us
  blocking collectives: 124 us -> 0 us
  local copies, waits for them, and re-layouts: 125 us -> 4.18 us
  starting transfers between devices: 9.58 us -> 55.1 us
  matrix products: 34.7 us -> 0 us
  Pallas kernels: 0 us -> 24.4 us
  between operations: 13.6 us -> 0.43 us
  other arithmetic: 17.2 us -> 6.58 us
    unnamed x3 -> x0, waiting for transfers between devices: 139 us -> none
    all_to_all x1 -> x0, blocking collectives: 102 us -> none  [per_device(): lax.all_to_all(jnp.stack(pieces, axis=1), 'row', split_axis=0, concat_axi...]
    all_to_all x2 -> x1, waiting for transfers between devices: 85.7 us -> 2.9 us  [per_device(): lax.all_to_all(jnp.broadcast_to(right_loc[:, 0][None, None], (STATES, 1,...]
    gather x20 -> x0, local copies, waits for them, and re-layouts: 71.7 us -> none  [the longest x17 65.5 us: per_device(): blocks = whole[left_src[0, position]]]
    ppermute x0 -> x38, waiting for transfers between devices: none -> 53.7 us  [the longest x33 53.7 us: hop(): return lax.ppermute(value, ('row', 'col'), pairs)]
    ppermute x0 -> x38, starting transfers between devices: none -> 47.4 us  [the longest x33 45.4 us: hop(): return lax.ppermute(value, ('row', 'col'), pairs)]
    all_gather x1 -> x0, waiting for transfers between devices: 47.3 us -> none  [per_device(): lax.all_gather(wavefunction, 'col', axis=1, tiled=True)]
    dot_general x10 -> x0, matrix products: 34.7 us -> none  [the longest x4 18.8 us: per_device(): jnp.einsum('kxy,ksyz->sxz', env_left[0, position], blocks, preferred_elem...]
  transfers between devices with their start and end apart: 4 -> 39, of which waited for: 3 -> 17; matrix products, arithmetic and copies ran while one was open for 22% -> 6% of each run, Pallas kernels for 0% -> 12%
where the time goes in v4:
time: 148 us; the launch traced here: 147 us
  waiting for transfers between devices  56.6 us (38%)
  starting transfers between devices  55.1 us (37%)
  Pallas kernels  24.4 us (16%)
  other arithmetic  6.58 us (4%)
  local copies, waits for them, and re-layouts  4.18 us (3%)
    ppermute x33, waiting for transfers between devices, hop(): return lax.ppermute(value, ('row', 'col'), pairs)  53.7 us
    ppermute x33, starting transfers between devices, hop(): return lax.ppermute(value, ('row', 'col'), pairs)  45.4 us
    pallas_call x2, Pallas kernels, apply_terms(): pl.pallas_call(functools.partial(apply_kernel, chosen), out_shape=[out] *...  14.1 us
    pallas_call x2, Pallas kernels, left_parts(): pl.pallas_call(kernel, out_shape=pltpu.HBM(out, jnp.bfloat16), in_specs=[...  10.3 us
    all_to_all x1, starting transfers between devices, per_device(): lax.all_to_all(jnp.broadcast_to(right_loc[:, 0][None, None], (STATES, 1,...  7.79 us
  transfers between devices with their start and end apart: 39, of which 17 were waited for; matrix products, arithmetic and copies ran while one was open for 6% of the time, Pallas kernels for 12%

profile of v4, /device:TPU:0, one launch (start us, length us, event | category | flops | bytes accessed | tf_op | source)
XLA Modules:
  0.0 147.4 jit_solution(12177951460467553189)
XLA Ops:
  0.0 1.6 %collective-permute-start = (bf16[4,256,256]{2,1,0:T(8,128)(2,1)}, bf16[4,256,256]{2,1,0:T(8,128)(2,1)S(1)}, u32[]{:S(2)}, u32[]{:S(2)}) collective-permute-start(bf16[4,256,256]{2,1,0:T(8,128)(2,1)} %bitcast.32), channel_id=1, source_target_pairs={{0,1},{1,2},{2,3},{3,0},{4,5},{5,6},{6,7},{7,4},{8,9},{9,10},{10,1... | collective-permute-start | bytes 1572872 | tf_op jit(solution)/shard_map/ppermute | solution.py:41
  1.6 1.9 %collective-permute-start.11 = (bf16[4,256,256]{2,1,0:T(8,128)(2,1)}, bf16[4,256,256]{2,1,0:T(8,128)(2,1)S(1)}, u32[]{:S(2)}, u32[]{:S(2)}) collective-permute-start(bf16[4,256,256]{2,1,0:T(8,128)(2,1)} %bitcast.33), channel_id=1, source_target_pairs={{0,4},{1,5},{2,6},{3,7},{4,8},{5,9},{6,10},{7,11},{8,12},{9,13},{1... | collective-permute-start | bytes 1572872 | tf_op jit(solution)/shard_map/ppermute | solution.py:41
  3.5 2.1 %collective-permute-start.13 = (bf16[4,256,256]{2,1,0:T(8,128)(2,1)}, bf16[4,256,256]{2,1,0:T(8,128)(2,1)S(1)}, u32[]{:S(2)}, u32[]{:S(2)}) collective-permute-start(bf16[4,256,256]{2,1,0:T(8,128)(2,1)} %bitcast.34), channel_id=1, source_target_pairs={{0,12},{1,13},{2,14},{3,15},{4,0},{5,1},{6,2},{7,3},{8,4},{9,5},{1... | collective-permute-start | bytes 1572872 | tf_op jit(solution)/shard_map/ppermute | solution.py:41
  5.6 1.7 %collective-permute-start.9 = (bf16[4,256,256]{2,1,0:T(8,128)(2,1)}, bf16[4,256,256]{2,1,0:T(8,128)(2,1)}, u32[]{:S(2)}, u32[]{:S(2)}) collective-permute-start(bf16[4,256,256]{2,1,0:T(8,128)(2,1)} %bitcast.35), channel_id=1, source_target_pairs={{0,3},{1,0},{2,1},{3,2},{4,7},{5,4},{6,5},{7,6},{8,11},{9,8},{10,9... | collective-permute-start | bytes 1572872 | tf_op jit(solution)/shard_map/ppermute | solution.py:41
  7.4 0.7 iota_compare_fusion
  8.1 2.9 %collective-permute-done.refs_1_ = bf16[4,256,256]{2,1,0:T(8,128)(2,1)S(1)} collective-permute-done((bf16[4,256,256]{2,1,0:T(8,128)(2,1)}, bf16[4,256,256]{2,1,0:T(8,128)(2,1)S(1)}, u32[]{:S(2)}, u32[]{:S(2)}) %collective-permute-start) | collective-permute-done | bytes 524320 | tf_op jit(solution)/shard_map/ppermute | solution.py:41
  11.0 1.4 copy.9
  12.4 0.8 fusion.1.refs_0_
  13.3 1.7 %collective-permute-start.1 = (bf16[4,256,256]{2,1,0:T(8,128)(2,1)}, bf16[4,256,256]{2,1,0:T(8,128)(2,1)}, u32[]{:S(2)}, u32[]{:S(2)}) collective-permute-start(bf16[4,256,256]{2,1,0:T(8,128)(2,1)} %fusion.1.refs_0_), channel_id=1, source_target_pairs={{0,32},{1,33},{2,34},{3,35},{4,36},{5,37},{6,38},{7,39},{8,40},{9,... | collective-permute-start | bytes 1572872 | tf_op jit(solution)/shard_map/ppermute | solution.py:41
  15.0 1.6 %collective-permute-start.8 = (bf16[4,256,256]{2,1,0:T(8,128)(2,1)S(1)}, bf16[4,256,256]{2,1,0:T(8,128)(2,1)S(1)}, u32[]{:S(2)}, u32[]{:S(2)}) collective-permute-start(bf16[4,256,256]{2,1,0:T(8,128)(2,1)S(1)} %collective-permute-done.refs_1_), channel_id=1, source_target_pairs={{0,1},{1,2},{2,3},{3,0},{4,5},{5,6},{6,7},{7,4},{8,9},{9,10},{10,1... | collective-permute-start | bytes 1572872 | tf_op jit(solution)/shard_map/ppermute | solution.py:41
  16.7 4.2 %collective-permute-start.12 = (bf16[4,256,256]{2,1,0:T(8,128)(2,1)S(1)}, bf16[4,256,256]{2,1,0:T(8,128)(2,1)S(1)}, u32[]{:S(2)}, u32[]{:S(2)}) collective-permute-start(bf16[4,256,256]{2,1,0:T(8,128)(2,1)S(1)} %collective-permute-done.11.refs_4_), channel_id=1, source_target_pairs={{0,4},{1,5},{2,6},{3,7},{4,8},{5,9},{6,10},{7,11},{8,12},{9,13},{1... | collective-permute-start | bytes 1572872 | tf_op jit(solution)/shard_map/ppermute | solution.py:41
  21.0 1.0 slice_bitcast_fusion.3
  22.0 3.6 %collective-permute-done.8.refs_2_ = bf16[4,256,256]{2,1,0:T(8,128)(2,1)S(1)} collective-permute-done((bf16[4,256,256]{2,1,0:T(8,128)(2,1)S(1)}, bf16[4,256,256]{2,1,0:T(8,128)(2,1)S(1)}, u32[]{:S(2)}, u32[]{:S(2)}) %collective-permute-start.8) | collective-permute-done | bytes 524320 | tf_op jit(solution)/shard_map/ppermute | solution.py:41
  25.7 0.8 copy-done.8
  26.5 1.0 pad_maximum_fusion
  27.5 4.1 %collective-permute-start.10 = (bf16[3,4,256,128]{3,2,1,0:T(8,128)(2,1)}, bf16[3,4,256,128]{3,2,1,0:T(8,128)(2,1)S(1)}, u32[]{:S(2)}, u32[]{:S(2)}) collective-permute-start(bf16[3,4,256,128]{3,2,1,0:T(8,128)(2,1)} %pad_maximum_fusion), channel_id=1, source_target_pairs={{0,4},{1,5},{2,6},{3,7},{4,8},{5,9},{6,10},{7,11},{8,12},{9,13},{1... | collective-permute-start | bytes 2359304 | tf_op jit(solution)/shard_map/ppermute | solution.py:41
  31.6 1.6 %collective-permute-start.2 = (bf16[4,256,256]{2,1,0:T(8,128)(2,1)}, bf16[4,256,256]{2,1,0:T(8,128)(2,1)}, u32[]{:S(2)}, u32[]{:S(2)}) collective-permute-start(bf16[4,256,256]{2,1,0:T(8,128)(2,1)} %collective-permute-done.1.refs_1_), channel_id=1, source_target_pairs={{0,32},{1,33},{2,34},{3,35},{4,36},{5,37},{6,38},{7,39},{8,40},{9,... | collective-permute-start | bytes 1572872 | tf_op jit(solution)/shard_map/ppermute | solution.py:41
  33.2 1.1 pad_maximum_fusion.1
  34.3 0.2 collective-permute-start.14
  34.5 1.0 collective-permute-start.15
  35.5 3.1 %collective-permute-start.17 = (bf16[3,4,256,128]{3,2,1,0:T(8,128)(2,1)}, bf16[3,4,256,128]{3,2,1,0:T(8,128)(2,1)}, u32[]{:S(2)}, u32[]{:S(2)}) collective-permute-start(bf16[3,4,256,128]{3,2,1,0:T(8,128)(2,1)} %pad_maximum_fusion.1), channel_id=1, source_target_pairs={{0,3},{1,0},{2,1},{3,2},{4,7},{5,4},{6,5},{7,6},{8,11},{9,8},{10,9... | collective-permute-start | bytes 2359304 | tf_op jit(solution)/shard_map/ppermute | solution.py:41
  38.5 3.7 %collective-permute-done.2.refs_2_ = bf16[4,256,256]{2,1,0:T(8,128)(2,1)} collective-permute-done((bf16[4,256,256]{2,1,0:T(8,128)(2,1)}, bf16[4,256,256]{2,1,0:T(8,128)(2,1)}, u32[]{:S(2)}, u32[]{:S(2)}) %collective-permute-start.2) | collective-permute-done | bytes 524320 | tf_op jit(solution)/shard_map/ppermute | solution.py:41
  42.3 4.1 %collective-permute-done.10.refs_0_.refs_8_ = bf16[3,4,256,128]{3,2,1,0:T(8,128)(2,1)S(1)} collective-permute-done((bf16[3,4,256,128]{3,2,1,0:T(8,128)(2,1)}, bf16[3,4,256,128]{3,2,1,0:T(8,128)(2,1)S(1)}, u32[]{:S(2)}, u32[]{:S(2)}) %collective-permute-start.10) | collective-permute-done | bytes 786464 | tf_op jit(solution)/shard_map/ppermute | solution.py:41
  46.4 1.8 %collective-permute-start.3 = (bf16[4,256,256]{2,1,0:T(8,128)(2,1)}, bf16[4,256,256]{2,1,0:T(8,128)(2,1)}, u32[]{:S(2)}, u32[]{:S(2)}) collective-permute-start(bf16[4,256,256]{2,1,0:T(8,128)(2,1)} %collective-permute-done.2.refs_2_), channel_id=1, source_target_pairs={{0,32},{1,33},{2,34},{3,35},{4,36},{5,37},{6,38},{7,39},{8,40},{9,... | collective-permute-start | bytes 1572872 | tf_op jit(solution)/shard_map/ppermute | solution.py:41
  48.3 5.7 %left_parts.2.refs_14_ = bf16[7,4,256,256]{3,2,1,0:T(8,128)(2,1)} custom-call(s32[4,2]{1,0:T(4,128)S(1)} %copy.12.src_ref, bf16[4,2,256,256]{3,2,1,0:T(8,128)(2,1)S(1)} %bitcast.28, bf16[4,256,256]{2,1,0:T(8,128)(2,1)} %bitcast.36, bf16[4,256,256]{2,1,0:T(8,128)(2,1)} %copy-done.5, bf16[4,256,256]{2,1,0:T(8,128)(2,1)} %copy-done.8, ...), custom_call_target="tpu_custom_call" | custom-call | flops 1879048192 | bytes 5242880 | tf_op jit(solution)/shard_map/left_parts/pallas_call | solution.py:122
  54.0 1.8 %collective-permute-done.14.refs_2_.refs_11_ = bf16[3,4,256,128]{3,2,1,0:T(8,128)(2,1)S(1)} collective-permute-done((bf16[3,4,256,128]{3,2,1,0:T(8,128)(2,1)}, bf16[3,4,256,128]{3,2,1,0:T(8,128)(2,1)S(1)}, u32[]{:S(2)}, u32[]{:S(2)}) %collective-permute-start.14) | collective-permute-done | bytes 786464 | tf_op jit(solution)/shard_map/ppermute | solution.py:41
  55.8 2.4 %collective-permute-start.16 = (bf16[3,4,256,128]{3,2,1,0:T(8,128)(2,1)S(1)}, bf16[3,4,256,128]{3,2,1,0:T(8,128)(2,1)}, u32[]{:S(2)}, u32[]{:S(2)}) collective-permute-start(bf16[3,4,256,128]{3,2,1,0:T(8,128)(2,1)S(1)} %collective-permute-done.10.refs_0_.refs_8_), channel_id=1, source_target_pairs={{0,4},{1,5},{2,6},{3,7},{4,8},{5,9},{6,10},{7,11},{8,12},{9,13},{1... | collective-permute-start | bytes 2359304 | tf_op jit(solution)/shard_map/ppermute | solution.py:41
  58.2 0.6 collective-permute-start.18
  58.8 0.5 collective-permute-start.6
  59.4 0.6 broadcast_in_dim.39
  60.0 7.8 %all-to-all-start = ((s32[16,1,4]{2,1,0:T(1,128)}), s32[16,1,4]{2,1,0:T(1,128)S(1)}, u32[]{:S(2)}, u32[]{:S(2)}) async-start(s32[16,1,4]{2,1,0:T(1,128)} %broadcast_in_dim.39), calls=%async_computation | async-start | bytes 16384 | tf_op jit(solution)/shard_map/all_to_all | solution.py:309
  67.9 4.6 %left_parts.3.refs_15_ = bf16[4,4,256,256]{3,2,1,0:T(8,128)(2,1)} custom-call(s32[4,2]{1,0:T(4,128)S(1)} %copy.12.src_ref, bf16[4,2,256,256]{3,2,1,0:T(8,128)(2,1)S(1)} %bitcast.29, bf16[3,4,256,128]{3,2,1,0:T(8,128)(2,1)} %copy-done.2, bf16[3,4,256,128]{3,2,1,0:T(8,128)(2,1)} %copy-done.4, bf16[3,4,256,128]{3,2,1,0:T(8,128)(2,1)} %copy-done.3, ...), custom_call_target="tpu_custom_call" | custom-call | flops 1073741824 | bytes 5242880 | tf_op jit(solution)/shard_map/left_parts/pallas_call | solution.py:122
  72.5 2.9 %all-to-all-done.loc_ref = s32[16,1,4]{2,1,0:T(1,128)S(1)} async-done(((s32[16,1,4]{2,1,0:T(1,128)}), s32[16,1,4]{2,1,0:T(1,128)S(1)}, u32[]{:S(2)}, u32[]{:S(2)}) %all-to-all-start) | async-done | bytes 288 | tf_op jit(solution)/shard_map/all_to_all | solution.py:309
  75.4 7.0 %apply_terms.2 = (bf16[4,256,256]{2,1,0:T(8,128)(2,1)S(1)}, bf16[4,256,256]{2,1,0:T(8,128)(2,1)S(1)}, bf16[4,256,256]{2,1,0:T(8,128)(2,1)S(1)}, bf16[4,256,256]{...) custom-call(s32[4,2]{1,0:T(4,128)S(1)} %copy.12.src_ref, ...), custom_call_target="tpu_custom_call" | custom-call | flops 2684354560 | bytes 8388608 | tf_op jit(solution)/shard_map/apply_terms/pallas_call | solution.py:254
  82.4 0.5 collective-permute-start.20
  82.9 0.6 collective-permute-start.30
  83.5 1.3 collective-permute-start.22
  84.8 1.5 %collective-permute-start.19 = (bf16[4,256,256]{2,1,0:T(8,128)(2,1)S(1)}, bf16[4,256,256]{2,1,0:T(8,128)(2,1)S(1)}, u32[]{:S(2)}, u32[]{:S(2)}) collective-permute-start(bf16[4,256,256]{2,1,0:T(8,128)(2,1)S(1)} %get-tuple-element.33), channel_id=1, source_target_pairs={{0,12},{1,13},{2,14},{3,15},{4,0},{5,1},{6,2},{7,3},{8,4},{9,5},{1... | collective-permute-start | bytes 1572872 | tf_op jit(solution)/shard_map/ppermute | solution.py:41
  86.3 2.7 %collective-permute-start.29 = (bf16[4,256,256]{2,1,0:T(8,128)(2,1)S(1)}, bf16[4,256,256]{2,1,0:T(8,128)(2,1)S(1)}, u32[]{:S(2)}, u32[]{:S(2)}) collective-permute-start(bf16[4,256,256]{2,1,0:T(8,128)(2,1)S(1)} %get-tuple-element.42), channel_id=1, source_target_pairs={{0,3},{1,0},{2,1},{3,2},{4,7},{5,4},{6,5},{7,6},{8,11},{9,8},{10,9... | collective-permute-start | bytes 1572872 | tf_op jit(solution)/shard_map/ppermute | solution.py:41
  89.0 7.1 %apply_terms.3 = (bf16[4,256,256]{2,1,0:T(8,128)(2,1)S(1)}, bf16[4,256,256]{2,1,0:T(8,128)(2,1)S(1)}, bf16[4,256,256]{2,1,0:T(8,128)(2,1)S(1)}, bf16[4,256,256]{...) custom-call(s32[4,2]{1,0:T(4,128)S(1)} %copy.12.src_ref, ...), custom_call_target="tpu_custom_call" | custom-call | flops 2684354560 | bytes 8388608 | tf_op jit(solution)/shard_map/apply_terms/pallas_call | solution.py:254
  96.2 0.9 collective-permute-done.20
  97.1 1.0 collective-permute-start.33
  98.1 0.1 add_convert_fusion.3
  98.3 0.3 collective-permute-start.21
  98.6 0.1 add_convert_fusion.1
  98.8 7.8 %collective-permute-done.24 = bf16[4,256,256]{2,1,0:T(8,128)(2,1)S(1)} collective-permute-done((bf16[4,256,256]{2,1,0:T(8,128)(2,1)S(1)}, bf16[4,256,256]{2,1,0:T(8,128)(2,1)S(1)}, u32[]{:S(2)}, u32[]{:S(2)}) %collective-permute-start.24) | collective-permute-done | bytes 524320 | tf_op jit(solution)/shard_map/ppermute | solution.py:41
  106.8 0.7 collective-permute-done.33
  107.5 1.3 collective-permute-start.25
  109.0 7.4 %collective-permute-done.21 = bf16[4,256,256]{2,1,0:T(8,128)(2,1)S(1)} collective-permute-done((bf16[4,256,256]{2,1,0:T(8,128)(2,1)S(1)}, bf16[4,256,256]{2,1,0:T(8,128)(2,1)S(1)}, u32[]{:S(2)}, u32[]{:S(2)}) %collective-permute-start.21) | collective-permute-done | bytes 524320 | tf_op jit(solution)/shard_map/ppermute | solution.py:41
  116.4 0.2 add_convert_fusion.23
  116.6 2.1 %collective-permute-start.34 = (bf16[4,256,256]{2,1,0:T(8,128)(2,1)S(1)}, bf16[4,256,256]{2,1,0:T(8,128)(2,1)S(1)}, u32[]{:S(2)}, u32[]{:S(2)}) collective-permute-start(bf16[4,256,256]{2,1,0:T(8,128)(2,1)S(1)} %add_convert_fusion), channel_id=1, source_target_pairs={{0,1},{1,2},{2,3},{3,0},{4,5},{5,6},{6,7},{7,4},{8,9},{9,10},{10,1... | collective-permute-start | bytes 1572872 | tf_op jit(solution)/shard_map/ppermute | solution.py:41
  118.7 3.5 %collective-permute-done.31 = bf16[4,256,256]{2,1,0:T(8,128)(2,1)S(1)} collective-permute-done((bf16[4,256,256]{2,1,0:T(8,128)(2,1)S(1)}, bf16[4,256,256]{2,1,0:T(8,128)(2,1)S(1)}, u32[]{:S(2)}, u32[]{:S(2)}) %collective-permute-start.31) | collective-permute-done | bytes 524320 | tf_op jit(solution)/shard_map/ppermute | solution.py:41
  122.2 0.2 add_convert_fusion.15
  122.4 1.0 collective-permute-done.25
  123.4 0.2 add_convert_fusion.22
  123.8 2.1 %collective-permute-start.27 = (bf16[2,256,256]{2,1,0:T(8,128)(2,1)S(1)}, bf16[2,256,256]{2,1,0:T(8,128)(2,1)S(1)}, u32[]{:S(2)}, u32[]{:S(2)}) collective-permute-start(bf16[2,256,256]{2,1,0:T(8,128)(2,1)S(1)} %pad_maximum_fusion.3), channel_id=1, source_target_pairs={{0,1},{1,2},{2,3},{3,0},{4,5},{5,6},{6,7},{7,4},{8,9},{9,10},{10,1... | collective-permute-start | bytes 786440 | tf_op jit(solution)/shard_map/ppermute | solution.py:41
  125.9 2.4 %collective-permute-done.32 = bf16[4,256,256]{2,1,0:T(8,128)(2,1)S(1)} collective-permute-done((bf16[4,256,256]{2,1,0:T(8,128)(2,1)S(1)}, bf16[4,256,256]{2,1,0:T(8,128)(2,1)S(1)}, u32[]{:S(2)}, u32[]{:S(2)}) %collective-permute-start.32) | collective-permute-done | bytes 524320 | tf_op jit(solution)/shard_map/ppermute | solution.py:41
  128.3 2.3 %collective-permute-done.34 = bf16[4,256,256]{2,1,0:T(8,128)(2,1)S(1)} collective-permute-done((bf16[4,256,256]{2,1,0:T(8,128)(2,1)S(1)}, bf16[4,256,256]{2,1,0:T(8,128)(2,1)S(1)}, u32[]{:S(2)}, u32[]{:S(2)}) %collective-permute-start.34) | collective-permute-done | bytes 524320 | tf_op jit(solution)/shard_map/ppermute | solution.py:41
  130.7 0.2 add_convert_fusion.14
  131.0 3.3 %collective-permute-start.35 = (bf16[2,256,256]{2,1,0:T(8,128)(2,1)S(1)}, bf16[2,256,256]{2,1,0:T(8,128)(2,1)S(1)}, u32[]{:S(2)}, u32[]{:S(2)}) collective-permute-start(bf16[2,256,256]{2,1,0:T(8,128)(2,1)S(1)} %pad_maximum_fusion.4), channel_id=1, source_target_pairs={{0,12},{1,13},{2,14},{3,15},{4,0},{5,1},{6,2},{7,3},{8,4},{9,5},{1... | collective-permute-start | bytes 786440 | tf_op jit(solution)/shard_map/ppermute | solution.py:41
  134.5 4.1 %collective-permute-done.36 = bf16[2,256,256]{2,1,0:T(8,128)(2,1)S(1)} collective-permute-done((bf16[2,256,256]{2,1,0:T(8,128)(2,1)S(1)}, bf16[2,256,256]{2,1,0:T(8,128)(2,1)S(1)}, u32[]{:S(2)}, u32[]{:S(2)}) %collective-permute-start.36) | collective-permute-done | bytes 262176 | tf_op jit(solution)/shard_map/ppermute | solution.py:41
  138.8 3.2 %collective-permute-done.28 = bf16[2,256,256]{2,1,0:T(8,128)(2,1)S(1)} collective-permute-done((bf16[2,256,256]{2,1,0:T(8,128)(2,1)S(1)}, bf16[2,256,256]{2,1,0:T(8,128)(2,1)S(1)}, u32[]{:S(2)}, u32[]{:S(2)}) %collective-permute-start.28) | collective-permute-done | bytes 262176 | tf_op jit(solution)/shard_map/ppermute | solution.py:41
  142.2 4.1 %collective-permute-done.37 = bf16[2,256,256]{2,1,0:T(8,128)(2,1)S(1)} collective-permute-done((bf16[2,256,256]{2,1,0:T(8,128)(2,1)S(1)}, bf16[2,256,256]{2,1,0:T(8,128)(2,1)S(1)}, u32[]{:S(2)}, u32[]{:S(2)}) %collective-permute-start.37) | collective-permute-done | bytes 262176 | tf_op jit(solution)/shard_map/ppermute | solution.py:41
  146.4 1.0 fusion
  (76 shorter events, 1.8 us)
Async XLA Ops:
  0.0 11.0 %collective-permute-start = (bf16[4,256,256]{2,1,0:T(8,128)(2,1)}, bf16[4,256,256]{2,1,0:T(8,128)(2,1)S(1)}, u32[]{:S(2)}, u32[]{:S(2)}) collective-permute-start(bf16[4,256,256]{2,1,0:T(8,128)(2,1)} %bitcast.32), channel_id=1, source_target_pairs={{0,1},{1,2},{2,3},{3,0},{4,5},{5,6},{6,7},{7,4},{8,9},{9,10},{10,1... | collective-permute-start | bytes 1572872 | tf_op jit(solution)/shard_map/ppermute | solution.py:41
  1.6 15.1 %collective-permute-start.11 = (bf16[4,256,256]{2,1,0:T(8,128)(2,1)}, bf16[4,256,256]{2,1,0:T(8,128)(2,1)S(1)}, u32[]{:S(2)}, u32[]{:S(2)}) collective-permute-start(bf16[4,256,256]{2,1,0:T(8,128)(2,1)} %bitcast.33), channel_id=1, source_target_pairs={{0,4},{1,5},{2,6},{3,7},{4,8},{5,9},{6,10},{7,11},{8,12},{9,13},{1... | collective-permute-start | bytes 1572872 | tf_op jit(solution)/shard_map/ppermute | solution.py:41
  3.5 18.4 %collective-permute-start.13 = (bf16[4,256,256]{2,1,0:T(8,128)(2,1)}, bf16[4,256,256]{2,1,0:T(8,128)(2,1)S(1)}, u32[]{:S(2)}, u32[]{:S(2)}) collective-permute-start(bf16[4,256,256]{2,1,0:T(8,128)(2,1)} %bitcast.34), channel_id=1, source_target_pairs={{0,12},{1,13},{2,14},{3,15},{4,0},{5,1},{6,2},{7,3},{8,4},{9,5},{1... | collective-permute-start | bytes 1572872 | tf_op jit(solution)/shard_map/ppermute | solution.py:41
  5.6 15.3 %collective-permute-start.9 = (bf16[4,256,256]{2,1,0:T(8,128)(2,1)}, bf16[4,256,256]{2,1,0:T(8,128)(2,1)}, u32[]{:S(2)}, u32[]{:S(2)}) collective-permute-start(bf16[4,256,256]{2,1,0:T(8,128)(2,1)} %bitcast.35), channel_id=1, source_target_pairs={{0,3},{1,0},{2,1},{3,2},{4,7},{5,4},{6,5},{7,6},{8,11},{9,8},{10,9... | collective-permute-start | bytes 1572872 | tf_op jit(solution)/shard_map/ppermute | solution.py:41
  11.0 14.7 %copy-start.5 = (bf16[4,256,256]{2,1,0:T(8,128)(2,1)}, bf16[4,256,256]{2,1,0:T(8,128)(2,1)S(1)}, u32[]{:S(2)}) copy-start(bf16[4,256,256]{2,1,0:T(8,128)(2,1)S(1)} %collective-permute-done.refs_1_) | copy-start | bytes 1572868
  12.4 35.8 %copy-start.10 = (s32[1,4,2]{1,2,0:T(2,128)S(1)}, s32[1,4,2]{1,2,0:T(2,128)}, u32[]{:S(2)}) copy-start(s32[1,4,2]{1,2,0:T(2,128)} %param.10) | copy-start | bytes 100
  12.4 35.8 %copy-start = (bf16[1,4,2,256,256]{4,3,2,1,0:T(8,128)(2,1)S(1)}, bf16[1,4,2,256,256]{4,3,2,1,0:T(8,128)(2,1)}, u32[]{:S(2)}) copy-start(bf16[1,4,2,256,256]{4,3,2,1,0:T(8,128)(2,1)} %param.9) | copy-start | bytes 3145732
  13.3 18.3 %collective-permute-start.1 = (bf16[4,256,256]{2,1,0:T(8,128)(2,1)}, bf16[4,256,256]{2,1,0:T(8,128)(2,1)}, u32[]{:S(2)}, u32[]{:S(2)}) collective-permute-start(bf16[4,256,256]{2,1,0:T(8,128)(2,1)} %fusion.1.refs_0_), channel_id=1, source_target_pairs={{0,32},{1,33},{2,34},{3,35},{4,36},{5,37},{6,38},{7,39},{8,40},{9,... | collective-permute-start | bytes 1572872 | tf_op jit(solution)/shard_map/ppermute | solution.py:41
  15.0 10.6 %collective-permute-start.8 = (bf16[4,256,256]{2,1,0:T(8,128)(2,1)S(1)}, bf16[4,256,256]{2,1,0:T(8,128)(2,1)S(1)}, u32[]{:S(2)}, u32[]{:S(2)}) collective-permute-start(bf16[4,256,256]{2,1,0:T(8,128)(2,1)S(1)} %collective-permute-done.refs_1_), channel_id=1, source_target_pairs={{0,1},{1,2},{2,3},{3,0},{4,5},{5,6},{6,7},{7,4},{8,9},{9,10},{10,1... | collective-permute-start | bytes 1572872 | tf_op jit(solution)/shard_map/ppermute | solution.py:41
  16.7 16.5 %copy-start.6 = (bf16[4,256,256]{2,1,0:T(8,128)(2,1)}, bf16[4,256,256]{2,1,0:T(8,128)(2,1)S(1)}, u32[]{:S(2)}) copy-start(bf16[4,256,256]{2,1,0:T(8,128)(2,1)S(1)} %collective-permute-done.11.refs_4_) | copy-start | bytes 1572868
  16.7 16.5 %collective-permute-start.12 = (bf16[4,256,256]{2,1,0:T(8,128)(2,1)S(1)}, bf16[4,256,256]{2,1,0:T(8,128)(2,1)S(1)}, u32[]{:S(2)}, u32[]{:S(2)}) collective-permute-start(bf16[4,256,256]{2,1,0:T(8,128)(2,1)S(1)} %collective-permute-done.11.refs_4_), channel_id=1, source_target_pairs={{0,4},{1,5},{2,6},{3,7},{4,8},{5,9},{6,10},{7,11},{8,12},{9,13},{1... | collective-permute-start | bytes 1572872 | tf_op jit(solution)/shard_map/ppermute | solution.py:41
  21.9 11.3 %copy-start.7 = (bf16[4,256,256]{2,1,0:T(8,128)(2,1)}, bf16[4,256,256]{2,1,0:T(8,128)(2,1)S(1)}, u32[]{:S(2)}) copy-start(bf16[4,256,256]{2,1,0:T(8,128)(2,1)S(1)} %collective-permute-done.13.refs_6_) | copy-start | bytes 1572868
  25.6 0.9 copy-start.8
  27.5 18.9 %collective-permute-start.10 = (bf16[3,4,256,128]{3,2,1,0:T(8,128)(2,1)}, bf16[3,4,256,128]{3,2,1,0:T(8,128)(2,1)S(1)}, u32[]{:S(2)}, u32[]{:S(2)}) collective-permute-start(bf16[3,4,256,128]{3,2,1,0:T(8,128)(2,1)} %pad_maximum_fusion), channel_id=1, source_target_pairs={{0,4},{1,5},{2,6},{3,7},{4,8},{5,9},{6,10},{7,11},{8,12},{9,13},{1... | collective-permute-start | bytes 2359304 | tf_op jit(solution)/shard_map/ppermute | solution.py:41
  31.6 10.7 %collective-permute-start.2 = (bf16[4,256,256]{2,1,0:T(8,128)(2,1)}, bf16[4,256,256]{2,1,0:T(8,128)(2,1)}, u32[]{:S(2)}, u32[]{:S(2)}) collective-permute-start(bf16[4,256,256]{2,1,0:T(8,128)(2,1)} %collective-permute-done.1.refs_1_), channel_id=1, source_target_pairs={{0,32},{1,33},{2,34},{3,35},{4,36},{5,37},{6,38},{7,39},{8,40},{9,... | collective-permute-start | bytes 1572872 | tf_op jit(solution)/shard_map/ppermute | solution.py:41
  33.1 15.0 %copy-start.9 = (bf16[4,256,256]{2,1,0:T(8,128)(2,1)}, bf16[4,256,256]{2,1,0:T(8,128)(2,1)S(1)}, u32[]{:S(2)}) copy-start(bf16[4,256,256]{2,1,0:T(8,128)(2,1)S(1)} %collective-permute-done.12.refs_5_) | copy-start | bytes 1572868
  34.3 21.5 %collective-permute-start.14 = (bf16[3,4,256,128]{3,2,1,0:T(8,128)(2,1)}, bf16[3,4,256,128]{3,2,1,0:T(8,128)(2,1)S(1)}, u32[]{:S(2)}, u32[]{:S(2)}) collective-permute-start(bf16[3,4,256,128]{3,2,1,0:T(8,128)(2,1)} %pad_maximum_fusion.1), channel_id=1, source_target_pairs={{0,1},{1,2},{2,3},{3,0},{4,5},{5,6},{6,7},{7,4},{8,9},{9,10},{10,1... | collective-permute-start | bytes 2359304 | tf_op jit(solution)/shard_map/ppermute | solution.py:41
  34.5 24.3 %collective-permute-start.15 = (bf16[3,4,256,128]{3,2,1,0:T(8,128)(2,1)}, bf16[3,4,256,128]{3,2,1,0:T(8,128)(2,1)S(1)}, u32[]{:S(2)}, u32[]{:S(2)}) collective-permute-start(bf16[3,4,256,128]{3,2,1,0:T(8,128)(2,1)} %pad_maximum_fusion), channel_id=1, source_target_pairs={{0,12},{1,13},{2,14},{3,15},{4,0},{5,1},{6,2},{7,3},{8,4},{9,5},{1... | collective-permute-start | bytes 2359304 | tf_op jit(solution)/shard_map/ppermute | solution.py:41
  35.5 23.4 %collective-permute-start.17 = (bf16[3,4,256,128]{3,2,1,0:T(8,128)(2,1)}, bf16[3,4,256,128]{3,2,1,0:T(8,128)(2,1)}, u32[]{:S(2)}, u32[]{:S(2)}) collective-permute-start(bf16[3,4,256,128]{3,2,1,0:T(8,128)(2,1)} %pad_maximum_fusion.1), channel_id=1, source_target_pairs={{0,3},{1,0},{2,1},{3,2},{4,7},{5,4},{6,5},{7,6},{8,11},{9,8},{10,9... | collective-permute-start | bytes 2359304 | tf_op jit(solution)/shard_map/ppermute | solution.py:41
  42.3 16.0 %collective-permute-start.4 = (bf16[4,256,256]{2,1,0:T(8,128)(2,1)}, bf16[4,256,256]{2,1,0:T(8,128)(2,1)}, u32[]{:S(2)}, u32[]{:S(2)}) collective-permute-start(bf16[4,256,256]{2,1,0:T(8,128)(2,1)} %fusion.1.refs_0_), channel_id=1, source_target_pairs={{0,16},{16,0},{32,48},{48,32},{64,80},{80,64},{96,112},{112,96},{1... | collective-permute-start | bytes 1572872 | tf_op jit(solution)/shard_map/ppermute | solution.py:57
  46.4 9.4 %copy-start.2 = (bf16[3,4,256,128]{3,2,1,0:T(8,128)(2,1)}, bf16[3,4,256,128]{3,2,1,0:T(8,128)(2,1)S(1)}, u32[]{:S(2)}) copy-start(bf16[3,4,256,128]{3,2,1,0:T(8,128)(2,1)S(1)} %collective-permute-done.10.refs_0_.refs_8_) | copy-start | bytes 2359300
  46.4 12.9 %collective-permute-start.3 = (bf16[4,256,256]{2,1,0:T(8,128)(2,1)}, bf16[4,256,256]{2,1,0:T(8,128)(2,1)}, u32[]{:S(2)}, u32[]{:S(2)}) collective-permute-start(bf16[4,256,256]{2,1,0:T(8,128)(2,1)} %collective-permute-done.2.refs_2_), channel_id=1, source_target_pairs={{0,32},{1,33},{2,34},{3,35},{4,36},{5,37},{6,38},{7,39},{8,40},{9,... | collective-permute-start | bytes 1572872 | tf_op jit(solution)/shard_map/ppermute | solution.py:41
  48.3 11.2 %copy-start.11 = (s32[4,1]{0,1:T(1,128)S(1)}, s32[4,1]{0,1:T(1,128)}, u32[]{:S(2)}) copy-start(s32[4,1]{0,1:T(1,128)} %param.13) | copy-start | bytes 52
  54.0 21.5 %copy-start.1 = (bf16[1,16,16]{2,1,0:T(8,128)(2,1)S(1)}, bf16[1,16,16]{2,1,0:T(8,128)(2,1)}, u32[]{:S(2)}) copy-start(bf16[1,16,16]{2,1,0:T(8,128)(2,1)} %two_site_ref.3) | copy-start | bytes 1540
  55.8 12.0 %copy-start.3 = (bf16[3,4,256,128]{3,2,1,0:T(8,128)(2,1)}, bf16[3,4,256,128]{3,2,1,0:T(8,128)(2,1)S(1)}, u32[]{:S(2)}) copy-start(bf16[3,4,256,128]{3,2,1,0:T(8,128)(2,1)S(1)} %collective-permute-done.14.refs_2_.refs_11_) | copy-start | bytes 2359300
  55.8 19.6 %collective-permute-start.16 = (bf16[3,4,256,128]{3,2,1,0:T(8,128)(2,1)S(1)}, bf16[3,4,256,128]{3,2,1,0:T(8,128)(2,1)}, u32[]{:S(2)}, u32[]{:S(2)}) collective-permute-start(bf16[3,4,256,128]{3,2,1,0:T(8,128)(2,1)S(1)} %collective-permute-done.10.refs_0_.refs_8_), channel_id=1, source_target_pairs={{0,4},{1,5},{2,6},{3,7},{4,8},{5,9},{6,10},{7,11},{8,12},{9,13},{1... | collective-permute-start | bytes 2359304 | tf_op jit(solution)/shard_map/ppermute | solution.py:41
  58.2 17.1 %collective-permute-start.18 = (bf16[3,4,256,128]{3,2,1,0:T(8,128)(2,1)S(1)}, bf16[3,4,256,128]{3,2,1,0:T(8,128)(2,1)}, u32[]{:S(2)}, u32[]{:S(2)}) collective-permute-start(bf16[3,4,256,128]{3,2,1,0:T(8,128)(2,1)S(1)} %collective-permute-done.14.refs_2_.refs_11_), channel_id=1, source_target_pairs={{0,1},{1,2},{2,3},{3,0},{4,5},{5,6},{6,7},{7,4},{8,9},{9,10},{10,1... | collective-permute-start | bytes 2359304 | tf_op jit(solution)/shard_map/ppermute | solution.py:41
  58.8 9.0 %copy-start.4 = (bf16[3,4,256,128]{3,2,1,0:T(8,128)(2,1)}, bf16[3,4,256,128]{3,2,1,0:T(8,128)(2,1)S(1)}, u32[]{:S(2)}) copy-start(bf16[3,4,256,128]{3,2,1,0:T(8,128)(2,1)S(1)} %collective-permute-done.15.refs_1_.refs_9_) | copy-start | bytes 2359300
  58.8 16.6 %collective-permute-start.5 = (bf16[4,256,256]{2,1,0:T(8,128)(2,1)}, bf16[4,256,256]{2,1,0:T(8,128)(2,1)}, u32[]{:S(2)}, u32[]{:S(2)}) collective-permute-start(bf16[4,256,256]{2,1,0:T(8,128)(2,1)} %collective-permute-done.1.refs_1_), channel_id=1, source_target_pairs={{0,16},{16,0},{32,48},{48,32},{64,80},{80,64},{96,112},{112,96},{1... | collective-permute-start | bytes 1572872 | tf_op jit(solution)/shard_map/ppermute | solution.py:57
  58.8 16.6 %collective-permute-start.6 = (bf16[4,256,256]{2,1,0:T(8,128)(2,1)}, bf16[4,256,256]{2,1,0:T(8,128)(2,1)}, u32[]{:S(2)}, u32[]{:S(2)}) collective-permute-start(bf16[4,256,256]{2,1,0:T(8,128)(2,1)} %collective-permute-done.2.refs_2_), channel_id=1, source_target_pairs={{0,16},{16,0},{32,48},{48,32},{64,80},{80,64},{96,112},{112,96},{1... | collective-permute-start | bytes 1572872 | tf_op jit(solution)/shard_map/ppermute | solution.py:57
  59.3 16.1 %collective-permute-start.7 = (bf16[4,256,256]{2,1,0:T(8,128)(2,1)}, bf16[4,256,256]{2,1,0:T(8,128)(2,1)}, u32[]{:S(2)}, u32[]{:S(2)}) collective-permute-start(bf16[4,256,256]{2,1,0:T(8,128)(2,1)} %collective-permute-done.3.refs_3_), channel_id=1, source_target_pairs={{0,16},{16,0},{32,48},{48,32},{64,80},{80,64},{96,112},{112,96},{1... | collective-permute-start | bytes 1572872 | tf_op jit(solution)/shard_map/ppermute | solution.py:57
  60.0 15.3 %all-to-all-start = ((s32[16,1,4]{2,1,0:T(1,128)}), s32[16,1,4]{2,1,0:T(1,128)S(1)}, u32[]{:S(2)}, u32[]{:S(2)}) async-start(s32[16,1,4]{2,1,0:T(1,128)} %broadcast_in_dim.39), calls=%async_computation | async-start | bytes 16384 | tf_op jit(solution)/shard_map/all_to_all | solution.py:309
  82.4 14.7 %collective-permute-start.20 = (bf16[4,256,256]{2,1,0:T(8,128)(2,1)S(1)}, bf16[4,256,256]{2,1,0:T(8,128)(2,1)S(1)}, u32[]{:S(2)}, u32[]{:S(2)}) collective-permute-start(bf16[4,256,256]{2,1,0:T(8,128)(2,1)S(1)} %get-tuple-element.35), channel_id=1, source_target_pairs={{0,4},{1,5},{2,6},{3,7},{4,8},{5,9},{6,10},{7,11},{8,12},{9,13},{1... | collective-permute-start | bytes 1572872 | tf_op jit(solution)/shard_map/ppermute | solution.py:41
  82.9 15.4 %collective-permute-start.30 = (bf16[4,256,256]{2,1,0:T(8,128)(2,1)S(1)}, bf16[4,256,256]{2,1,0:T(8,128)(2,1)S(1)}, u32[]{:S(2)}, u32[]{:S(2)}) collective-permute-start(bf16[4,256,256]{2,1,0:T(8,128)(2,1)S(1)} %get-tuple-element.44), channel_id=1, source_target_pairs={{0,1},{1,2},{2,3},{3,0},{4,5},{5,6},{6,7},{7,4},{8,9},{9,10},{10,1... | collective-permute-start | bytes 1572872 | tf_op jit(solution)/shard_map/ppermute | solution.py:41
  83.5 5.5 %collective-permute-start.22 = (bf16[16,128]{1,0:T(8,128)(2,1)S(1)}, bf16[16,128]{1,0:T(8,128)(2,1)S(1)}, u32[]{:S(2)}, u32[]{:S(2)}) collective-permute-start(bf16[16,128]{1,0:T(8,128)(2,1)S(1)} %get-tuple-element.36), channel_id=1, source_target_pairs={{0,16},{16,0},{32,48},{48,32},{64,80},{80,64},{96,112},{112,96},{1... | collective-permute-start | bytes 12296 | tf_op jit(solution)/shard_map/ppermute | solution.py:57
  84.8 21.9 %collective-permute-start.19 = (bf16[4,256,256]{2,1,0:T(8,128)(2,1)S(1)}, bf16[4,256,256]{2,1,0:T(8,128)(2,1)S(1)}, u32[]{:S(2)}, u32[]{:S(2)}) collective-permute-start(bf16[4,256,256]{2,1,0:T(8,128)(2,1)S(1)} %get-tuple-element.33), channel_id=1, source_target_pairs={{0,12},{1,13},{2,14},{3,15},{4,0},{5,1},{6,2},{7,3},{8,4},{9,5},{1... | collective-permute-start | bytes 1572872 | tf_op jit(solution)/shard_map/ppermute | solution.py:41
  86.3 30.3 %collective-permute-start.29 = (bf16[4,256,256]{2,1,0:T(8,128)(2,1)S(1)}, bf16[4,256,256]{2,1,0:T(8,128)(2,1)S(1)}, u32[]{:S(2)}, u32[]{:S(2)}) collective-permute-start(bf16[4,256,256]{2,1,0:T(8,128)(2,1)S(1)} %get-tuple-element.42), channel_id=1, source_target_pairs={{0,3},{1,0},{2,1},{3,2},{4,7},{5,4},{6,5},{7,6},{8,11},{9,8},{10,9... | collective-permute-start | bytes 1572872 | tf_op jit(solution)/shard_map/ppermute | solution.py:41
  96.1 10.5 %collective-permute-start.24 = (bf16[4,256,256]{2,1,0:T(8,128)(2,1)S(1)}, bf16[4,256,256]{2,1,0:T(8,128)(2,1)S(1)}, u32[]{:S(2)}, u32[]{:S(2)}) collective-permute-start(bf16[4,256,256]{2,1,0:T(8,128)(2,1)S(1)} %get-tuple-element.40), channel_id=1, source_target_pairs={{0,4},{1,5},{2,6},{3,7},{4,8},{5,9},{6,10},{7,11},{8,12},{9,13},{1... | collective-permute-start | bytes 1572872 | tf_op jit(solution)/shard_map/ppermute | solution.py:41
  97.1 10.4 %collective-permute-start.33 = (bf16[4,256,256]{2,1,0:T(8,128)(2,1)S(1)}, bf16[4,256,256]{2,1,0:T(8,128)(2,1)S(1)}, u32[]{:S(2)}, u32[]{:S(2)}) collective-permute-start(bf16[4,256,256]{2,1,0:T(8,128)(2,1)S(1)} %get-tuple-element.48), channel_id=1, source_target_pairs={{0,1},{1,2},{2,3},{3,0},{4,5},{5,6},{6,7},{7,4},{8,9},{9,10},{10,1... | collective-permute-start | bytes 1572872 | tf_op jit(solution)/shard_map/ppermute | solution.py:41
  98.3 18.0 %collective-permute-start.21 = (bf16[4,256,256]{2,1,0:T(8,128)(2,1)S(1)}, bf16[4,256,256]{2,1,0:T(8,128)(2,1)S(1)}, u32[]{:S(2)}, u32[]{:S(2)}) collective-permute-start(bf16[4,256,256]{2,1,0:T(8,128)(2,1)S(1)} %add_convert_fusion.3), channel_id=1, source_target_pairs={{0,4},{1,5},{2,6},{3,7},{4,8},{5,9},{6,10},{7,11},{8,12},{9,13},{1... | collective-permute-start | bytes 1572872 | tf_op jit(solution)/shard_map/ppermute | solution.py:41
  106.6 15.6 %collective-permute-start.31 = (bf16[4,256,256]{2,1,0:T(8,128)(2,1)S(1)}, bf16[4,256,256]{2,1,0:T(8,128)(2,1)S(1)}, u32[]{:S(2)}, u32[]{:S(2)}) collective-permute-start(bf16[4,256,256]{2,1,0:T(8,128)(2,1)S(1)} %add_convert_fusion.1), channel_id=1, source_target_pairs={{0,1},{1,2},{2,3},{3,0},{4,5},{5,6},{6,7},{7,4},{8,9},{9,10},{10,1... | collective-permute-start | bytes 1572872 | tf_op jit(solution)/shard_map/ppermute | solution.py:41
  106.7 15.7 %collective-permute-start.23 = (bf16[4,256,256]{2,1,0:T(8,128)(2,1)S(1)}, bf16[4,256,256]{2,1,0:T(8,128)(2,1)S(1)}, u32[]{:S(2)}, u32[]{:S(2)}) collective-permute-start(bf16[4,256,256]{2,1,0:T(8,128)(2,1)S(1)} %get-tuple-element.38), channel_id=1, source_target_pairs={{0,12},{1,13},{2,14},{3,15},{4,0},{5,1},{6,2},{7,3},{8,4},{9,5},{1... | collective-permute-start | bytes 1572872 | tf_op jit(solution)/shard_map/ppermute | solution.py:41
  107.5 15.9 %collective-permute-start.25 = (bf16[4,256,256]{2,1,0:T(8,128)(2,1)S(1)}, bf16[4,256,256]{2,1,0:T(8,128)(2,1)S(1)}, u32[]{:S(2)}, u32[]{:S(2)}) collective-permute-start(bf16[4,256,256]{2,1,0:T(8,128)(2,1)S(1)} %add_convert_fusion.2), channel_id=1, source_target_pairs={{0,4},{1,5},{2,6},{3,7},{4,8},{5,9},{6,10},{7,11},{8,12},{9,13},{1... | collective-permute-start | bytes 1572872 | tf_op jit(solution)/shard_map/ppermute | solution.py:41
  116.3 12.0 %collective-permute-start.32 = (bf16[4,256,256]{2,1,0:T(8,128)(2,1)S(1)}, bf16[4,256,256]{2,1,0:T(8,128)(2,1)S(1)}, u32[]{:S(2)}, u32[]{:S(2)}) collective-permute-start(bf16[4,256,256]{2,1,0:T(8,128)(2,1)S(1)} %get-tuple-element.46), channel_id=1, source_target_pairs={{0,3},{1,0},{2,1},{3,2},{4,7},{5,4},{6,5},{7,6},{8,11},{9,8},{10,9... | collective-permute-start | bytes 1572872 | tf_op jit(solution)/shard_map/ppermute | solution.py:41
  116.6 14.1 %collective-permute-start.34 = (bf16[4,256,256]{2,1,0:T(8,128)(2,1)S(1)}, bf16[4,256,256]{2,1,0:T(8,128)(2,1)S(1)}, u32[]{:S(2)}, u32[]{:S(2)}) collective-permute-start(bf16[4,256,256]{2,1,0:T(8,128)(2,1)S(1)} %add_convert_fusion), channel_id=1, source_target_pairs={{0,1},{1,2},{2,3},{3,0},{4,5},{5,6},{6,7},{7,4},{8,9},{9,10},{10,1... | collective-permute-start | bytes 1572872 | tf_op jit(solution)/shard_map/ppermute | solution.py:41
  123.4 15.3 %copy-start.12 = (s32[4]{0:T(128)S(1)}, s32[4]{0:T(128)}, u32[]{:S(2)}) copy-start(s32[4]{0:T(128)} %param.14) | copy-start | bytes 52
  123.7 15.1 %collective-permute-start.26 = (bf16[2,256,256]{2,1,0:T(8,128)(2,1)S(1)}, bf16[2,256,256]{2,1,0:T(8,128)(2,1)S(1)}, u32[]{:S(2)}, u32[]{:S(2)}) collective-permute-start(bf16[2,256,256]{2,1,0:T(8,128)(2,1)S(1)} %pad_maximum_fusion.2), channel_id=1, source_target_pairs={{0,3},{1,0},{2,1},{3,2},{4,7},{5,4},{6,5},{7,6},{8,11},{9,8},{10,9... | collective-permute-start | bytes 786440 | tf_op jit(solution)/shard_map/ppermute | solution.py:41
  123.8 10.5 %collective-permute-start.27 = (bf16[2,256,256]{2,1,0:T(8,128)(2,1)S(1)}, bf16[2,256,256]{2,1,0:T(8,128)(2,1)S(1)}, u32[]{:S(2)}, u32[]{:S(2)}) collective-permute-start(bf16[2,256,256]{2,1,0:T(8,128)(2,1)S(1)} %pad_maximum_fusion.3), channel_id=1, source_target_pairs={{0,1},{1,2},{2,3},{3,0},{4,5},{5,6},{6,7},{7,4},{8,9},{9,10},{10,1... | collective-permute-start | bytes 786440 | tf_op jit(solution)/shard_map/ppermute | solution.py:41
  130.9 7.7 %collective-permute-start.36 = (bf16[2,256,256]{2,1,0:T(8,128)(2,1)S(1)}, bf16[2,256,256]{2,1,0:T(8,128)(2,1)S(1)}, u32[]{:S(2)}, u32[]{:S(2)}) collective-permute-start(bf16[2,256,256]{2,1,0:T(8,128)(2,1)S(1)} %pad_maximum_fusion.5), channel_id=1, source_target_pairs={{0,4},{1,5},{2,6},{3,7},{4,8},{5,9},{6,10},{7,11},{8,12},{9,13},{1... | collective-permute-start | bytes 786440 | tf_op jit(solution)/shard_map/ppermute | solution.py:41
  131.0 11.1 %collective-permute-start.35 = (bf16[2,256,256]{2,1,0:T(8,128)(2,1)S(1)}, bf16[2,256,256]{2,1,0:T(8,128)(2,1)S(1)}, u32[]{:S(2)}, u32[]{:S(2)}) collective-permute-start(bf16[2,256,256]{2,1,0:T(8,128)(2,1)S(1)} %pad_maximum_fusion.4), channel_id=1, source_target_pairs={{0,12},{1,13},{2,14},{3,15},{4,0},{5,1},{6,2},{7,3},{8,4},{9,5},{1... | collective-permute-start | bytes 786440 | tf_op jit(solution)/shard_map/ppermute | solution.py:41
  134.4 7.7 %collective-permute-start.28 = (bf16[2,256,256]{2,1,0:T(8,128)(2,1)S(1)}, bf16[2,256,256]{2,1,0:T(8,128)(2,1)S(1)}, u32[]{:S(2)}, u32[]{:S(2)}) collective-permute-start(bf16[2,256,256]{2,1,0:T(8,128)(2,1)S(1)} %add_convert_fusion.7), channel_id=1, source_target_pairs={{0,1},{1,2},{2,3},{3,0},{4,5},{5,6},{6,7},{7,4},{8,9},{9,10},{10,1... | collective-permute-start | bytes 786440 | tf_op jit(solution)/shard_map/ppermute | solution.py:41
  138.6 7.7 %collective-permute-start.37 = (bf16[2,256,256]{2,1,0:T(8,128)(2,1)S(1)}, bf16[2,256,256]{2,1,0:T(8,128)(2,1)S(1)}, u32[]{:S(2)}, u32[]{:S(2)}) collective-permute-start(bf16[2,256,256]{2,1,0:T(8,128)(2,1)S(1)} %add_convert_fusion.5), channel_id=1, source_target_pairs={{0,4},{1,5},{2,6},{3,7},{4,8},{5,9},{6,10},{7,11},{8,12},{9,13},{1... | collective-permute-start | bytes 786440 | tf_op jit(solution)/shard_map/ppermute | solution.py:41

commit v5 on v4

--- a/solution.py
+++ b/solution.py
@@ -13,6 +13,7 @@
 CORES = 2
 LIMIT = 48 << 20
 CALLS = ((0, 2), (1, 3))
+WAYS = (1, -1)
 AXIS = ((0, 0), (0, 1), (0, 2), (0, 3), (1, 0), (2, 0), (3, 0))
 NEAR = ((1, 1), (1, 3), (3, 1), (3, 3))
 FAR = ((1, 2), (2, 1), (2, 2), (2, 3), (3, 2))
@@ -27,10 +28,18 @@
 
 
 def hop(value, axis, distance=1):
+    return ring_send(value, axis, (distance, -distance))
+
+
+def shift(value, axis, distance):
+    return ring_send(value, axis, (distance, distance))
+
+
+def ring_send(value, axis, distances):
     pairs = []
     for row in range(RING * CORES):
         for col in range(STATES):
-            step = distance if row % CORES == 0 else -distance
+            step = distances[row % CORES]
             y, z, x = row // CORES, col // RING, col % RING
             y, z, x = (
                 (v + (step if name == axis else 0)) % RING
@@ -39,18 +48,6 @@
             target = (y * CORES + row % CORES) * STATES + z * RING + x
             pairs.append((row * STATES + col, target))
     return lax.ppermute(value, ("row", "col"), pairs)
-
-
-def send(value, axis, step):
-    pairs = []
-    for device in range(STATES):
-        z, x = device // RING, device % RING
-        if axis == "z":
-            z = (z + step) % RING
-        else:
-            x = (x + step) % RING
-        pairs.append((device, z * RING + x))
-    return lax.ppermute(value, "col", pairs)
 
 
 def swap_cores(value):
@@ -224,7 +221,7 @@
 
     order = AXIS + NEAR + FAR
     for number, a in enumerate(chosen):
-        half = a // 2
+        half, way = a // 2, WAYS[a % 2]
         for n, (i, k) in enumerate(FAR):
             block = joined(first.at[i - 1, k - 1], second.at[k - 1, i - 1])
             part[number, len(AXIS) + len(NEAR) + n] = left_product(left, src_ref, a, block)
@@ -240,7 +237,7 @@
                 get.wait()
         for ring in (2, 3, 1, 0):
             for inner in range(RING):
-                i, k = slot_state(half, (flow * ring) & 3, (flow * inner) & 3)
+                i, k = slot_state(half, (way * ring) & 3, inner)
                 outs[number * RING + ring][inner] = term(
                     mixed[i * RING + k], right, loc_ref, a, (i, k), spot
                 )
@@ -274,17 +271,19 @@
     )(src, loc, two_site, token, left, *(in_hbm(v) for v in (*right, *pieces, *near)))
 
 
-def ring_sum(blocks, axis):
+def ring_sum(blocks, axis, way):
     own, behind, far, ahead = blocks
-    straight = hop(ahead, axis, -1)
-    return own, straight, hop(add(behind, hop(far, axis, 1)), axis, 1)
+    moving, straight = lax.optimization_barrier(
+        (shift(far, axis, way), shift(ahead, axis, -way))
+    )
+    return own, straight, shift(add(behind, moving), axis, way)
 
 
 def last_sum(tiles, axis):
     blocks = [
         jnp.stack([add(*(part[n] for part in parts)) for parts in tiles]) for n in range(RING)
     ]
-    return add(*ring_sum(blocks, axis))
+    return add(blocks[0], *(shift(blocks[step], axis, step) for step in (2, 1, 3)))
 
 
 def per_device(
@@ -299,16 +298,17 @@
     ahead_x, ahead_z = hop(shard, "x", -1), hop(shard, "z", -1)
     far_x, far_z = hop(behind_x, "x", 1), hop(behind_z, "z", 1)
 
-    env_right, right_loc, _ = lax.optimization_barrier((env_right, right_loc, behind_x))
+    loc = lax.all_to_all(
+        jnp.broadcast_to(right_loc[:, 0][None, None], (STATES, 1, tiles)), "col", 0, 0, tiled=True
+    )
+    env_right, _ = lax.optimization_barrier((env_right, behind_x))
     lane = lax.broadcasted_iota(jnp.int32, (1, 1, tile), 2)
     right = jnp.swapaxes(env_right[0], 1, 2)
-    right = [jnp.where(lane < right_size[:, None, None], right, 0).astype(jnp.bfloat16)]
-    for _ in range(RING - 1):
-        right.append(hop(right[-1], "y"))
+    right = jnp.where(lane < right_size[:, None, None], right, 0).astype(jnp.bfloat16)
+    right_behind, right_ahead = hop(right, "y", 1), hop(right, "y", -1)
+    right = [right, right_behind, hop(right_behind, "y", 1), right_ahead]
     right += [swap_cores(block) for block in right]
-    loc = lax.all_to_all(
-        jnp.broadcast_to(right_loc[:, 0][None, None], (STATES, 1, tiles)), "col", 0, 0, tiled=True
-    )
+    far_x, far_z, loc = lax.optimization_barrier((far_x, far_z, loc))
 
     axis_blocks = (shard, behind_x, far_x, ahead_x, behind_z, far_z, ahead_z)
     corner_a = jnp.stack([block[:, :, :cut] for block in axis_blocks[1:4]])
@@ -316,7 +316,6 @@
     behind_a, behind_b = hop(corner_a, "z", 1), hop(corner_b, "x", 1)
     ahead_a, ahead_b = hop(corner_a, "z", -1), hop(corner_b, "x", -1)
     part_axis = left_parts(axis_kernel, len(AXIS), src, left, axis_blocks)
-    behind_a, behind_b, part_axis = lax.optimization_barrier((behind_a, behind_b, part_axis))
     far_a, far_b = hop(behind_a, "z", 1), hop(behind_b, "x", 1)
     near = (behind_a, ahead_a, behind_b, ahead_b)
     part_near = left_parts(near_kernel, len(NEAR), src, left, near)
@@ -329,7 +328,8 @@
         )
         token = swap_cores(token)
         for number, a in enumerate(chosen):
-            sums[a] = ring_sum(outs[RING * number : RING * (number + 1)], "z" if a < 2 else "x")
+            blocks, axis = outs[RING * number : RING * (number + 1)], "z" if a < 2 else "x"
+            sums[a] = ring_sum(blocks, axis, WAYS[a % 2])
     summed = jnp.concatenate(
         [last_sum((sums[0], sums[1]), "x"), last_sum((sums[2], sums[3]), "z")]
     )

time: 148 us -> 141 us (0.953)
  waiting for transfers between devices: 56.6 us -> 48.1 us
  local copies, waits for them, and re-layouts: 4.18 us -> 7.94 us
  starting transfers between devices: 55.1 us -> 53 us
    ppermute x33, waiting for transfers between devices: 53.7 us -> 46.9 us  [ring_send(): return lax.ppermute(value, ('row', 'col'), pairs)]
    all_to_all x1, starting transfers between devices: 7.79 us -> 4.65 us  [per_device(): lax.all_to_all(jnp.broadcast_to(right_loc[:, 0][None, None], (STATES, 1,...]
    all_to_all x1, waiting for transfers between devices: 2.9 us -> 0.01 us  [per_device(): lax.all_to_all(jnp.broadcast_to(right_loc[:, 0][None, None], (STATES, 1,...]
    another operation x3, local copies, waits for them, and re-layouts: 0.14 us -> 2.69 us  [per_device(): corner_b = jnp.stack([block[:, :, cut:] for block in axis_blocks[4:]])]
  transfers between devices with their start and end apart: 39 -> 39, of which waited for: 17 -> 16; matrix products, arithmetic and copies ran while one was open for 6% -> 9% of each run, Pallas kernels for 12% -> 12%
where the time goes in v5:
time: 141 us; the launch traced here: 140 us
  starting transfers between devices  53 us (38%)
  waiting for transfers between devices  48.1 us (34%)
  Pallas kernels  24.2 us (17%)
  local copies, waits for them, and re-layouts  7.94 us (6%)
  other arithmetic  6.65 us (5%)
    ppermute x33, waiting for transfers between devices, ring_send(): return lax.ppermute(value, ('row', 'col'), pairs)  46.9 us
    ppermute x33, starting transfers between devices, ring_send(): return lax.ppermute(value, ('row', 'col'), pairs)  45.9 us
    pallas_call x2, Pallas kernels, apply_terms(): pl.pallas_call(functools.partial(apply_kernel, chosen), out_shape=[out] *...  13.9 us
    pallas_call x2, Pallas kernels, left_parts(): pl.pallas_call(kernel, out_shape=pltpu.HBM(out, jnp.bfloat16), in_specs=[...  10.3 us
    all_to_all x1, starting transfers between devices, per_device(): lax.all_to_all(jnp.broadcast_to(right_loc[:, 0][None, None], (STATES, 1,...  4.65 us
  transfers between devices with their start and end apart: 39, of which 16 were waited for; matrix products, arithmetic and copies ran while one was open for 9% of the time, Pallas kernels for 12%

profile of v5, /device:TPU:0, one launch (start us, length us, event | category | flops | bytes accessed | tf_op | source)
XLA Modules:
  0.0 140.2 jit_solution(17270508964428843423)
XLA Ops:
  0.0 1.6 %collective-permute-start = (bf16[4,256,256]{2,1,0:T(8,128)(2,1)}, bf16[4,256,256]{2,1,0:T(8,128)(2,1)S(1)}, u32[]{:S(2)}, u32[]{:S(2)}) collective-permute-start(bf16[4,256,256]{2,1,0:T(8,128)(2,1)} %bitcast.32), channel_id=1, source_target_pairs={{0,1},{1,2},{2,3},{3,0},{4,5},{5,6},{6,7},{7,4},{8,9},{9,10},{10,1... | collective-permute-start | bytes 1572872 | tf_op jit(solution)/shard_map/ppermute | solution.py:50
  1.6 1.9 %collective-permute-start.2 = (bf16[4,256,256]{2,1,0:T(8,128)(2,1)}, bf16[4,256,256]{2,1,0:T(8,128)(2,1)S(1)}, u32[]{:S(2)}, u32[]{:S(2)}) collective-permute-start(bf16[4,256,256]{2,1,0:T(8,128)(2,1)} %bitcast.33), channel_id=1, source_target_pairs={{0,4},{1,5},{2,6},{3,7},{4,8},{5,9},{6,10},{7,11},{8,12},{9,13},{1... | collective-permute-start | bytes 1572872 | tf_op jit(solution)/shard_map/ppermute | solution.py:50
  3.5 1.7 %collective-permute-start.11 = (bf16[4,256,256]{2,1,0:T(8,128)(2,1)}, bf16[4,256,256]{2,1,0:T(8,128)(2,1)S(1)}, u32[]{:S(2)}, u32[]{:S(2)}) collective-permute-start(bf16[4,256,256]{2,1,0:T(8,128)(2,1)} %bitcast.34), channel_id=1, source_target_pairs={{0,3},{1,0},{2,1},{3,2},{4,7},{5,4},{6,5},{7,6},{8,11},{9,8},{10,9... | collective-permute-start | bytes 1572872 | tf_op jit(solution)/shard_map/ppermute | solution.py:50
  5.2 2.1 %collective-permute-start.15 = (bf16[4,256,256]{2,1,0:T(8,128)(2,1)}, bf16[4,256,256]{2,1,0:T(8,128)(2,1)}, u32[]{:S(2)}, u32[]{:S(2)}) collective-permute-start(bf16[4,256,256]{2,1,0:T(8,128)(2,1)} %bitcast.35), channel_id=1, source_target_pairs={{0,12},{1,13},{2,14},{3,15},{4,0},{5,1},{6,2},{7,3},{8,4},{9,5},{1... | collective-permute-start | bytes 1572872 | tf_op jit(solution)/shard_map/ppermute | solution.py:50
  7.4 1.3 broadcast_in_dim.39
  8.6 4.7 %all-to-all-start = ((s32[16,1,4]{2,1,0:T(1,128)}), s32[16,1,4]{2,1,0:T(1,128)S(1)}, u32[]{:S(2)}, u32[]{:S(2)}) async-start(s32[16,1,4]{2,1,0:T(1,128)} %broadcast_in_dim.39), calls=%async_computation | async-start | bytes 16384 | tf_op jit(solution)/shard_map/all_to_all | solution.py:301
  13.3 0.7 iota_compare_fusion
  14.0 1.4 %copy.9 = bf16[1,4,256,256]{2,3,1,0:T(8,128)(2,1)S(1)} copy(bf16[1,4,256,256]{3,2,1,0:T(8,128)(2,1)} %param.12) | data formatting | bytes 1048576 | tf_op jit(solution)/shard_map/optimization_barrier | solution.py:304
  15.5 0.8 fusion.1.refs_0_
  16.3 1.6 %collective-permute-start.4 = (bf16[4,256,256]{2,1,0:T(8,128)(2,1)}, bf16[4,256,256]{2,1,0:T(8,128)(2,1)}, u32[]{:S(2)}, u32[]{:S(2)}) collective-permute-start(bf16[4,256,256]{2,1,0:T(8,128)(2,1)} %fusion.1.refs_0_), channel_id=1, source_target_pairs={{0,32},{1,33},{2,34},{3,35},{4,36},{5,37},{6,38},{7,39},{8,40},{9,... | collective-permute-start | bytes 1572872 | tf_op jit(solution)/shard_map/ppermute | solution.py:50
  17.9 1.9 %collective-permute-start.1 = (bf16[4,256,256]{2,1,0:T(8,128)(2,1)S(1)}, bf16[4,256,256]{2,1,0:T(8,128)(2,1)S(1)}, u32[]{:S(2)}, u32[]{:S(2)}) collective-permute-start(bf16[4,256,256]{2,1,0:T(8,128)(2,1)S(1)} %collective-permute-done.refs_1_), channel_id=1, source_target_pairs={{0,1},{1,2},{2,3},{3,0},{4,5},{5,6},{6,7},{7,4},{8,9},{9,10},{10,1... | collective-permute-start | bytes 1572872 | tf_op jit(solution)/shard_map/ppermute | solution.py:50
  19.8 0.7 slice_bitcast_fusion.3
  20.6 2.4 %collective-permute-start.3 = (bf16[4,256,256]{2,1,0:T(8,128)(2,1)S(1)}, bf16[4,256,256]{2,1,0:T(8,128)(2,1)}, u32[]{:S(2)}, u32[]{:S(2)}) collective-permute-start(bf16[4,256,256]{2,1,0:T(8,128)(2,1)S(1)} %collective-permute-done.2.refs_4_), channel_id=1, source_target_pairs={{0,4},{1,5},{2,6},{3,7},{4,8},{5,9},{6,10},{7,11},{8,12},{9,13},{1... | collective-permute-start | bytes 1572872 | tf_op jit(solution)/shard_map/ppermute | solution.py:50
  23.0 1.7 %collective-permute-start.6 = (bf16[4,256,256]{2,1,0:T(8,128)(2,1)}, bf16[4,256,256]{2,1,0:T(8,128)(2,1)}, u32[]{:S(2)}, u32[]{:S(2)}) collective-permute-start(bf16[4,256,256]{2,1,0:T(8,128)(2,1)} %fusion.1.refs_0_), channel_id=1, source_target_pairs={{0,96},{1,97},{2,98},{3,99},{4,100},{5,101},{6,102},{7,103},{8,104... | collective-permute-start | bytes 1572872 | tf_op jit(solution)/shard_map/ppermute | solution.py:50
  24.7 0.8 slice_bitcast_fusion.2
  25.5 1.2 collective-permute-start.7
  26.7 1.7 %slice_bitcast_fusion = bf16[1,4,256,128]{3,2,1,0:T(8,128)(2,1)} fusion(bf16[4,256,256]{2,1,0:T(8,128)(2,1)} %collective-permute-done.15.refs_6_), kind=kLoop, calls=%fused_computation.14 | loop fusion | bytes 524288 | tf_op jit(solution)/shard_map/stack | solution.py:315
  28.4 3.9 %collective-permute-done.3.refs_5_ = bf16[4,256,256]{2,1,0:T(8,128)(2,1)} collective-permute-done((bf16[4,256,256]{2,1,0:T(8,128)(2,1)S(1)}, bf16[4,256,256]{2,1,0:T(8,128)(2,1)}, u32[]{:S(2)}, u32[]{:S(2)}) %collective-permute-start.3) | collective-permute-done | bytes 524320 | tf_op jit(solution)/shard_map/ppermute | solution.py:50
  32.3 1.1 pad_maximum_fusion
  33.5 1.0 slice_bitcast_fusion.4
  34.5 1.0 pad_maximum_fusion.1
  35.5 1.1 collective-permute-start.16
  36.7 3.2 %collective-permute-start.13 = (bf16[3,4,256,128]{3,2,1,0:T(8,128)(2,1)S(1)}, bf16[3,4,256,128]{3,2,1,0:T(8,128)(2,1)S(1)}, u32[]{:S(2)}, u32[]{:S(2)}) collective-permute-start(bf16[3,4,256,128]{3,2,1,0:T(8,128)(2,1)S(1)} %pad_maximum_fusion), channel_id=1, source_target_pairs={{0,12},{1,13},{2,14},{3,15},{4,0},{5,1},{6,2},{7,3},{8,4},{9,5},{1... | collective-permute-start | bytes 2359304 | tf_op jit(solution)/shard_map/ppermute | solution.py:50
  39.9 2.2 %collective-permute-start.17 = (bf16[3,4,256,128]{3,2,1,0:T(8,128)(2,1)S(1)}, bf16[3,4,256,128]{3,2,1,0:T(8,128)(2,1)S(1)}, u32[]{:S(2)}, u32[]{:S(2)}) collective-permute-start(bf16[3,4,256,128]{3,2,1,0:T(8,128)(2,1)S(1)} %pad_maximum_fusion.1), channel_id=1, source_target_pairs={{0,3},{1,0},{2,1},{3,2},{4,7},{5,4},{6,5},{7,6},{8,11},{9,8},{10,9... | collective-permute-start | bytes 2359304 | tf_op jit(solution)/shard_map/ppermute | solution.py:50
  42.1 1.6 %collective-permute-start.5 = (bf16[4,256,256]{2,1,0:T(8,128)(2,1)}, bf16[4,256,256]{2,1,0:T(8,128)(2,1)}, u32[]{:S(2)}, u32[]{:S(2)}) collective-permute-start(bf16[4,256,256]{2,1,0:T(8,128)(2,1)} %collective-permute-done.4.refs_1_), channel_id=1, source_target_pairs={{0,32},{1,33},{2,34},{3,35},{4,36},{5,37},{6,38},{7,39},{8,40},{9,... | collective-permute-start | bytes 1572872 | tf_op jit(solution)/shard_map/ppermute | solution.py:50
  43.6 6.9 %collective-permute-done.12.refs_0_.refs_8_ = bf16[3,4,256,128]{3,2,1,0:T(8,128)(2,1)S(1)} collective-permute-done((bf16[3,4,256,128]{3,2,1,0:T(8,128)(2,1)S(1)}, bf16[3,4,256,128]{3,2,1,0:T(8,128)(2,1)S(1)}, u32[]{:S(2)}, u32[]{:S(2)}) %collective-permute-start.12) | collective-permute-done | bytes 786464 | tf_op jit(solution)/shard_map/ppermute | solution.py:50
  50.6 4.1 %collective-permute-done.16.refs_2_.refs_11_ = bf16[3,4,256,128]{3,2,1,0:T(8,128)(2,1)S(1)} collective-permute-done((bf16[3,4,256,128]{3,2,1,0:T(8,128)(2,1)S(1)}, bf16[3,4,256,128]{3,2,1,0:T(8,128)(2,1)S(1)}, u32[]{:S(2)}, u32[]{:S(2)}) %collective-permute-start.16) | collective-permute-done | bytes 786464 | tf_op jit(solution)/shard_map/ppermute | solution.py:50
  54.7 1.1 collective-permute-start.8
  55.9 1.9 %collective-permute-done.17.refs_3_.refs_12_ = bf16[3,4,256,128]{3,2,1,0:T(8,128)(2,1)S(1)} collective-permute-done((bf16[3,4,256,128]{3,2,1,0:T(8,128)(2,1)S(1)}, bf16[3,4,256,128]{3,2,1,0:T(8,128)(2,1)S(1)}, u32[]{:S(2)}, u32[]{:S(2)}) %collective-permute-start.17) | collective-permute-done | bytes 786464 | tf_op jit(solution)/shard_map/ppermute | solution.py:50
  57.9 0.9 copy-done.5
  58.9 5.7 %left_parts.2.refs_14_ = bf16[7,4,256,256]{3,2,1,0:T(8,128)(2,1)} custom-call(s32[4,2]{1,0:T(4,128)S(1)} %copy.12.src_ref, bf16[4,2,256,256]{3,2,1,0:T(8,128)(2,1)S(1)} %bitcast.28, bf16[4,256,256]{2,1,0:T(8,128)(2,1)} %bitcast.36, bf16[4,256,256]{2,1,0:T(8,128)(2,1)} %copy-done.6, bf16[4,256,256]{2,1,0:T(8,128)(2,1)} %copy-done.9, ...), custom_call_target="tpu_custom_call" | custom-call | flops 1879048192 | bytes 5242880 | tf_op jit(solution)/shard_map/left_parts/pallas_call | solution.py:119
  64.6 4.6 %left_parts.3.refs_15_ = bf16[4,4,256,256]{3,2,1,0:T(8,128)(2,1)} custom-call(s32[4,2]{1,0:T(4,128)S(1)} %copy.12.src_ref, bf16[4,2,256,256]{3,2,1,0:T(8,128)(2,1)S(1)} %bitcast.29, bf16[3,4,256,128]{3,2,1,0:T(8,128)(2,1)} %copy-done.2, bf16[3,4,256,128]{3,2,1,0:T(8,128)(2,1)} %copy-done.4, bf16[3,4,256,128]{3,2,1,0:T(8,128)(2,1)} %copy-done.3, ...), custom_call_target="tpu_custom_call" | custom-call | flops 1073741824 | bytes 5242880 | tf_op jit(solution)/shard_map/left_parts/pallas_call | solution.py:119
  69.3 6.9 %apply_terms.2 = (bf16[4,256,256]{2,1,0:T(8,128)(2,1)S(1)}, bf16[4,256,256]{2,1,0:T(8,128)(2,1)S(1)}, bf16[4,256,256]{2,1,0:T(8,128)(2,1)S(1)}, bf16[4,256,256]{...) custom-call(s32[4,2]{1,0:T(4,128)S(1)} %copy.12.src_ref, ...), custom_call_target="tpu_custom_call" | custom-call | flops 2684354560 | bytes 8388608 | tf_op jit(solution)/shard_map/apply_terms/pallas_call | solution.py:251
  76.2 2.8 %collective-permute-start.19 = (bf16[4,256,256]{2,1,0:T(8,128)(2,1)S(1)}, bf16[4,256,256]{2,1,0:T(8,128)(2,1)S(1)}, u32[]{:S(2)}, u32[]{:S(2)}) collective-permute-start(bf16[4,256,256]{2,1,0:T(8,128)(2,1)S(1)} %get-tuple-element.39), channel_id=1, source_target_pairs={{0,4},{1,5},{2,6},{3,7},{4,8},{5,9},{6,10},{7,11},{8,12},{9,13},{1... | collective-permute-start | bytes 1572872 | tf_op jit(solution)/shard_map/ppermute | solution.py:50
  79.0 0.5 collective-permute-start.20
  79.7 3.0 %collective-permute-start.30 = (bf16[4,256,256]{2,1,0:T(8,128)(2,1)S(1)}, bf16[4,256,256]{2,1,0:T(8,128)(2,1)S(1)}, u32[]{:S(2)}, u32[]{:S(2)}) collective-permute-start(bf16[4,256,256]{2,1,0:T(8,128)(2,1)S(1)} %get-tuple-element.53), channel_id=1, source_target_pairs={{0,3},{1,0},{2,1},{3,2},{4,7},{5,4},{6,5},{7,6},{8,11},{9,8},{10,9... | collective-permute-start | bytes 1572872 | tf_op jit(solution)/shard_map/ppermute | solution.py:50
  82.7 1.2 collective-permute-done.22.token_ref
  83.9 7.0 %apply_terms.3 = (bf16[4,256,256]{2,1,0:T(8,128)(2,1)S(1)}, bf16[4,256,256]{2,1,0:T(8,128)(2,1)S(1)}, bf16[4,256,256]{2,1,0:T(8,128)(2,1)S(1)}, bf16[4,256,256]{...) custom-call(s32[4,2]{1,0:T(4,128)S(1)} %copy.12.src_ref, ...), custom_call_target="tpu_custom_call" | custom-call | flops 2684354560 | bytes 8388608 | tf_op jit(solution)/shard_map/apply_terms/pallas_call | solution.py:251
  90.9 1.8 %collective-permute-start.23 = (bf16[4,256,256]{2,1,0:T(8,128)(2,1)S(1)}, bf16[4,256,256]{2,1,0:T(8,128)(2,1)S(1)}, u32[]{:S(2)}, u32[]{:S(2)}) collective-permute-start(bf16[4,256,256]{2,1,0:T(8,128)(2,1)S(1)} %get-tuple-element.46), channel_id=1, source_target_pairs={{0,12},{1,13},{2,14},{3,15},{4,0},{5,1},{6,2},{7,3},{8,4},{9,5},{1... | collective-permute-start | bytes 1572872 | tf_op jit(solution)/shard_map/ppermute | solution.py:50
  92.7 0.3 collective-permute-start.24
  93.0 1.9 %collective-permute-start.32 = (bf16[4,256,256]{2,1,0:T(8,128)(2,1)S(1)}, bf16[4,256,256]{2,1,0:T(8,128)(2,1)S(1)}, u32[]{:S(2)}, u32[]{:S(2)}) collective-permute-start(bf16[4,256,256]{2,1,0:T(8,128)(2,1)S(1)} %get-tuple-element.58), channel_id=1, source_target_pairs={{0,3},{1,0},{2,1},{3,2},{4,7},{5,4},{6,5},{7,6},{8,11},{9,8},{10,9... | collective-permute-start | bytes 1572872 | tf_op jit(solution)/shard_map/ppermute | solution.py:50
  95.3 1.5 %collective-permute-start.21 = (bf16[4,256,256]{2,1,0:T(8,128)(2,1)S(1)}, bf16[4,256,256]{2,1,0:T(8,128)(2,1)S(1)}, u32[]{:S(2)}, u32[]{:S(2)}) collective-permute-start(bf16[4,256,256]{2,1,0:T(8,128)(2,1)S(1)} %add_convert_fusion.3), channel_id=1, source_target_pairs={{0,4},{1,5},{2,6},{3,7},{4,8},{5,9},{6,10},{7,11},{8,12},{9,13},{1... | collective-permute-start | bytes 1572872 | tf_op jit(solution)/shard_map/ppermute | solution.py:50
  97.0 8.0 %collective-permute-done.23 = bf16[4,256,256]{2,1,0:T(8,128)(2,1)S(1)} collective-permute-done((bf16[4,256,256]{2,1,0:T(8,128)(2,1)S(1)}, bf16[4,256,256]{2,1,0:T(8,128)(2,1)S(1)}, u32[]{:S(2)}, u32[]{:S(2)}) %collective-permute-start.23) | collective-permute-done | bytes 524320 | tf_op jit(solution)/shard_map/ppermute | solution.py:50
  105.0 3.8 %collective-permute-done.24 = bf16[4,256,256]{2,1,0:T(8,128)(2,1)S(1)} collective-permute-done((bf16[4,256,256]{2,1,0:T(8,128)(2,1)S(1)}, bf16[4,256,256]{2,1,0:T(8,128)(2,1)S(1)}, u32[]{:S(2)}, u32[]{:S(2)}) %collective-permute-start.24) | collective-permute-done | bytes 524320 | tf_op jit(solution)/shard_map/ppermute | solution.py:50
  108.9 0.8 collective-permute-start.25
  109.9 1.7 %collective-permute-start.34 = (bf16[4,256,256]{2,1,0:T(8,128)(2,1)S(1)}, bf16[4,256,256]{2,1,0:T(8,128)(2,1)S(1)}, u32[]{:S(2)}, u32[]{:S(2)}) collective-permute-start(bf16[4,256,256]{2,1,0:T(8,128)(2,1)S(1)} %add_convert_fusion), channel_id=1, source_target_pairs={{0,3},{1,0},{2,1},{3,2},{4,7},{5,4},{6,5},{7,6},{8,11},{9,8},{10,9... | collective-permute-start | bytes 1572872 | tf_op jit(solution)/shard_map/ppermute | solution.py:50
  111.6 7.3 %collective-permute-done.21 = bf16[4,256,256]{2,1,0:T(8,128)(2,1)S(1)} collective-permute-done((bf16[4,256,256]{2,1,0:T(8,128)(2,1)S(1)}, bf16[4,256,256]{2,1,0:T(8,128)(2,1)S(1)}, u32[]{:S(2)}, u32[]{:S(2)}) %collective-permute-start.21) | collective-permute-done | bytes 524320 | tf_op jit(solution)/shard_map/ppermute | solution.py:50
  118.9 0.2 add_convert_fusion.21
  119.1 1.1 collective-permute-done.31
  120.4 0.3 collective-permute-done.25
  121.0 0.2 collective-permute-start.26
  121.2 1.9 %collective-permute-start.27 = (bf16[2,256,256]{2,1,0:T(8,128)(2,1)S(1)}, bf16[2,256,256]{2,1,0:T(8,128)(2,1)S(1)}, u32[]{:S(2)}, u32[]{:S(2)}) collective-permute-start(bf16[2,256,256]{2,1,0:T(8,128)(2,1)S(1)} %pad_maximum_fusion.3), channel_id=1, source_target_pairs={{0,1},{1,2},{2,3},{3,0},{4,5},{5,6},{6,7},{7,4},{8,9},{9,10},{10,1... | collective-permute-start | bytes 786440 | tf_op jit(solution)/shard_map/ppermute | solution.py:50
  123.1 1.5 %collective-permute-start.28 = (bf16[2,256,256]{2,1,0:T(8,128)(2,1)S(1)}, bf16[2,256,256]{2,1,0:T(8,128)(2,1)S(1)}, u32[]{:S(2)}, u32[]{:S(2)}) collective-permute-start(bf16[2,256,256]{2,1,0:T(8,128)(2,1)S(1)} %pad_maximum_fusion.4), channel_id=1, source_target_pairs={{0,3},{1,0},{2,1},{3,2},{4,7},{5,4},{6,5},{7,6},{8,11},{9,8},{10,9... | collective-permute-start | bytes 786440 | tf_op jit(solution)/shard_map/ppermute | solution.py:50
  124.6 2.2 %collective-permute-done.34 = bf16[4,256,256]{2,1,0:T(8,128)(2,1)S(1)} collective-permute-done((bf16[4,256,256]{2,1,0:T(8,128)(2,1)S(1)}, bf16[4,256,256]{2,1,0:T(8,128)(2,1)S(1)}, u32[]{:S(2)}, u32[]{:S(2)}) %collective-permute-start.34) | collective-permute-done | bytes 524320 | tf_op jit(solution)/shard_map/ppermute | solution.py:50
  126.9 0.2 add_convert_fusion.12
  127.1 0.4 collective-permute-start.35
  127.5 2.0 %collective-permute-start.36 = (bf16[2,256,256]{2,1,0:T(8,128)(2,1)S(1)}, bf16[2,256,256]{2,1,0:T(8,128)(2,1)S(1)}, u32[]{:S(2)}, u32[]{:S(2)}) collective-permute-start(bf16[2,256,256]{2,1,0:T(8,128)(2,1)S(1)} %pad_maximum_fusion.6), channel_id=1, source_target_pairs={{0,4},{1,5},{2,6},{3,7},{4,8},{5,9},{6,10},{7,11},{8,12},{9,13},{1... | collective-permute-start | bytes 786440 | tf_op jit(solution)/shard_map/ppermute | solution.py:50
  129.5 2.3 %collective-permute-done.26 = bf16[2,256,256]{2,1,0:T(8,128)(2,1)S(1)} collective-permute-done((bf16[2,256,256]{2,1,0:T(8,128)(2,1)S(1)}, bf16[2,256,256]{2,1,0:T(8,128)(2,1)S(1)}, u32[]{:S(2)}, u32[]{:S(2)}) %collective-permute-start.26) | collective-permute-done | bytes 262176 | tf_op jit(solution)/shard_map/ppermute | solution.py:50
  131.8 2.1 %collective-permute-start.37 = (bf16[2,256,256]{2,1,0:T(8,128)(2,1)S(1)}, bf16[2,256,256]{2,1,0:T(8,128)(2,1)S(1)}, u32[]{:S(2)}, u32[]{:S(2)}) collective-permute-start(bf16[2,256,256]{2,1,0:T(8,128)(2,1)S(1)} %pad_maximum_fusion.7), channel_id=1, source_target_pairs={{0,12},{1,13},{2,14},{3,15},{4,0},{5,1},{6,2},{7,3},{8,4},{9,5},{1... | collective-permute-start | bytes 786440 | tf_op jit(solution)/shard_map/ppermute | solution.py:50
  133.9 1.3 collective-permute-done.27
  135.4 0.6 collective-permute-done.35
  136.0 2.7 %collective-permute-done.36 = bf16[2,256,256]{2,1,0:T(8,128)(2,1)S(1)} collective-permute-done((bf16[2,256,256]{2,1,0:T(8,128)(2,1)S(1)}, bf16[2,256,256]{2,1,0:T(8,128)(2,1)S(1)}, u32[]{:S(2)}, u32[]{:S(2)}) %collective-permute-start.36) | collective-permute-done | bytes 262176 | tf_op jit(solution)/shard_map/ppermute | solution.py:50
  138.7 0.4 collective-permute-done.37
  139.2 1.0 fusion
  (74 shorter events, 2.4 us)
Async XLA Ops:
  0.0 14.0 %collective-permute-start = (bf16[4,256,256]{2,1,0:T(8,128)(2,1)}, bf16[4,256,256]{2,1,0:T(8,128)(2,1)S(1)}, u32[]{:S(2)}, u32[]{:S(2)}) collective-permute-start(bf16[4,256,256]{2,1,0:T(8,128)(2,1)} %bitcast.32), channel_id=1, source_target_pairs={{0,1},{1,2},{2,3},{3,0},{4,5},{5,6},{6,7},{7,4},{8,9},{9,10},{10,1... | collective-permute-start | bytes 1572872 | tf_op jit(solution)/shard_map/ppermute | solution.py:50
  1.6 19.0 %collective-permute-start.2 = (bf16[4,256,256]{2,1,0:T(8,128)(2,1)}, bf16[4,256,256]{2,1,0:T(8,128)(2,1)S(1)}, u32[]{:S(2)}, u32[]{:S(2)}) collective-permute-start(bf16[4,256,256]{2,1,0:T(8,128)(2,1)} %bitcast.33), channel_id=1, source_target_pairs={{0,4},{1,5},{2,6},{3,7},{4,8},{5,9},{6,10},{7,11},{8,12},{9,13},{1... | collective-permute-start | bytes 1572872 | tf_op jit(solution)/shard_map/ppermute | solution.py:50
  3.5 19.5 %collective-permute-start.11 = (bf16[4,256,256]{2,1,0:T(8,128)(2,1)}, bf16[4,256,256]{2,1,0:T(8,128)(2,1)S(1)}, u32[]{:S(2)}, u32[]{:S(2)}) collective-permute-start(bf16[4,256,256]{2,1,0:T(8,128)(2,1)} %bitcast.34), channel_id=1, source_target_pairs={{0,3},{1,0},{2,1},{3,2},{4,7},{5,4},{6,5},{7,6},{8,11},{9,8},{10,9... | collective-permute-start | bytes 1572872 | tf_op jit(solution)/shard_map/ppermute | solution.py:50
  5.2 20.2 %collective-permute-start.15 = (bf16[4,256,256]{2,1,0:T(8,128)(2,1)}, bf16[4,256,256]{2,1,0:T(8,128)(2,1)}, u32[]{:S(2)}, u32[]{:S(2)}) collective-permute-start(bf16[4,256,256]{2,1,0:T(8,128)(2,1)} %bitcast.35), channel_id=1, source_target_pairs={{0,12},{1,13},{2,14},{3,15},{4,0},{5,1},{6,2},{7,3},{8,4},{9,5},{1... | collective-permute-start | bytes 1572872 | tf_op jit(solution)/shard_map/ppermute | solution.py:50
  8.6 19.7 %all-to-all-start = ((s32[16,1,4]{2,1,0:T(1,128)}), s32[16,1,4]{2,1,0:T(1,128)S(1)}, u32[]{:S(2)}, u32[]{:S(2)}) async-start(s32[16,1,4]{2,1,0:T(1,128)} %broadcast_in_dim.39), calls=%async_computation | async-start | bytes 16384 | tf_op jit(solution)/shard_map/all_to_all | solution.py:301
  14.0 18.3 %copy-start.6 = (bf16[4,256,256]{2,1,0:T(8,128)(2,1)}, bf16[4,256,256]{2,1,0:T(8,128)(2,1)S(1)}, u32[]{:S(2)}) copy-start(bf16[4,256,256]{2,1,0:T(8,128)(2,1)S(1)} %collective-permute-done.refs_1_) | copy-start | bytes 1572868
  15.4 43.3 %copy-start.10 = (s32[1,4,2]{1,2,0:T(2,128)S(1)}, s32[1,4,2]{1,2,0:T(2,128)}, u32[]{:S(2)}) copy-start(s32[1,4,2]{1,2,0:T(2,128)} %param.10) | copy-start | bytes 100
  15.5 43.4 %copy-start = (bf16[1,4,2,256,256]{4,3,2,1,0:T(8,128)(2,1)S(1)}, bf16[1,4,2,256,256]{4,3,2,1,0:T(8,128)(2,1)}, u32[]{:S(2)}) copy-start(bf16[1,4,2,256,256]{4,3,2,1,0:T(8,128)(2,1)} %param.9) | copy-start | bytes 3145732
  16.3 20.3 %collective-permute-start.4 = (bf16[4,256,256]{2,1,0:T(8,128)(2,1)}, bf16[4,256,256]{2,1,0:T(8,128)(2,1)}, u32[]{:S(2)}, u32[]{:S(2)}) collective-permute-start(bf16[4,256,256]{2,1,0:T(8,128)(2,1)} %fusion.1.refs_0_), channel_id=1, source_target_pairs={{0,32},{1,33},{2,34},{3,35},{4,36},{5,37},{6,38},{7,39},{8,40},{9,... | collective-permute-start | bytes 1572872 | tf_op jit(solution)/shard_map/ppermute | solution.py:50
  17.9 10.5 %collective-permute-start.1 = (bf16[4,256,256]{2,1,0:T(8,128)(2,1)S(1)}, bf16[4,256,256]{2,1,0:T(8,128)(2,1)S(1)}, u32[]{:S(2)}, u32[]{:S(2)}) collective-permute-start(bf16[4,256,256]{2,1,0:T(8,128)(2,1)S(1)} %collective-permute-done.refs_1_), channel_id=1, source_target_pairs={{0,1},{1,2},{2,3},{3,0},{4,5},{5,6},{6,7},{7,4},{8,9},{9,10},{10,1... | collective-permute-start | bytes 1572872 | tf_op jit(solution)/shard_map/ppermute | solution.py:50
  20.6 13.9 %copy-start.7 = (bf16[4,256,256]{2,1,0:T(8,128)(2,1)}, bf16[4,256,256]{2,1,0:T(8,128)(2,1)S(1)}, u32[]{:S(2)}) copy-start(bf16[4,256,256]{2,1,0:T(8,128)(2,1)S(1)} %collective-permute-done.2.refs_4_) | copy-start | bytes 1572868
  20.6 11.7 %collective-permute-start.3 = (bf16[4,256,256]{2,1,0:T(8,128)(2,1)S(1)}, bf16[4,256,256]{2,1,0:T(8,128)(2,1)}, u32[]{:S(2)}, u32[]{:S(2)}) collective-permute-start(bf16[4,256,256]{2,1,0:T(8,128)(2,1)S(1)} %collective-permute-done.2.refs_4_), channel_id=1, source_target_pairs={{0,4},{1,5},{2,6},{3,7},{4,8},{5,9},{6,10},{7,11},{8,12},{9,13},{1... | collective-permute-start | bytes 1572872 | tf_op jit(solution)/shard_map/ppermute | solution.py:50
  23.0 11.5 %copy-start.8 = (bf16[4,256,256]{2,1,0:T(8,128)(2,1)}, bf16[4,256,256]{2,1,0:T(8,128)(2,1)S(1)}, u32[]{:S(2)}) copy-start(bf16[4,256,256]{2,1,0:T(8,128)(2,1)S(1)} %collective-permute-done.11.refs_3_) | copy-start | bytes 1572868
  23.0 16.9 %collective-permute-start.6 = (bf16[4,256,256]{2,1,0:T(8,128)(2,1)}, bf16[4,256,256]{2,1,0:T(8,128)(2,1)}, u32[]{:S(2)}, u32[]{:S(2)}) collective-permute-start(bf16[4,256,256]{2,1,0:T(8,128)(2,1)} %fusion.1.refs_0_), channel_id=1, source_target_pairs={{0,96},{1,97},{2,98},{3,99},{4,100},{5,101},{6,102},{7,103},{8,104... | collective-permute-start | bytes 1572872 | tf_op jit(solution)/shard_map/ppermute | solution.py:50
  25.5 16.6 %collective-permute-start.7 = (bf16[4,256,256]{2,1,0:T(8,128)(2,1)}, bf16[4,256,256]{2,1,0:T(8,128)(2,1)}, u32[]{:S(2)}, u32[]{:S(2)}) collective-permute-start(bf16[4,256,256]{2,1,0:T(8,128)(2,1)} %fusion.1.refs_0_), channel_id=1, source_target_pairs={{0,16},{16,0},{32,48},{48,32},{64,80},{80,64},{96,112},{112,96},{1... | collective-permute-start | bytes 1572872 | tf_op jit(solution)/shard_map/ppermute | solution.py:54
  28.4 3.9 %copy-start.9 = (bf16[4,256,256]{2,1,0:T(8,128)(2,1)}, bf16[4,256,256]{2,1,0:T(8,128)(2,1)S(1)}, u32[]{:S(2)}) copy-start(bf16[4,256,256]{2,1,0:T(8,128)(2,1)S(1)} %collective-permute-done.1.refs_2_) | copy-start | bytes 1572868
  33.4 17.1 %collective-permute-start.12 = (bf16[3,4,256,128]{3,2,1,0:T(8,128)(2,1)S(1)}, bf16[3,4,256,128]{3,2,1,0:T(8,128)(2,1)S(1)}, u32[]{:S(2)}, u32[]{:S(2)}) collective-permute-start(bf16[3,4,256,128]{3,2,1,0:T(8,128)(2,1)S(1)} %pad_maximum_fusion), channel_id=1, source_target_pairs={{0,4},{1,5},{2,6},{3,7},{4,8},{5,9},{6,10},{7,11},{8,12},{9,13},{1... | collective-permute-start | bytes 2359304 | tf_op jit(solution)/shard_map/ppermute | solution.py:50
  35.5 19.2 %collective-permute-start.16 = (bf16[3,4,256,128]{3,2,1,0:T(8,128)(2,1)S(1)}, bf16[3,4,256,128]{3,2,1,0:T(8,128)(2,1)S(1)}, u32[]{:S(2)}, u32[]{:S(2)}) collective-permute-start(bf16[3,4,256,128]{3,2,1,0:T(8,128)(2,1)S(1)} %pad_maximum_fusion.1), channel_id=1, source_target_pairs={{0,1},{1,2},{2,3},{3,0},{4,5},{5,6},{6,7},{7,4},{8,9},{9,10},{10,1... | collective-permute-start | bytes 2359304 | tf_op jit(solution)/shard_map/ppermute | solution.py:50
  36.7 19.2 %collective-permute-start.13 = (bf16[3,4,256,128]{3,2,1,0:T(8,128)(2,1)S(1)}, bf16[3,4,256,128]{3,2,1,0:T(8,128)(2,1)S(1)}, u32[]{:S(2)}, u32[]{:S(2)}) collective-permute-start(bf16[3,4,256,128]{3,2,1,0:T(8,128)(2,1)S(1)} %pad_maximum_fusion), channel_id=1, source_target_pairs={{0,12},{1,13},{2,14},{3,15},{4,0},{5,1},{6,2},{7,3},{8,4},{9,5},{1... | collective-permute-start | bytes 2359304 | tf_op jit(solution)/shard_map/ppermute | solution.py:50
  39.9 18.0 %collective-permute-start.17 = (bf16[3,4,256,128]{3,2,1,0:T(8,128)(2,1)S(1)}, bf16[3,4,256,128]{3,2,1,0:T(8,128)(2,1)S(1)}, u32[]{:S(2)}, u32[]{:S(2)}) collective-permute-start(bf16[3,4,256,128]{3,2,1,0:T(8,128)(2,1)S(1)} %pad_maximum_fusion.1), channel_id=1, source_target_pairs={{0,3},{1,0},{2,1},{3,2},{4,7},{5,4},{6,5},{7,6},{8,11},{9,8},{10,9... | collective-permute-start | bytes 2359304 | tf_op jit(solution)/shard_map/ppermute | solution.py:50
  42.1 12.6 %collective-permute-start.5 = (bf16[4,256,256]{2,1,0:T(8,128)(2,1)}, bf16[4,256,256]{2,1,0:T(8,128)(2,1)}, u32[]{:S(2)}, u32[]{:S(2)}) collective-permute-start(bf16[4,256,256]{2,1,0:T(8,128)(2,1)} %collective-permute-done.4.refs_1_), channel_id=1, source_target_pairs={{0,32},{1,33},{2,34},{3,35},{4,36},{5,37},{6,38},{7,39},{8,40},{9,... | collective-permute-start | bytes 1572872 | tf_op jit(solution)/shard_map/ppermute | solution.py:50
  50.6 14.0 %copy-start.2 = (bf16[3,4,256,128]{3,2,1,0:T(8,128)(2,1)}, bf16[3,4,256,128]{3,2,1,0:T(8,128)(2,1)S(1)}, u32[]{:S(2)}) copy-start(bf16[3,4,256,128]{3,2,1,0:T(8,128)(2,1)S(1)} %collective-permute-done.12.refs_0_.refs_8_) | copy-start | bytes 2359300
  50.6 18.7 %collective-permute-start.14 = (bf16[3,4,256,128]{3,2,1,0:T(8,128)(2,1)S(1)}, bf16[3,4,256,128]{3,2,1,0:T(8,128)(2,1)}, u32[]{:S(2)}, u32[]{:S(2)}) collective-permute-start(bf16[3,4,256,128]{3,2,1,0:T(8,128)(2,1)S(1)} %collective-permute-done.12.refs_0_.refs_8_), channel_id=1, source_target_pairs={{0,4},{1,5},{2,6},{3,7},{4,8},{5,9},{6,10},{7,11},{8,12},{9,13},{1... | collective-permute-start | bytes 2359304 | tf_op jit(solution)/shard_map/ppermute | solution.py:50
  54.7 9.9 %copy-start.3 = (bf16[3,4,256,128]{3,2,1,0:T(8,128)(2,1)}, bf16[3,4,256,128]{3,2,1,0:T(8,128)(2,1)S(1)}, u32[]{:S(2)}) copy-start(bf16[3,4,256,128]{3,2,1,0:T(8,128)(2,1)S(1)} %collective-permute-done.16.refs_2_.refs_11_) | copy-start | bytes 2359300
  54.7 14.6 %collective-permute-start.18 = (bf16[3,4,256,128]{3,2,1,0:T(8,128)(2,1)S(1)}, bf16[3,4,256,128]{3,2,1,0:T(8,128)(2,1)}, u32[]{:S(2)}, u32[]{:S(2)}) collective-permute-start(bf16[3,4,256,128]{3,2,1,0:T(8,128)(2,1)S(1)} %collective-permute-done.16.refs_2_.refs_11_), channel_id=1, source_target_pairs={{0,1},{1,2},{2,3},{3,0},{4,5},{5,6},{6,7},{7,4},{8,9},{9,10},{10,1... | collective-permute-start | bytes 2359304 | tf_op jit(solution)/shard_map/ppermute | solution.py:50
  54.7 14.5 %collective-permute-start.8 = (bf16[4,256,256]{2,1,0:T(8,128)(2,1)}, bf16[4,256,256]{2,1,0:T(8,128)(2,1)}, u32[]{:S(2)}, u32[]{:S(2)}) collective-permute-start(bf16[4,256,256]{2,1,0:T(8,128)(2,1)} %collective-permute-done.4.refs_1_), channel_id=1, source_target_pairs={{0,16},{16,0},{32,48},{48,32},{64,80},{80,64},{96,112},{112,96},{1... | collective-permute-start | bytes 1572872 | tf_op jit(solution)/shard_map/ppermute | solution.py:54
  55.8 8.7 %copy-start.4 = (bf16[3,4,256,128]{3,2,1,0:T(8,128)(2,1)}, bf16[3,4,256,128]{3,2,1,0:T(8,128)(2,1)S(1)}, u32[]{:S(2)}) copy-start(bf16[3,4,256,128]{3,2,1,0:T(8,128)(2,1)S(1)} %collective-permute-done.13.refs_1_.refs_9_) | copy-start | bytes 2359300
  55.8 13.4 %collective-permute-start.10 = (bf16[4,256,256]{2,1,0:T(8,128)(2,1)}, bf16[4,256,256]{2,1,0:T(8,128)(2,1)}, u32[]{:S(2)}, u32[]{:S(2)}) collective-permute-start(bf16[4,256,256]{2,1,0:T(8,128)(2,1)} %collective-permute-done.6.refs_3_), channel_id=1, source_target_pairs={{0,16},{16,0},{32,48},{48,32},{64,80},{80,64},{96,112},{112,96},{1... | collective-permute-start | bytes 1572872 | tf_op jit(solution)/shard_map/ppermute | solution.py:54
  57.9 0.9 copy-start.5
  57.9 11.4 %collective-permute-start.9 = (bf16[4,256,256]{2,1,0:T(8,128)(2,1)}, bf16[4,256,256]{2,1,0:T(8,128)(2,1)}, u32[]{:S(2)}, u32[]{:S(2)}) collective-permute-start(bf16[4,256,256]{2,1,0:T(8,128)(2,1)} %collective-permute-done.5.refs_2_), channel_id=1, source_target_pairs={{0,16},{16,0},{32,48},{48,32},{64,80},{80,64},{96,112},{112,96},{1... | collective-permute-start | bytes 1572872 | tf_op jit(solution)/shard_map/ppermute | solution.py:54
  64.6 4.7 %copy-start.1 = (bf16[1,16,16]{2,1,0:T(8,128)(2,1)S(1)}, bf16[1,16,16]{2,1,0:T(8,128)(2,1)}, u32[]{:S(2)}) copy-start(bf16[1,16,16]{2,1,0:T(8,128)(2,1)} %two_site_ref.3) | copy-start | bytes 1540
  76.2 16.6 %collective-permute-start.19 = (bf16[4,256,256]{2,1,0:T(8,128)(2,1)S(1)}, bf16[4,256,256]{2,1,0:T(8,128)(2,1)S(1)}, u32[]{:S(2)}, u32[]{:S(2)}) collective-permute-start(bf16[4,256,256]{2,1,0:T(8,128)(2,1)S(1)} %get-tuple-element.39), channel_id=1, source_target_pairs={{0,4},{1,5},{2,6},{3,7},{4,8},{5,9},{6,10},{7,11},{8,12},{9,13},{1... | collective-permute-start | bytes 1572872 | tf_op jit(solution)/shard_map/ppermute | solution.py:50
  79.0 14.0 %collective-permute-start.20 = (bf16[4,256,256]{2,1,0:T(8,128)(2,1)S(1)}, bf16[4,256,256]{2,1,0:T(8,128)(2,1)S(1)}, u32[]{:S(2)}, u32[]{:S(2)}) collective-permute-start(bf16[4,256,256]{2,1,0:T(8,128)(2,1)S(1)} %get-tuple-element.40), channel_id=1, source_target_pairs={{0,12},{1,13},{2,14},{3,15},{4,0},{5,1},{6,2},{7,3},{8,4},{9,5},{1... | collective-permute-start | bytes 1572872 | tf_op jit(solution)/shard_map/ppermute | solution.py:50
  79.5 15.6 %collective-permute-start.29 = (bf16[4,256,256]{2,1,0:T(8,128)(2,1)S(1)}, bf16[4,256,256]{2,1,0:T(8,128)(2,1)S(1)}, u32[]{:S(2)}, u32[]{:S(2)}) collective-permute-start(bf16[4,256,256]{2,1,0:T(8,128)(2,1)S(1)} %get-tuple-element.52), channel_id=1, source_target_pairs={{0,1},{1,2},{2,3},{3,0},{4,5},{5,6},{6,7},{7,4},{8,9},{9,10},{10,1... | collective-permute-start | bytes 1572872 | tf_op jit(solution)/shard_map/ppermute | solution.py:50
  79.7 15.6 %collective-permute-start.30 = (bf16[4,256,256]{2,1,0:T(8,128)(2,1)S(1)}, bf16[4,256,256]{2,1,0:T(8,128)(2,1)S(1)}, u32[]{:S(2)}, u32[]{:S(2)}) collective-permute-start(bf16[4,256,256]{2,1,0:T(8,128)(2,1)S(1)} %get-tuple-element.53), channel_id=1, source_target_pairs={{0,3},{1,0},{2,1},{3,2},{4,7},{5,4},{6,5},{7,6},{8,11},{9,8},{10,9... | collective-permute-start | bytes 1572872 | tf_op jit(solution)/shard_map/ppermute | solution.py:50
  82.7 1.2 collective-permute-start.22
  90.9 14.1 %collective-permute-start.23 = (bf16[4,256,256]{2,1,0:T(8,128)(2,1)S(1)}, bf16[4,256,256]{2,1,0:T(8,128)(2,1)S(1)}, u32[]{:S(2)}, u32[]{:S(2)}) collective-permute-start(bf16[4,256,256]{2,1,0:T(8,128)(2,1)S(1)} %get-tuple-element.46), channel_id=1, source_target_pairs={{0,12},{1,13},{2,14},{3,15},{4,0},{5,1},{6,2},{7,3},{8,4},{9,5},{1... | collective-permute-start | bytes 1572872 | tf_op jit(solution)/shard_map/ppermute | solution.py:50
  92.7 16.0 %collective-permute-start.24 = (bf16[4,256,256]{2,1,0:T(8,128)(2,1)S(1)}, bf16[4,256,256]{2,1,0:T(8,128)(2,1)S(1)}, u32[]{:S(2)}, u32[]{:S(2)}) collective-permute-start(bf16[4,256,256]{2,1,0:T(8,128)(2,1)S(1)} %get-tuple-element.47), channel_id=1, source_target_pairs={{0,4},{1,5},{2,6},{3,7},{4,8},{5,9},{6,10},{7,11},{8,12},{9,13},{1... | collective-permute-start | bytes 1572872 | tf_op jit(solution)/shard_map/ppermute | solution.py:50
  93.0 16.7 %collective-permute-start.32 = (bf16[4,256,256]{2,1,0:T(8,128)(2,1)S(1)}, bf16[4,256,256]{2,1,0:T(8,128)(2,1)S(1)}, u32[]{:S(2)}, u32[]{:S(2)}) collective-permute-start(bf16[4,256,256]{2,1,0:T(8,128)(2,1)S(1)} %get-tuple-element.58), channel_id=1, source_target_pairs={{0,3},{1,0},{2,1},{3,2},{4,7},{5,4},{6,5},{7,6},{8,11},{9,8},{10,9... | collective-permute-start | bytes 1572872 | tf_op jit(solution)/shard_map/ppermute | solution.py:50
  95.1 14.7 %collective-permute-start.33 = (bf16[4,256,256]{2,1,0:T(8,128)(2,1)S(1)}, bf16[4,256,256]{2,1,0:T(8,128)(2,1)S(1)}, u32[]{:S(2)}, u32[]{:S(2)}) collective-permute-start(bf16[4,256,256]{2,1,0:T(8,128)(2,1)S(1)} %get-tuple-element.59), channel_id=1, source_target_pairs={{0,1},{1,2},{2,3},{3,0},{4,5},{5,6},{6,7},{7,4},{8,9},{9,10},{10,1... | collective-permute-start | bytes 1572872 | tf_op jit(solution)/shard_map/ppermute | solution.py:50
  95.3 23.6 %collective-permute-start.21 = (bf16[4,256,256]{2,1,0:T(8,128)(2,1)S(1)}, bf16[4,256,256]{2,1,0:T(8,128)(2,1)S(1)}, u32[]{:S(2)}, u32[]{:S(2)}) collective-permute-start(bf16[4,256,256]{2,1,0:T(8,128)(2,1)S(1)} %add_convert_fusion.3), channel_id=1, source_target_pairs={{0,4},{1,5},{2,6},{3,7},{4,8},{5,9},{6,10},{7,11},{8,12},{9,13},{1... | collective-permute-start | bytes 1572872 | tf_op jit(solution)/shard_map/ppermute | solution.py:50
  105.0 15.2 %collective-permute-start.31 = (bf16[4,256,256]{2,1,0:T(8,128)(2,1)S(1)}, bf16[4,256,256]{2,1,0:T(8,128)(2,1)S(1)}, u32[]{:S(2)}, u32[]{:S(2)}) collective-permute-start(bf16[4,256,256]{2,1,0:T(8,128)(2,1)S(1)} %add_convert_fusion.1), channel_id=1, source_target_pairs={{0,1},{1,2},{2,3},{3,0},{4,5},{5,6},{6,7},{7,4},{8,9},{9,10},{10,1... | collective-permute-start | bytes 1572872 | tf_op jit(solution)/shard_map/ppermute | solution.py:50
  108.9 11.8 %collective-permute-start.25 = (bf16[4,256,256]{2,1,0:T(8,128)(2,1)S(1)}, bf16[4,256,256]{2,1,0:T(8,128)(2,1)S(1)}, u32[]{:S(2)}, u32[]{:S(2)}) collective-permute-start(bf16[4,256,256]{2,1,0:T(8,128)(2,1)S(1)} %add_convert_fusion.2), channel_id=1, source_target_pairs={{0,12},{1,13},{2,14},{3,15},{4,0},{5,1},{6,2},{7,3},{8,4},{9,5},{1... | collective-permute-start | bytes 1572872 | tf_op jit(solution)/shard_map/ppermute | solution.py:50
  109.9 17.0 %collective-permute-start.34 = (bf16[4,256,256]{2,1,0:T(8,128)(2,1)S(1)}, bf16[4,256,256]{2,1,0:T(8,128)(2,1)S(1)}, u32[]{:S(2)}, u32[]{:S(2)}) collective-permute-start(bf16[4,256,256]{2,1,0:T(8,128)(2,1)S(1)} %add_convert_fusion), channel_id=1, source_target_pairs={{0,3},{1,0},{2,1},{3,2},{4,7},{5,4},{6,5},{7,6},{8,11},{9,8},{10,9... | collective-permute-start | bytes 1572872 | tf_op jit(solution)/shard_map/ppermute | solution.py:50
  120.7 13.1 %copy-start.11 = (s32[4]{0:T(128)S(1)}, s32[4]{0:T(128)}, u32[]{:S(2)}) copy-start(s32[4]{0:T(128)} %param.14) | copy-start | bytes 52
  121.0 10.8 %collective-permute-start.26 = (bf16[2,256,256]{2,1,0:T(8,128)(2,1)S(1)}, bf16[2,256,256]{2,1,0:T(8,128)(2,1)S(1)}, u32[]{:S(2)}, u32[]{:S(2)}) collective-permute-start(bf16[2,256,256]{2,1,0:T(8,128)(2,1)S(1)} %pad_maximum_fusion.2), channel_id=1, source_target_pairs={{0,2},{1,3},{2,0},{3,1},{4,6},{5,7},{6,4},{7,5},{8,10},{9,11},{10,... | collective-permute-start | bytes 786440 | tf_op jit(solution)/shard_map/ppermute | solution.py:50
  121.2 14.0 %collective-permute-start.27 = (bf16[2,256,256]{2,1,0:T(8,128)(2,1)S(1)}, bf16[2,256,256]{2,1,0:T(8,128)(2,1)S(1)}, u32[]{:S(2)}, u32[]{:S(2)}) collective-permute-start(bf16[2,256,256]{2,1,0:T(8,128)(2,1)S(1)} %pad_maximum_fusion.3), channel_id=1, source_target_pairs={{0,1},{1,2},{2,3},{3,0},{4,5},{5,6},{6,7},{7,4},{8,9},{9,10},{10,1... | collective-permute-start | bytes 786440 | tf_op jit(solution)/shard_map/ppermute | solution.py:50
  123.1 12.1 %collective-permute-start.28 = (bf16[2,256,256]{2,1,0:T(8,128)(2,1)S(1)}, bf16[2,256,256]{2,1,0:T(8,128)(2,1)S(1)}, u32[]{:S(2)}, u32[]{:S(2)}) collective-permute-start(bf16[2,256,256]{2,1,0:T(8,128)(2,1)S(1)} %pad_maximum_fusion.4), channel_id=1, source_target_pairs={{0,3},{1,0},{2,1},{3,2},{4,7},{5,4},{6,5},{7,6},{8,11},{9,8},{10,9... | collective-permute-start | bytes 786440 | tf_op jit(solution)/shard_map/ppermute | solution.py:50
  127.1 8.8 %collective-permute-start.35 = (bf16[2,256,256]{2,1,0:T(8,128)(2,1)S(1)}, bf16[2,256,256]{2,1,0:T(8,128)(2,1)S(1)}, u32[]{:S(2)}, u32[]{:S(2)}) collective-permute-start(bf16[2,256,256]{2,1,0:T(8,128)(2,1)S(1)} %pad_maximum_fusion.5), channel_id=1, source_target_pairs={{0,8},{1,9},{2,10},{3,11},{4,12},{5,13},{6,14},{7,15},{8,0},{9,1},... | collective-permute-start | bytes 786440 | tf_op jit(solution)/shard_map/ppermute | solution.py:50
  127.5 11.1 %collective-permute-start.36 = (bf16[2,256,256]{2,1,0:T(8,128)(2,1)S(1)}, bf16[2,256,256]{2,1,0:T(8,128)(2,1)S(1)}, u32[]{:S(2)}, u32[]{:S(2)}) collective-permute-start(bf16[2,256,256]{2,1,0:T(8,128)(2,1)S(1)} %pad_maximum_fusion.6), channel_id=1, source_target_pairs={{0,4},{1,5},{2,6},{3,7},{4,8},{5,9},{6,10},{7,11},{8,12},{9,13},{1... | collective-permute-start | bytes 786440 | tf_op jit(solution)/shard_map/ppermute | solution.py:50
  131.8 7.2 %collective-permute-start.37 = (bf16[2,256,256]{2,1,0:T(8,128)(2,1)S(1)}, bf16[2,256,256]{2,1,0:T(8,128)(2,1)S(1)}, u32[]{:S(2)}, u32[]{:S(2)}) collective-permute-start(bf16[2,256,256]{2,1,0:T(8,128)(2,1)S(1)} %pad_maximum_fusion.7), channel_id=1, source_target_pairs={{0,12},{1,13},{2,14},{3,15},{4,0},{5,1},{6,2},{7,3},{8,4},{9,5},{1... | collective-permute-start | bytes 786440 | tf_op jit(solution)/shard_map/ppermute | solution.py:50

commit v6 on v5

--- a/solution.py
+++ b/solution.py
@@ -111,6 +111,32 @@
         puts[n].start()
     for put in puts:
         put.wait()
+
+
+def join_kernel(start, first, second, third, out, sem):
+    cols = pl.ds(start, out.shape[-1])
+    copies = [
+        pltpu.make_async_copy(block.at[:, :, cols], out.at[n], sem.at[n])
+        for n, block in enumerate((first, second, third))
+    ]
+    for copy in copies:
+        copy.start()
+    for copy in copies:
+        copy.wait()
+
+
+def join(blocks, start):
+    tiles, tile, _ = blocks[0].shape
+    return pl.pallas_call(
+        functools.partial(join_kernel, start),
+        out_shape=jax.ShapeDtypeStruct((len(blocks), tiles, tile, tile // 2), jnp.bfloat16),
+        in_specs=[pl.BlockSpec(memory_space=pl.ANY)] * 3,
+        out_specs=VMEM,
+        scratch_shapes=[pltpu.SemaphoreType.DMA((3,))],
+        compiler_params=pltpu.CompilerParams(vmem_limit_bytes=4 << 20),
+        cost_estimate=pl.CostEstimate(flops=1, bytes_accessed=1 << 19, transcendentals=0),
+        name="join",
+    )(*blocks)
 
 
 def left_parts(kernel, count, src, left, pieces):
@@ -296,23 +322,24 @@
     shard, cut = wavefunction[:, 0], tile // 2
     behind_x, behind_z = hop(shard, "x", 1), hop(shard, "z", 1)
     ahead_x, ahead_z = hop(shard, "x", -1), hop(shard, "z", -1)
+    behind_x, ahead_x = lax.optimization_barrier((behind_x, ahead_x))
+    behind_z, ahead_z = lax.optimization_barrier((behind_z, ahead_z))
     far_x, far_z = hop(behind_x, "x", 1), hop(behind_z, "z", 1)
 
     loc = lax.all_to_all(
         jnp.broadcast_to(right_loc[:, 0][None, None], (STATES, 1, tiles)), "col", 0, 0, tiled=True
     )
-    env_right, _ = lax.optimization_barrier((env_right, behind_x))
+    env_right, loc, _ = lax.optimization_barrier((env_right, loc, behind_x))
     lane = lax.broadcasted_iota(jnp.int32, (1, 1, tile), 2)
     right = jnp.swapaxes(env_right[0], 1, 2)
     right = jnp.where(lane < right_size[:, None, None], right, 0).astype(jnp.bfloat16)
-    right_behind, right_ahead = hop(right, "y", 1), hop(right, "y", -1)
-    right = [right, right_behind, hop(right_behind, "y", 1), right_ahead]
+    right = [right]
+    for _ in range(RING - 1):
+        right.append(hop(right[-1], "y"))
     right += [swap_cores(block) for block in right]
-    far_x, far_z, loc = lax.optimization_barrier((far_x, far_z, loc))
 
     axis_blocks = (shard, behind_x, far_x, ahead_x, behind_z, far_z, ahead_z)
-    corner_a = jnp.stack([block[:, :, :cut] for block in axis_blocks[1:4]])
-    corner_b = jnp.stack([block[:, :, cut:] for block in axis_blocks[4:]])
+    corner_a, corner_b = join(axis_blocks[1:4], 0), join(axis_blocks[4:], cut)
     behind_a, behind_b = hop(corner_a, "z", 1), hop(corner_b, "x", 1)
     ahead_a, ahead_b = hop(corner_a, "z", -1), hop(corner_b, "x", -1)
     part_axis = left_parts(axis_kernel, len(AXIS), src, left, axis_blocks)

time: 141 us -> 137 us (0.972)
  local copies, waits for them, and re-layouts: 7.94 us -> 3.45 us
  other arithmetic: 6.65 us -> 4.58 us
  Pallas kernels: 24.2 us -> 26.2 us
    another operation x6 -> x0, local copies, waits for them, and re-layouts: 4.24 us -> none  [the longest x3 2.69 us: per_device(): corner_b = jnp.stack([block[:, :, cut:] for block in axis_blocks[4:]])]
    ppermute x5, starting transfers between devices: 2.42 us -> 5.79 us  [swap_cores(): return lax.ppermute(value, 'row', [(r, r ^ 1) for r in range(RING * CORES)])]
    ppermute x33, starting transfers between devices: 45.9 us -> 42.8 us  [ring_send(): return lax.ppermute(value, ('row', 'col'), pairs)]
    another operation x2 -> x0, other arithmetic: 2.16 us -> none  [the longest x1 1.12 us: per_device(): corner_a = jnp.stack([block[:, :, :cut] for block in axis_blocks[1:4]])]
    pallas_call x0 -> x2, Pallas kernels: none -> 2.05 us  [join(): pl.pallas_call(functools.partial(join_kernel, start), out_shape=jax.Shape...]
  transfers between devices with their start and end apart: 39 -> 39, of which waited for: 16 -> 23; matrix products, arithmetic and copies ran while one was open for 9% -> 5% of each run, Pallas kernels for 12% -> 14%
where the time goes in v6:
time: 137 us
  starting transfers between devices  53.3 us (39%)
  waiting for transfers between devices  49.1 us (36%)
  Pallas kernels  26.2 us (19%)
  other arithmetic  4.58 us (3%)
  local copies, waits for them, and re-layouts  3.45 us (3%)
    ppermute x33, waiting for transfers between devices, ring_send(): return lax.ppermute(value, ('row', 'col'), pairs)  47.3 us
    ppermute x33, starting transfers between devices, ring_send(): return lax.ppermute(value, ('row', 'col'), pairs)  42.8 us
    pallas_call x2, Pallas kernels, apply_terms(): pl.pallas_call(functools.partial(apply_kernel, chosen), out_shape=[out] *...  13.9 us
    pallas_call x2, Pallas kernels, left_parts(): pl.pallas_call(kernel, out_shape=pltpu.HBM(out, jnp.bfloat16), in_specs=[...  10.3 us
    ppermute x5, starting transfers between devices, swap_cores(): return lax.ppermute(value, 'row', [(r, r ^ 1) for r in range(RING * CORES)])  5.79 us
    all_to_all x1, starting transfers between devices, per_device(): lax.all_to_all(jnp.broadcast_to(right_loc[:, 0][None, None], (STATES, 1,...  4.65 us
  transfers between devices with their start and end apart: 39, of which 23 were waited for; matrix products, arithmetic and copies ran while one was open for 5% of the time, Pallas kernels for 14%

profile of v6, /device:TPU:0, one launch (start us, length us, event | category | flops | bytes accessed | tf_op | source)
XLA Modules:
  0.0 137.0 jit_solution(5358613272653270752)
XLA Ops:
  0.0 1.6 %collective-permute-start = (bf16[4,256,256]{2,1,0:T(8,128)(2,1)}, bf16[4,256,256]{2,1,0:T(8,128)(2,1)S(1)}, u32[]{:S(2)}, u32[]{:S(2)}) collective-permute-start(bf16[4,256,256]{2,1,0:T(8,128)(2,1)} %bitcast.20), channel_id=1, source_target_pairs={{0,1},{1,2},{2,3},{3,0},{4,5},{5,6},{6,7},{7,4},{8,9},{9,10},{10,1... | collective-permute-start | bytes 1572872 | tf_op jit(solution)/shard_map/ppermute | solution.py:50
  1.6 1.7 %collective-permute-start.1 = (bf16[4,256,256]{2,1,0:T(8,128)(2,1)}, bf16[4,256,256]{2,1,0:T(8,128)(2,1)S(1)}, u32[]{:S(2)}, u32[]{:S(2)}) collective-permute-start(bf16[4,256,256]{2,1,0:T(8,128)(2,1)} %bitcast.21), channel_id=1, source_target_pairs={{0,3},{1,0},{2,1},{3,2},{4,7},{5,4},{6,5},{7,6},{8,11},{9,8},{10,9... | collective-permute-start | bytes 1572872 | tf_op jit(solution)/shard_map/ppermute | solution.py:50
  3.2 2.0 %collective-permute-start.13 = (bf16[4,256,256]{2,1,0:T(8,128)(2,1)}, bf16[4,256,256]{2,1,0:T(8,128)(2,1)S(1)}, u32[]{:S(2)}, u32[]{:S(2)}) collective-permute-start(bf16[4,256,256]{2,1,0:T(8,128)(2,1)} %bitcast.22), channel_id=1, source_target_pairs={{0,4},{1,5},{2,6},{3,7},{4,8},{5,9},{6,10},{7,11},{8,12},{9,13},{1... | collective-permute-start | bytes 1572872 | tf_op jit(solution)/shard_map/ppermute | solution.py:50
  5.2 2.1 %collective-permute-start.14 = (bf16[4,256,256]{2,1,0:T(8,128)(2,1)}, bf16[4,256,256]{2,1,0:T(8,128)(2,1)S(1)}, u32[]{:S(2)}, u32[]{:S(2)}) collective-permute-start(bf16[4,256,256]{2,1,0:T(8,128)(2,1)} %bitcast.23), channel_id=1, source_target_pairs={{0,12},{1,13},{2,14},{3,15},{4,0},{5,1},{6,2},{7,3},{8,4},{9,5},{1... | collective-permute-start | bytes 1572872 | tf_op jit(solution)/shard_map/ppermute | solution.py:50
  7.4 1.3 broadcast_in_dim.39
  8.6 4.7 %all-to-all-start = ((s32[16,1,4]{2,1,0:T(1,128)}), s32[16,1,4]{2,1,0:T(1,128)S(1)}, u32[]{:S(2)}, u32[]{:S(2)}) async-start(s32[16,1,4]{2,1,0:T(1,128)} %broadcast_in_dim.39), calls=%async_computation | async-start | bytes 16384 | tf_op jit(solution)/shard_map/all_to_all | solution.py:329
  13.3 0.7 iota_compare_fusion
  14.0 0.7 collective-permute-done.first.refs_1_
  14.7 1.7 %collective-permute-start.9 = (bf16[4,256,256]{2,1,0:T(8,128)(2,1)S(1)}, bf16[4,256,256]{2,1,0:T(8,128)(2,1)}, u32[]{:S(2)}, u32[]{:S(2)}) collective-permute-start(bf16[4,256,256]{2,1,0:T(8,128)(2,1)S(1)} %collective-permute-done.first.refs_1_), channel_id=1, source_target_pairs={{0,1},{1,2},{2,3},{3,0},{4,5},{5,6},{6,7},{7,4},{8,9},{9,10},{10,1... | collective-permute-start | bytes 1572872 | tf_op jit(solution)/shard_map/ppermute | solution.py:50
  16.5 2.9 %collective-permute-done.13.first.refs_4_ = bf16[4,256,256]{2,1,0:T(8,128)(2,1)S(1)} collective-permute-done((bf16[4,256,256]{2,1,0:T(8,128)(2,1)}, bf16[4,256,256]{2,1,0:T(8,128)(2,1)S(1)}, u32[]{:S(2)}, u32[]{:S(2)}) %collective-permute-start.13) | collective-permute-done | bytes 524320 | tf_op jit(solution)/shard_map/ppermute | solution.py:50
  19.4 0.7 collective-permute-start.15
  20.1 0.6 all-to-all-done.loc_ref
  20.8 2.0 %copy.9 = bf16[1,4,256,256]{2,3,1,0:T(8,128)(2,1)} copy(bf16[1,4,256,256]{3,2,1,0:T(8,128)(2,1)} %param.12) | data formatting | bytes 1048576 | tf_op jit(solution)/shard_map/optimization_barrier | solution.py:332
  22.8 1.1 fusion.1.refs_0_
  23.9 1.6 %collective-permute-start.2 = (bf16[4,256,256]{2,1,0:T(8,128)(2,1)S(1)}, bf16[4,256,256]{2,1,0:T(8,128)(2,1)}, u32[]{:S(2)}, u32[]{:S(2)}) collective-permute-start(bf16[4,256,256]{2,1,0:T(8,128)(2,1)S(1)} %fusion.1.refs_0_), channel_id=1, source_target_pairs={{0,32},{1,33},{2,34},{3,35},{4,36},{5,37},{6,38},{7,39},{8,40},{9,... | collective-permute-start | bytes 1572872 | tf_op jit(solution)/shard_map/ppermute | solution.py:50
  25.5 1.3 collective-permute-start.5
  26.8 1.0 join.2
  27.8 1.6 %collective-permute-start.10 = (bf16[3,4,256,128]{3,2,1,0:T(8,128)(2,1)S(1)}, bf16[3,4,256,128]{3,2,1,0:T(8,128)(2,1)}, u32[]{:S(2)}, u32[]{:S(2)}) collective-permute-start(bf16[3,4,256,128]{3,2,1,0:T(8,128)(2,1)S(1)} %join.2), channel_id=1, source_target_pairs={{0,4},{1,5},{2,6},{3,7},{4,8},{5,9},{6,10},{7,11},{8,12},{9,13},{1... | collective-permute-start | bytes 2359304 | tf_op jit(solution)/shard_map/ppermute | solution.py:50
  29.5 0.5 collective-permute-done.15.second.refs_5_
  29.9 1.0 join.3
  31.1 3.4 %collective-permute-done.2.refs_1_ = bf16[4,256,256]{2,1,0:T(8,128)(2,1)} collective-permute-done((bf16[4,256,256]{2,1,0:T(8,128)(2,1)S(1)}, bf16[4,256,256]{2,1,0:T(8,128)(2,1)}, u32[]{:S(2)}, u32[]{:S(2)}) %collective-permute-start.2) | collective-permute-done | bytes 524320 | tf_op jit(solution)/shard_map/ppermute | solution.py:50
  34.5 0.4 collective-permute-start.3
  34.8 1.9 %collective-permute-start.11 = (bf16[3,4,256,128]{3,2,1,0:T(8,128)(2,1)S(1)}, bf16[3,4,256,128]{3,2,1,0:T(8,128)(2,1)S(1)}, u32[]{:S(2)}, u32[]{:S(2)}) collective-permute-start(bf16[3,4,256,128]{3,2,1,0:T(8,128)(2,1)S(1)} %join.2), channel_id=1, source_target_pairs={{0,12},{1,13},{2,14},{3,15},{4,0},{5,1},{6,2},{7,3},{8,4},{9,5},{1... | collective-permute-start | bytes 2359304 | tf_op jit(solution)/shard_map/ppermute | solution.py:50
  36.8 2.2 %collective-permute-start.17 = (bf16[3,4,256,128]{3,2,1,0:T(8,128)(2,1)S(1)}, bf16[3,4,256,128]{3,2,1,0:T(8,128)(2,1)S(1)}, u32[]{:S(2)}, u32[]{:S(2)}) collective-permute-start(bf16[3,4,256,128]{3,2,1,0:T(8,128)(2,1)S(1)} %join.3), channel_id=1, source_target_pairs={{0,3},{1,0},{2,1},{3,2},{4,7},{5,4},{6,5},{7,6},{8,11},{9,8},{10,9... | collective-permute-start | bytes 2359304 | tf_op jit(solution)/shard_map/ppermute | solution.py:50
  39.0 6.2 %collective-permute-done.3.refs_2_ = bf16[4,256,256]{2,1,0:T(8,128)(2,1)} collective-permute-done((bf16[4,256,256]{2,1,0:T(8,128)(2,1)}, bf16[4,256,256]{2,1,0:T(8,128)(2,1)}, u32[]{:S(2)}, u32[]{:S(2)}) %collective-permute-start.3) | collective-permute-done | bytes 524320 | tf_op jit(solution)/shard_map/ppermute | solution.py:50
  45.2 0.6 collective-permute-start.12
  45.8 1.5 %collective-permute-done.16.refs_2_.refs_11_ = bf16[3,4,256,128]{3,2,1,0:T(8,128)(2,1)} collective-permute-done((bf16[3,4,256,128]{3,2,1,0:T(8,128)(2,1)S(1)}, bf16[3,4,256,128]{3,2,1,0:T(8,128)(2,1)}, u32[]{:S(2)}, u32[]{:S(2)}) %collective-permute-start.16) | collective-permute-done | bytes 786464 | tf_op jit(solution)/shard_map/ppermute | solution.py:50
  47.4 2.0 %collective-permute-start.6 = (bf16[4,256,256]{2,1,0:T(8,128)(2,1)}, bf16[4,256,256]{2,1,0:T(8,128)(2,1)}, u32[]{:S(2)}, u32[]{:S(2)}) collective-permute-start(bf16[4,256,256]{2,1,0:T(8,128)(2,1)} %collective-permute-done.2.refs_1_), channel_id=1, source_target_pairs={{0,16},{16,0},{32,48},{48,32},{64,80},{80,64},{96,112},{112,96},{1... | collective-permute-start | bytes 1572872 | tf_op jit(solution)/shard_map/ppermute | solution.py:54
  49.4 1.3 collective-permute-done.17.refs_3_.refs_12_
  50.7 2.5 %collective-permute-start.7 = (bf16[4,256,256]{2,1,0:T(8,128)(2,1)}, bf16[4,256,256]{2,1,0:T(8,128)(2,1)}, u32[]{:S(2)}, u32[]{:S(2)}) collective-permute-start(bf16[4,256,256]{2,1,0:T(8,128)(2,1)} %collective-permute-done.3.refs_2_), channel_id=1, source_target_pairs={{0,16},{16,0},{32,48},{48,32},{64,80},{80,64},{96,112},{112,96},{1... | collective-permute-start | bytes 1572872 | tf_op jit(solution)/shard_map/ppermute | solution.py:54
  53.2 2.7 %collective-permute-done.4.refs_3_ = bf16[4,256,256]{2,1,0:T(8,128)(2,1)} collective-permute-done((bf16[4,256,256]{2,1,0:T(8,128)(2,1)}, bf16[4,256,256]{2,1,0:T(8,128)(2,1)}, u32[]{:S(2)}, u32[]{:S(2)}) %collective-permute-start.4) | collective-permute-done | bytes 524320 | tf_op jit(solution)/shard_map/ppermute | solution.py:50
  56.0 5.7 %left_parts.2.refs_14_ = bf16[7,4,256,256]{3,2,1,0:T(8,128)(2,1)} custom-call(s32[4,2]{1,0:T(4,128)S(1)} %copy.12.src_ref, bf16[4,2,256,256]{3,2,1,0:T(8,128)(2,1)S(1)} %bitcast.16, bf16[4,256,256]{2,1,0:T(8,128)(2,1)} %bitcast.24, bf16[4,256,256]{2,1,0:T(8,128)(2,1)} %copy-done.1, bf16[4,256,256]{2,1,0:T(8,128)(2,1)} %collective-permute-done.9.second.refs_2_, ...), custom_call_target="tpu_custom_call" | custom-call | flops 1879048192 | bytes 5242880 | tf_op jit(solution)/shard_map/left_parts/pallas_call | solution.py:145
  61.8 4.6 %left_parts.3.refs_15_ = bf16[4,4,256,256]{3,2,1,0:T(8,128)(2,1)} custom-call(s32[4,2]{1,0:T(4,128)S(1)} %copy.12.src_ref, bf16[4,2,256,256]{3,2,1,0:T(8,128)(2,1)S(1)} %bitcast.17, bf16[3,4,256,128]{3,2,1,0:T(8,128)(2,1)} %collective-permute-done.10.refs_0_.refs_8_, bf16[3,4,256,128]{3,2,1,0:T(8,128)(2,1)} %copy-done.6, ...), custom_call_target="tpu_custom_call" | custom-call | flops 1073741824 | bytes 5242880 | tf_op jit(solution)/shard_map/left_parts/pallas_call | solution.py:145
  66.5 6.9 %apply_terms.2 = (bf16[4,256,256]{2,1,0:T(8,128)(2,1)S(1)}, bf16[4,256,256]{2,1,0:T(8,128)(2,1)S(1)}, bf16[4,256,256]{2,1,0:T(8,128)(2,1)S(1)}, bf16[4,256,256]{...) custom-call(s32[4,2]{1,0:T(4,128)S(1)} %copy.12.src_ref, ...), custom_call_target="tpu_custom_call" | custom-call | flops 2684354560 | bytes 8388608 | tf_op jit(solution)/shard_map/apply_terms/pallas_call | solution.py:277
  73.3 0.6 collective-permute-start.19
  74.0 2.7 %collective-permute-start.20 = (bf16[4,256,256]{2,1,0:T(8,128)(2,1)S(1)}, bf16[4,256,256]{2,1,0:T(8,128)(2,1)S(1)}, u32[]{:S(2)}, u32[]{:S(2)}) collective-permute-start(bf16[4,256,256]{2,1,0:T(8,128)(2,1)S(1)} %get-tuple-element.44), channel_id=1, source_target_pairs={{0,12},{1,13},{2,14},{3,15},{4,0},{5,1},{6,2},{7,3},{8,4},{9,5},{1... | collective-permute-start | bytes 1572872 | tf_op jit(solution)/shard_map/ppermute | solution.py:50
  76.6 0.6 collective-permute-start.29
  77.2 2.7 %collective-permute-start.30 = (bf16[4,256,256]{2,1,0:T(8,128)(2,1)S(1)}, bf16[4,256,256]{2,1,0:T(8,128)(2,1)S(1)}, u32[]{:S(2)}, u32[]{:S(2)}) collective-permute-start(bf16[4,256,256]{2,1,0:T(8,128)(2,1)S(1)} %get-tuple-element.57), channel_id=1, source_target_pairs={{0,3},{1,0},{2,1},{3,2},{4,7},{5,4},{6,5},{7,6},{8,11},{9,8},{10,9... | collective-permute-start | bytes 1572872 | tf_op jit(solution)/shard_map/ppermute | solution.py:50
  79.9 1.2 collective-permute-done.22.token_ref
  81.1 7.0 %apply_terms.3 = (bf16[4,256,256]{2,1,0:T(8,128)(2,1)S(1)}, bf16[4,256,256]{2,1,0:T(8,128)(2,1)S(1)}, bf16[4,256,256]{2,1,0:T(8,128)(2,1)S(1)}, bf16[4,256,256]{...) custom-call(s32[4,2]{1,0:T(4,128)S(1)} %copy.12.src_ref, ...), custom_call_target="tpu_custom_call" | custom-call | flops 2684354560 | bytes 8388608 | tf_op jit(solution)/shard_map/apply_terms/pallas_call | solution.py:277
  88.1 0.8 collective-permute-start.23
  88.9 1.2 collective-permute-start.24
  90.2 1.1 collective-permute-start.32
  91.4 0.2 collective-permute-done.29
  91.6 0.8 collective-permute-start.33
  92.4 1.5 %collective-permute-start.21 = (bf16[4,256,256]{2,1,0:T(8,128)(2,1)S(1)}, bf16[4,256,256]{2,1,0:T(8,128)(2,1)S(1)}, u32[]{:S(2)}, u32[]{:S(2)}) collective-permute-start(bf16[4,256,256]{2,1,0:T(8,128)(2,1)S(1)} %add_convert_fusion.3), channel_id=1, source_target_pairs={{0,4},{1,5},{2,6},{3,7},{4,8},{5,9},{6,10},{7,11},{8,12},{9,13},{1... | collective-permute-start | bytes 1572872 | tf_op jit(solution)/shard_map/ppermute | solution.py:50
  94.0 8.1 %collective-permute-done.23 = bf16[4,256,256]{2,1,0:T(8,128)(2,1)S(1)} collective-permute-done((bf16[4,256,256]{2,1,0:T(8,128)(2,1)S(1)}, bf16[4,256,256]{2,1,0:T(8,128)(2,1)S(1)}, u32[]{:S(2)}, u32[]{:S(2)}) %collective-permute-start.23) | collective-permute-done | bytes 524320 | tf_op jit(solution)/shard_map/ppermute | solution.py:50
  102.1 2.8 %collective-permute-done.24 = bf16[4,256,256]{2,1,0:T(8,128)(2,1)S(1)} collective-permute-done((bf16[4,256,256]{2,1,0:T(8,128)(2,1)S(1)}, bf16[4,256,256]{2,1,0:T(8,128)(2,1)S(1)}, u32[]{:S(2)}, u32[]{:S(2)}) %collective-permute-start.24) | collective-permute-done | bytes 524320 | tf_op jit(solution)/shard_map/ppermute | solution.py:50
  105.2 1.3 collective-permute-done.33
  106.7 1.0 collective-permute-start.34
  107.7 7.3 %collective-permute-done.21 = bf16[4,256,256]{2,1,0:T(8,128)(2,1)S(1)} collective-permute-done((bf16[4,256,256]{2,1,0:T(8,128)(2,1)S(1)}, bf16[4,256,256]{2,1,0:T(8,128)(2,1)S(1)}, u32[]{:S(2)}, u32[]{:S(2)}) %collective-permute-start.21) | collective-permute-done | bytes 524320 | tf_op jit(solution)/shard_map/ppermute | solution.py:50
  115.2 2.0 %collective-permute-done.31 = bf16[4,256,256]{2,1,0:T(8,128)(2,1)S(1)} collective-permute-done((bf16[4,256,256]{2,1,0:T(8,128)(2,1)S(1)}, bf16[4,256,256]{2,1,0:T(8,128)(2,1)S(1)}, u32[]{:S(2)}, u32[]{:S(2)}) %collective-permute-start.31) | collective-permute-done | bytes 524320 | tf_op jit(solution)/shard_map/ppermute | solution.py:50
  117.6 0.6 collective-permute-start.26
  118.2 1.9 %collective-permute-start.27 = (bf16[2,256,256]{2,1,0:T(8,128)(2,1)S(1)}, bf16[2,256,256]{2,1,0:T(8,128)(2,1)S(1)}, u32[]{:S(2)}, u32[]{:S(2)}) collective-permute-start(bf16[2,256,256]{2,1,0:T(8,128)(2,1)S(1)} %pad_maximum_fusion.1), channel_id=1, source_target_pairs={{0,1},{1,2},{2,3},{3,0},{4,5},{5,6},{6,7},{7,4},{8,9},{9,10},{10,1... | collective-permute-start | bytes 786440 | tf_op jit(solution)/shard_map/ppermute | solution.py:50
  120.1 1.5 %collective-permute-start.28 = (bf16[2,256,256]{2,1,0:T(8,128)(2,1)S(1)}, bf16[2,256,256]{2,1,0:T(8,128)(2,1)S(1)}, u32[]{:S(2)}, u32[]{:S(2)}) collective-permute-start(bf16[2,256,256]{2,1,0:T(8,128)(2,1)S(1)} %pad_maximum_fusion.2), channel_id=1, source_target_pairs={{0,3},{1,0},{2,1},{3,2},{4,7},{5,4},{6,5},{7,6},{8,11},{9,8},{10,9... | collective-permute-start | bytes 786440 | tf_op jit(solution)/shard_map/ppermute | solution.py:50
  121.9 2.2 %collective-permute-start.35 = (bf16[2,256,256]{2,1,0:T(8,128)(2,1)S(1)}, bf16[2,256,256]{2,1,0:T(8,128)(2,1)S(1)}, u32[]{:S(2)}, u32[]{:S(2)}) collective-permute-start(bf16[2,256,256]{2,1,0:T(8,128)(2,1)S(1)} %pad_maximum_fusion.3), channel_id=1, source_target_pairs={{0,8},{1,9},{2,10},{3,11},{4,12},{5,13},{6,14},{7,15},{8,0},{9,1},... | collective-permute-start | bytes 786440 | tf_op jit(solution)/shard_map/ppermute | solution.py:50
  124.1 2.4 %collective-permute-start.36 = (bf16[2,256,256]{2,1,0:T(8,128)(2,1)S(1)}, bf16[2,256,256]{2,1,0:T(8,128)(2,1)S(1)}, u32[]{:S(2)}, u32[]{:S(2)}) collective-permute-start(bf16[2,256,256]{2,1,0:T(8,128)(2,1)S(1)} %pad_maximum_fusion.4), channel_id=1, source_target_pairs={{0,4},{1,5},{2,6},{3,7},{4,8},{5,9},{6,10},{7,11},{8,12},{9,13},{1... | collective-permute-start | bytes 786440 | tf_op jit(solution)/shard_map/ppermute | solution.py:50
  126.6 1.9 %collective-permute-done.26 = bf16[2,256,256]{2,1,0:T(8,128)(2,1)S(1)} collective-permute-done((bf16[2,256,256]{2,1,0:T(8,128)(2,1)S(1)}, bf16[2,256,256]{2,1,0:T(8,128)(2,1)S(1)}, u32[]{:S(2)}, u32[]{:S(2)}) %collective-permute-start.26) | collective-permute-done | bytes 262176 | tf_op jit(solution)/shard_map/ppermute | solution.py:50
  128.5 3.0 %collective-permute-start.37 = (bf16[2,256,256]{2,1,0:T(8,128)(2,1)S(1)}, bf16[2,256,256]{2,1,0:T(8,128)(2,1)S(1)}, u32[]{:S(2)}, u32[]{:S(2)}) collective-permute-start(bf16[2,256,256]{2,1,0:T(8,128)(2,1)S(1)} %pad_maximum_fusion.5), channel_id=1, source_target_pairs={{0,12},{1,13},{2,14},{3,15},{4,0},{5,1},{6,2},{7,3},{8,4},{9,5},{1... | collective-permute-start | bytes 786440 | tf_op jit(solution)/shard_map/ppermute | solution.py:50
  131.5 0.5 collective-permute-done.27
  132.1 0.5 collective-permute-done.35
  132.5 2.8 %collective-permute-done.36 = bf16[2,256,256]{2,1,0:T(8,128)(2,1)S(1)} collective-permute-done((bf16[2,256,256]{2,1,0:T(8,128)(2,1)S(1)}, bf16[2,256,256]{2,1,0:T(8,128)(2,1)S(1)}, u32[]{:S(2)}, u32[]{:S(2)}) %collective-permute-start.36) | collective-permute-done | bytes 262176 | tf_op jit(solution)/shard_map/ppermute | solution.py:50
  135.3 0.5 collective-permute-done.37
  136.0 1.0 fusion
  (68 shorter events, 2.3 us)
Async XLA Ops:
  0.0 55.9 %copy-start.10 = (s32[1,4,2]{1,2,0:T(2,128)S(1)}, s32[1,4,2]{1,2,0:T(2,128)}, u32[]{:S(2)}) copy-start(s32[1,4,2]{1,2,0:T(2,128)} %param.10) | copy-start | bytes 100
  0.0 56.0 %copy-start = (bf16[1,4,2,256,256]{4,3,2,1,0:T(8,128)(2,1)S(1)}, bf16[1,4,2,256,256]{4,3,2,1,0:T(8,128)(2,1)}, u32[]{:S(2)}) copy-start(bf16[1,4,2,256,256]{4,3,2,1,0:T(8,128)(2,1)} %param.9) | copy-start | bytes 3145732
  0.0 14.7 %collective-permute-start = (bf16[4,256,256]{2,1,0:T(8,128)(2,1)}, bf16[4,256,256]{2,1,0:T(8,128)(2,1)S(1)}, u32[]{:S(2)}, u32[]{:S(2)}) collective-permute-start(bf16[4,256,256]{2,1,0:T(8,128)(2,1)} %bitcast.20), channel_id=1, source_target_pairs={{0,1},{1,2},{2,3},{3,0},{4,5},{5,6},{6,7},{7,4},{8,9},{9,10},{10,1... | collective-permute-start | bytes 1572872 | tf_op jit(solution)/shard_map/ppermute | solution.py:50
  1.6 13.2 %collective-permute-start.1 = (bf16[4,256,256]{2,1,0:T(8,128)(2,1)}, bf16[4,256,256]{2,1,0:T(8,128)(2,1)S(1)}, u32[]{:S(2)}, u32[]{:S(2)}) collective-permute-start(bf16[4,256,256]{2,1,0:T(8,128)(2,1)} %bitcast.21), channel_id=1, source_target_pairs={{0,3},{1,0},{2,1},{3,2},{4,7},{5,4},{6,5},{7,6},{8,11},{9,8},{10,9... | collective-permute-start | bytes 1572872 | tf_op jit(solution)/shard_map/ppermute | solution.py:50
  3.2 16.1 %collective-permute-start.13 = (bf16[4,256,256]{2,1,0:T(8,128)(2,1)}, bf16[4,256,256]{2,1,0:T(8,128)(2,1)S(1)}, u32[]{:S(2)}, u32[]{:S(2)}) collective-permute-start(bf16[4,256,256]{2,1,0:T(8,128)(2,1)} %bitcast.22), channel_id=1, source_target_pairs={{0,4},{1,5},{2,6},{3,7},{4,8},{5,9},{6,10},{7,11},{8,12},{9,13},{1... | collective-permute-start | bytes 1572872 | tf_op jit(solution)/shard_map/ppermute | solution.py:50
  5.2 14.1 %collective-permute-start.14 = (bf16[4,256,256]{2,1,0:T(8,128)(2,1)}, bf16[4,256,256]{2,1,0:T(8,128)(2,1)S(1)}, u32[]{:S(2)}, u32[]{:S(2)}) collective-permute-start(bf16[4,256,256]{2,1,0:T(8,128)(2,1)} %bitcast.23), channel_id=1, source_target_pairs={{0,12},{1,13},{2,14},{3,15},{4,0},{5,1},{6,2},{7,3},{8,4},{9,5},{1... | collective-permute-start | bytes 1572872 | tf_op jit(solution)/shard_map/ppermute | solution.py:50
  8.6 12.1 %all-to-all-start = ((s32[16,1,4]{2,1,0:T(1,128)}), s32[16,1,4]{2,1,0:T(1,128)S(1)}, u32[]{:S(2)}, u32[]{:S(2)}) async-start(s32[16,1,4]{2,1,0:T(1,128)} %broadcast_in_dim.39), calls=%async_computation | async-start | bytes 16384 | tf_op jit(solution)/shard_map/all_to_all | solution.py:329
  14.7 41.3 %copy-start.1 = (bf16[4,256,256]{2,1,0:T(8,128)(2,1)}, bf16[4,256,256]{2,1,0:T(8,128)(2,1)S(1)}, u32[]{:S(2)}) copy-start(bf16[4,256,256]{2,1,0:T(8,128)(2,1)S(1)} %collective-permute-done.first.refs_1_) | copy-start | bytes 1572868
  14.7 41.3 %copy-start.2 = (bf16[4,256,256]{2,1,0:T(8,128)(2,1)}, bf16[4,256,256]{2,1,0:T(8,128)(2,1)S(1)}, u32[]{:S(2)}) copy-start(bf16[4,256,256]{2,1,0:T(8,128)(2,1)S(1)} %collective-permute-done.1.third.refs_3_) | copy-start | bytes 1572868
  14.7 12.1 %collective-permute-start.9 = (bf16[4,256,256]{2,1,0:T(8,128)(2,1)S(1)}, bf16[4,256,256]{2,1,0:T(8,128)(2,1)}, u32[]{:S(2)}, u32[]{:S(2)}) collective-permute-start(bf16[4,256,256]{2,1,0:T(8,128)(2,1)S(1)} %collective-permute-done.first.refs_1_), channel_id=1, source_target_pairs={{0,1},{1,2},{2,3},{3,0},{4,5},{5,6},{6,7},{7,4},{8,9},{9,10},{10,1... | collective-permute-start | bytes 1572872 | tf_op jit(solution)/shard_map/ppermute | solution.py:50
  19.4 36.6 %copy-start.3 = (bf16[4,256,256]{2,1,0:T(8,128)(2,1)}, bf16[4,256,256]{2,1,0:T(8,128)(2,1)S(1)}, u32[]{:S(2)}) copy-start(bf16[4,256,256]{2,1,0:T(8,128)(2,1)S(1)} %collective-permute-done.13.first.refs_4_) | copy-start | bytes 1572868
  19.4 36.6 %copy-start.4 = (bf16[4,256,256]{2,1,0:T(8,128)(2,1)}, bf16[4,256,256]{2,1,0:T(8,128)(2,1)S(1)}, u32[]{:S(2)}) copy-start(bf16[4,256,256]{2,1,0:T(8,128)(2,1)S(1)} %collective-permute-done.14.third.refs_6_) | copy-start | bytes 1572868
  19.4 10.6 %collective-permute-start.15 = (bf16[4,256,256]{2,1,0:T(8,128)(2,1)S(1)}, bf16[4,256,256]{2,1,0:T(8,128)(2,1)}, u32[]{:S(2)}, u32[]{:S(2)}) collective-permute-start(bf16[4,256,256]{2,1,0:T(8,128)(2,1)S(1)} %collective-permute-done.13.first.refs_4_), channel_id=1, source_target_pairs={{0,4},{1,5},{2,6},{3,7},{4,8},{5,9},{6,10},{7,11},{8,12},{9,13},{1... | collective-permute-start | bytes 1572872 | tf_op jit(solution)/shard_map/ppermute | solution.py:50
  23.9 32.0 %copy-start.8 = (bf16[4,256,256]{2,1,0:T(8,128)(2,1)}, bf16[4,256,256]{2,1,0:T(8,128)(2,1)S(1)}, u32[]{:S(2)}) copy-start(bf16[4,256,256]{2,1,0:T(8,128)(2,1)S(1)} %fusion.1.refs_0_) | copy-start | bytes 1572868
  23.9 10.6 %collective-permute-start.2 = (bf16[4,256,256]{2,1,0:T(8,128)(2,1)S(1)}, bf16[4,256,256]{2,1,0:T(8,128)(2,1)}, u32[]{:S(2)}, u32[]{:S(2)}) collective-permute-start(bf16[4,256,256]{2,1,0:T(8,128)(2,1)S(1)} %fusion.1.refs_0_), channel_id=1, source_target_pairs={{0,32},{1,33},{2,34},{3,35},{4,36},{5,37},{6,38},{7,39},{8,40},{9,... | collective-permute-start | bytes 1572872 | tf_op jit(solution)/shard_map/ppermute | solution.py:50
  25.5 11.2 %collective-permute-start.5 = (bf16[4,256,256]{2,1,0:T(8,128)(2,1)S(1)}, bf16[4,256,256]{2,1,0:T(8,128)(2,1)S(1)}, u32[]{:S(2)}, u32[]{:S(2)}) collective-permute-start(bf16[4,256,256]{2,1,0:T(8,128)(2,1)S(1)} %fusion.1.refs_0_), channel_id=1, source_target_pairs={{0,16},{16,0},{32,48},{48,32},{64,80},{80,64},{96,112},{112,96},{1... | collective-permute-start | bytes 1572872 | tf_op jit(solution)/shard_map/ppermute | solution.py:54
  27.8 17.3 %collective-permute-start.10 = (bf16[3,4,256,128]{3,2,1,0:T(8,128)(2,1)S(1)}, bf16[3,4,256,128]{3,2,1,0:T(8,128)(2,1)}, u32[]{:S(2)}, u32[]{:S(2)}) collective-permute-start(bf16[3,4,256,128]{3,2,1,0:T(8,128)(2,1)S(1)} %join.2), channel_id=1, source_target_pairs={{0,4},{1,5},{2,6},{3,7},{4,8},{5,9},{6,10},{7,11},{8,12},{9,13},{1... | collective-permute-start | bytes 2359304 | tf_op jit(solution)/shard_map/ppermute | solution.py:50
  31.0 16.3 %collective-permute-start.16 = (bf16[3,4,256,128]{3,2,1,0:T(8,128)(2,1)S(1)}, bf16[3,4,256,128]{3,2,1,0:T(8,128)(2,1)}, u32[]{:S(2)}, u32[]{:S(2)}) collective-permute-start(bf16[3,4,256,128]{3,2,1,0:T(8,128)(2,1)S(1)} %join.3), channel_id=1, source_target_pairs={{0,1},{1,2},{2,3},{3,0},{4,5},{5,6},{6,7},{7,4},{8,9},{9,10},{10,1... | collective-permute-start | bytes 2359304 | tf_op jit(solution)/shard_map/ppermute | solution.py:50
  34.5 10.7 %collective-permute-start.3 = (bf16[4,256,256]{2,1,0:T(8,128)(2,1)}, bf16[4,256,256]{2,1,0:T(8,128)(2,1)}, u32[]{:S(2)}, u32[]{:S(2)}) collective-permute-start(bf16[4,256,256]{2,1,0:T(8,128)(2,1)} %collective-permute-done.2.refs_1_), channel_id=1, source_target_pairs={{0,32},{1,33},{2,34},{3,35},{4,36},{5,37},{6,38},{7,39},{8,40},{9,... | collective-permute-start | bytes 1572872 | tf_op jit(solution)/shard_map/ppermute | solution.py:50
  34.8 12.5 %collective-permute-start.11 = (bf16[3,4,256,128]{3,2,1,0:T(8,128)(2,1)S(1)}, bf16[3,4,256,128]{3,2,1,0:T(8,128)(2,1)S(1)}, u32[]{:S(2)}, u32[]{:S(2)}) collective-permute-start(bf16[3,4,256,128]{3,2,1,0:T(8,128)(2,1)S(1)} %join.2), channel_id=1, source_target_pairs={{0,12},{1,13},{2,14},{3,15},{4,0},{5,1},{6,2},{7,3},{8,4},{9,5},{1... | collective-permute-start | bytes 2359304 | tf_op jit(solution)/shard_map/ppermute | solution.py:50
  36.8 19.1 %copy-start.9 = (bf16[4,256,256]{2,1,0:T(8,128)(2,1)}, bf16[4,256,256]{2,1,0:T(8,128)(2,1)S(1)}, u32[]{:S(2)}) copy-start(bf16[4,256,256]{2,1,0:T(8,128)(2,1)S(1)} %collective-permute-done.5.refs_4_) | copy-start | bytes 1572868
  36.8 13.9 %collective-permute-start.17 = (bf16[3,4,256,128]{3,2,1,0:T(8,128)(2,1)S(1)}, bf16[3,4,256,128]{3,2,1,0:T(8,128)(2,1)S(1)}, u32[]{:S(2)}, u32[]{:S(2)}) collective-permute-start(bf16[3,4,256,128]{3,2,1,0:T(8,128)(2,1)S(1)} %join.3), channel_id=1, source_target_pairs={{0,3},{1,0},{2,1},{3,2},{4,7},{5,4},{6,5},{7,6},{8,11},{9,8},{10,9... | collective-permute-start | bytes 2359304 | tf_op jit(solution)/shard_map/ppermute | solution.py:50
  45.2 10.7 %collective-permute-start.4 = (bf16[4,256,256]{2,1,0:T(8,128)(2,1)}, bf16[4,256,256]{2,1,0:T(8,128)(2,1)}, u32[]{:S(2)}, u32[]{:S(2)}) collective-permute-start(bf16[4,256,256]{2,1,0:T(8,128)(2,1)} %collective-permute-done.3.refs_2_), channel_id=1, source_target_pairs={{0,32},{1,33},{2,34},{3,35},{4,36},{5,37},{6,38},{7,39},{8,40},{9,... | collective-permute-start | bytes 1572872 | tf_op jit(solution)/shard_map/ppermute | solution.py:50
  45.2 21.2 %collective-permute-start.12 = (bf16[3,4,256,128]{3,2,1,0:T(8,128)(2,1)}, bf16[3,4,256,128]{3,2,1,0:T(8,128)(2,1)}, u32[]{:S(2)}, u32[]{:S(2)}) collective-permute-start(bf16[3,4,256,128]{3,2,1,0:T(8,128)(2,1)} %collective-permute-done.10.refs_0_.refs_8_), channel_id=1, source_target_pairs={{0,4},{1,5},{2,6},{3,7},{4,8},{5,9},{6,10},{7,11},{8,12},{9,13},{1... | collective-permute-start | bytes 2359304 | tf_op jit(solution)/shard_map/ppermute | solution.py:50
  47.3 19.1 %collective-permute-start.18 = (bf16[3,4,256,128]{3,2,1,0:T(8,128)(2,1)}, bf16[3,4,256,128]{3,2,1,0:T(8,128)(2,1)}, u32[]{:S(2)}, u32[]{:S(2)}) collective-permute-start(bf16[3,4,256,128]{3,2,1,0:T(8,128)(2,1)} %collective-permute-done.16.refs_2_.refs_11_), channel_id=1, source_target_pairs={{0,1},{1,2},{2,3},{3,0},{4,5},{5,6},{6,7},{7,4},{8,9},{9,10},{10,1... | collective-permute-start | bytes 2359304 | tf_op jit(solution)/shard_map/ppermute | solution.py:50
  47.4 8.5 %copy-start.6 = (bf16[3,4,256,128]{3,2,1,0:T(8,128)(2,1)}, bf16[3,4,256,128]{3,2,1,0:T(8,128)(2,1)S(1)}, u32[]{:S(2)}) copy-start(bf16[3,4,256,128]{3,2,1,0:T(8,128)(2,1)S(1)} %collective-permute-done.11.refs_1_.refs_9_) | copy-start | bytes 2359300
  47.4 19.0 %collective-permute-start.6 = (bf16[4,256,256]{2,1,0:T(8,128)(2,1)}, bf16[4,256,256]{2,1,0:T(8,128)(2,1)}, u32[]{:S(2)}, u32[]{:S(2)}) collective-permute-start(bf16[4,256,256]{2,1,0:T(8,128)(2,1)} %collective-permute-done.2.refs_1_), channel_id=1, source_target_pairs={{0,16},{16,0},{32,48},{48,32},{64,80},{80,64},{96,112},{112,96},{1... | collective-permute-start | bytes 1572872 | tf_op jit(solution)/shard_map/ppermute | solution.py:54
  50.7 5.2 %copy-start.7 = (bf16[3,4,256,128]{3,2,1,0:T(8,128)(2,1)}, bf16[3,4,256,128]{3,2,1,0:T(8,128)(2,1)S(1)}, u32[]{:S(2)}) copy-start(bf16[3,4,256,128]{3,2,1,0:T(8,128)(2,1)S(1)} %collective-permute-done.17.refs_3_.refs_12_) | copy-start | bytes 2359300
  50.7 15.7 %collective-permute-start.7 = (bf16[4,256,256]{2,1,0:T(8,128)(2,1)}, bf16[4,256,256]{2,1,0:T(8,128)(2,1)}, u32[]{:S(2)}, u32[]{:S(2)}) collective-permute-start(bf16[4,256,256]{2,1,0:T(8,128)(2,1)} %collective-permute-done.3.refs_2_), channel_id=1, source_target_pairs={{0,16},{16,0},{32,48},{48,32},{64,80},{80,64},{96,112},{112,96},{1... | collective-permute-start | bytes 1572872 | tf_op jit(solution)/shard_map/ppermute | solution.py:54
  55.9 10.6 %collective-permute-start.8 = (bf16[4,256,256]{2,1,0:T(8,128)(2,1)}, bf16[4,256,256]{2,1,0:T(8,128)(2,1)}, u32[]{:S(2)}, u32[]{:S(2)}) collective-permute-start(bf16[4,256,256]{2,1,0:T(8,128)(2,1)} %collective-permute-done.4.refs_3_), channel_id=1, source_target_pairs={{0,16},{16,0},{32,48},{48,32},{64,80},{80,64},{96,112},{112,96},{1... | collective-permute-start | bytes 1572872 | tf_op jit(solution)/shard_map/ppermute | solution.py:54
  61.8 4.7 %copy-start.5 = (bf16[1,16,16]{2,1,0:T(8,128)(2,1)S(1)}, bf16[1,16,16]{2,1,0:T(8,128)(2,1)}, u32[]{:S(2)}) copy-start(bf16[1,16,16]{2,1,0:T(8,128)(2,1)} %two_site_ref.3) | copy-start | bytes 1540
  73.3 15.6 %collective-permute-start.19 = (bf16[4,256,256]{2,1,0:T(8,128)(2,1)S(1)}, bf16[4,256,256]{2,1,0:T(8,128)(2,1)S(1)}, u32[]{:S(2)}, u32[]{:S(2)}) collective-permute-start(bf16[4,256,256]{2,1,0:T(8,128)(2,1)S(1)} %get-tuple-element.43), channel_id=1, source_target_pairs={{0,4},{1,5},{2,6},{3,7},{4,8},{5,9},{6,10},{7,11},{8,12},{9,13},{1... | collective-permute-start | bytes 1572872 | tf_op jit(solution)/shard_map/ppermute | solution.py:50
  74.0 16.2 %collective-permute-start.20 = (bf16[4,256,256]{2,1,0:T(8,128)(2,1)S(1)}, bf16[4,256,256]{2,1,0:T(8,128)(2,1)S(1)}, u32[]{:S(2)}, u32[]{:S(2)}) collective-permute-start(bf16[4,256,256]{2,1,0:T(8,128)(2,1)S(1)} %get-tuple-element.44), channel_id=1, source_target_pairs={{0,12},{1,13},{2,14},{3,15},{4,0},{5,1},{6,2},{7,3},{8,4},{9,5},{1... | collective-permute-start | bytes 1572872 | tf_op jit(solution)/shard_map/ppermute | solution.py:50
  76.6 15.0 %collective-permute-start.29 = (bf16[4,256,256]{2,1,0:T(8,128)(2,1)S(1)}, bf16[4,256,256]{2,1,0:T(8,128)(2,1)S(1)}, u32[]{:S(2)}, u32[]{:S(2)}) collective-permute-start(bf16[4,256,256]{2,1,0:T(8,128)(2,1)S(1)} %get-tuple-element.56), channel_id=1, source_target_pairs={{0,1},{1,2},{2,3},{3,0},{4,5},{5,6},{6,7},{7,4},{8,9},{9,10},{10,1... | collective-permute-start | bytes 1572872 | tf_op jit(solution)/shard_map/ppermute | solution.py:50
  77.2 15.2 %collective-permute-start.30 = (bf16[4,256,256]{2,1,0:T(8,128)(2,1)S(1)}, bf16[4,256,256]{2,1,0:T(8,128)(2,1)S(1)}, u32[]{:S(2)}, u32[]{:S(2)}) collective-permute-start(bf16[4,256,256]{2,1,0:T(8,128)(2,1)S(1)} %get-tuple-element.57), channel_id=1, source_target_pairs={{0,3},{1,0},{2,1},{3,2},{4,7},{5,4},{6,5},{7,6},{8,11},{9,8},{10,9... | collective-permute-start | bytes 1572872 | tf_op jit(solution)/shard_map/ppermute | solution.py:50
  79.9 1.2 collective-permute-start.22
  88.1 14.1 %collective-permute-start.23 = (bf16[4,256,256]{2,1,0:T(8,128)(2,1)S(1)}, bf16[4,256,256]{2,1,0:T(8,128)(2,1)S(1)}, u32[]{:S(2)}, u32[]{:S(2)}) collective-permute-start(bf16[4,256,256]{2,1,0:T(8,128)(2,1)S(1)} %get-tuple-element.50), channel_id=1, source_target_pairs={{0,12},{1,13},{2,14},{3,15},{4,0},{5,1},{6,2},{7,3},{8,4},{9,5},{1... | collective-permute-start | bytes 1572872 | tf_op jit(solution)/shard_map/ppermute | solution.py:50
  88.9 16.0 %collective-permute-start.24 = (bf16[4,256,256]{2,1,0:T(8,128)(2,1)S(1)}, bf16[4,256,256]{2,1,0:T(8,128)(2,1)S(1)}, u32[]{:S(2)}, u32[]{:S(2)}) collective-permute-start(bf16[4,256,256]{2,1,0:T(8,128)(2,1)S(1)} %get-tuple-element.51), channel_id=1, source_target_pairs={{0,4},{1,5},{2,6},{3,7},{4,8},{5,9},{6,10},{7,11},{8,12},{9,13},{1... | collective-permute-start | bytes 1572872 | tf_op jit(solution)/shard_map/ppermute | solution.py:50
  90.2 15.0 %collective-permute-start.32 = (bf16[4,256,256]{2,1,0:T(8,128)(2,1)S(1)}, bf16[4,256,256]{2,1,0:T(8,128)(2,1)S(1)}, u32[]{:S(2)}, u32[]{:S(2)}) collective-permute-start(bf16[4,256,256]{2,1,0:T(8,128)(2,1)S(1)} %get-tuple-element.62), channel_id=1, source_target_pairs={{0,3},{1,0},{2,1},{3,2},{4,7},{5,4},{6,5},{7,6},{8,11},{9,8},{10,9... | collective-permute-start | bytes 1572872 | tf_op jit(solution)/shard_map/ppermute | solution.py:50
  91.6 14.9 %collective-permute-start.33 = (bf16[4,256,256]{2,1,0:T(8,128)(2,1)S(1)}, bf16[4,256,256]{2,1,0:T(8,128)(2,1)S(1)}, u32[]{:S(2)}, u32[]{:S(2)}) collective-permute-start(bf16[4,256,256]{2,1,0:T(8,128)(2,1)S(1)} %get-tuple-element.63), channel_id=1, source_target_pairs={{0,1},{1,2},{2,3},{3,0},{4,5},{5,6},{6,7},{7,4},{8,9},{9,10},{10,1... | collective-permute-start | bytes 1572872 | tf_op jit(solution)/shard_map/ppermute | solution.py:50
  92.4 22.6 %collective-permute-start.21 = (bf16[4,256,256]{2,1,0:T(8,128)(2,1)S(1)}, bf16[4,256,256]{2,1,0:T(8,128)(2,1)S(1)}, u32[]{:S(2)}, u32[]{:S(2)}) collective-permute-start(bf16[4,256,256]{2,1,0:T(8,128)(2,1)S(1)} %add_convert_fusion.3), channel_id=1, source_target_pairs={{0,4},{1,5},{2,6},{3,7},{4,8},{5,9},{6,10},{7,11},{8,12},{9,13},{1... | collective-permute-start | bytes 1572872 | tf_op jit(solution)/shard_map/ppermute | solution.py:50
  102.1 15.0 %collective-permute-start.31 = (bf16[4,256,256]{2,1,0:T(8,128)(2,1)S(1)}, bf16[4,256,256]{2,1,0:T(8,128)(2,1)S(1)}, u32[]{:S(2)}, u32[]{:S(2)}) collective-permute-start(bf16[4,256,256]{2,1,0:T(8,128)(2,1)S(1)} %add_convert_fusion.1), channel_id=1, source_target_pairs={{0,1},{1,2},{2,3},{3,0},{4,5},{5,6},{6,7},{7,4},{8,9},{9,10},{10,1... | collective-permute-start | bytes 1572872 | tf_op jit(solution)/shard_map/ppermute | solution.py:50
  105.1 12.3 %collective-permute-start.25 = (bf16[4,256,256]{2,1,0:T(8,128)(2,1)S(1)}, bf16[4,256,256]{2,1,0:T(8,128)(2,1)S(1)}, u32[]{:S(2)}, u32[]{:S(2)}) collective-permute-start(bf16[4,256,256]{2,1,0:T(8,128)(2,1)S(1)} %add_convert_fusion.2), channel_id=1, source_target_pairs={{0,12},{1,13},{2,14},{3,15},{4,0},{5,1},{6,2},{7,3},{8,4},{9,5},{1... | collective-permute-start | bytes 1572872 | tf_op jit(solution)/shard_map/ppermute | solution.py:50
  106.7 15.0 %collective-permute-start.34 = (bf16[4,256,256]{2,1,0:T(8,128)(2,1)S(1)}, bf16[4,256,256]{2,1,0:T(8,128)(2,1)S(1)}, u32[]{:S(2)}, u32[]{:S(2)}) collective-permute-start(bf16[4,256,256]{2,1,0:T(8,128)(2,1)S(1)} %add_convert_fusion), channel_id=1, source_target_pairs={{0,3},{1,0},{2,1},{3,2},{4,7},{5,4},{6,5},{7,6},{8,11},{9,8},{10,9... | collective-permute-start | bytes 1572872 | tf_op jit(solution)/shard_map/ppermute | solution.py:50
  117.4 14.0 %copy-start.11 = (s32[4]{0:T(128)S(1)}, s32[4]{0:T(128)}, u32[]{:S(2)}) copy-start(s32[4]{0:T(128)} %param.14) | copy-start | bytes 52
  117.6 10.8 %collective-permute-start.26 = (bf16[2,256,256]{2,1,0:T(8,128)(2,1)S(1)}, bf16[2,256,256]{2,1,0:T(8,128)(2,1)S(1)}, u32[]{:S(2)}, u32[]{:S(2)}) collective-permute-start(bf16[2,256,256]{2,1,0:T(8,128)(2,1)S(1)} %pad_maximum_fusion), channel_id=1, source_target_pairs={{0,2},{1,3},{2,0},{3,1},{4,6},{5,7},{6,4},{7,5},{8,10},{9,11},{10,... | collective-permute-start | bytes 786440 | tf_op jit(solution)/shard_map/ppermute | solution.py:50
  118.2 13.7 %collective-permute-start.27 = (bf16[2,256,256]{2,1,0:T(8,128)(2,1)S(1)}, bf16[2,256,256]{2,1,0:T(8,128)(2,1)S(1)}, u32[]{:S(2)}, u32[]{:S(2)}) collective-permute-start(bf16[2,256,256]{2,1,0:T(8,128)(2,1)S(1)} %pad_maximum_fusion.1), channel_id=1, source_target_pairs={{0,1},{1,2},{2,3},{3,0},{4,5},{5,6},{6,7},{7,4},{8,9},{9,10},{10,1... | collective-permute-start | bytes 786440 | tf_op jit(solution)/shard_map/ppermute | solution.py:50
  120.1 11.8 %collective-permute-start.28 = (bf16[2,256,256]{2,1,0:T(8,128)(2,1)S(1)}, bf16[2,256,256]{2,1,0:T(8,128)(2,1)S(1)}, u32[]{:S(2)}, u32[]{:S(2)}) collective-permute-start(bf16[2,256,256]{2,1,0:T(8,128)(2,1)S(1)} %pad_maximum_fusion.2), channel_id=1, source_target_pairs={{0,3},{1,0},{2,1},{3,2},{4,7},{5,4},{6,5},{7,6},{8,11},{9,8},{10,9... | collective-permute-start | bytes 786440 | tf_op jit(solution)/shard_map/ppermute | solution.py:50
  121.9 10.7 %collective-permute-start.35 = (bf16[2,256,256]{2,1,0:T(8,128)(2,1)S(1)}, bf16[2,256,256]{2,1,0:T(8,128)(2,1)S(1)}, u32[]{:S(2)}, u32[]{:S(2)}) collective-permute-start(bf16[2,256,256]{2,1,0:T(8,128)(2,1)S(1)} %pad_maximum_fusion.3), channel_id=1, source_target_pairs={{0,8},{1,9},{2,10},{3,11},{4,12},{5,13},{6,14},{7,15},{8,0},{9,1},... | collective-permute-start | bytes 786440 | tf_op jit(solution)/shard_map/ppermute | solution.py:50
  124.1 11.2 %collective-permute-start.36 = (bf16[2,256,256]{2,1,0:T(8,128)(2,1)S(1)}, bf16[2,256,256]{2,1,0:T(8,128)(2,1)S(1)}, u32[]{:S(2)}, u32[]{:S(2)}) collective-permute-start(bf16[2,256,256]{2,1,0:T(8,128)(2,1)S(1)} %pad_maximum_fusion.4), channel_id=1, source_target_pairs={{0,4},{1,5},{2,6},{3,7},{4,8},{5,9},{6,10},{7,11},{8,12},{9,13},{1... | collective-permute-start | bytes 786440 | tf_op jit(solution)/shard_map/ppermute | solution.py:50
  128.5 7.4 %collective-permute-start.37 = (bf16[2,256,256]{2,1,0:T(8,128)(2,1)S(1)}, bf16[2,256,256]{2,1,0:T(8,128)(2,1)S(1)}, u32[]{:S(2)}, u32[]{:S(2)}) collective-permute-start(bf16[2,256,256]{2,1,0:T(8,128)(2,1)S(1)} %pad_maximum_fusion.5), channel_id=1, source_target_pairs={{0,12},{1,13},{2,14},{3,15},{4,0},{5,1},{6,2},{7,3},{8,4},{9,5},{1... | collective-permute-start | bytes 786440 | tf_op jit(solution)/shard_map/ppermute | solution.py:50

commit v7 on v6

--- a/solution.py
+++ b/solution.py
@@ -191,7 +191,9 @@
     other = (group + core) & 1
     back = (flow * (1 - 2 * other) * (y - group // CORES)) & 3
     tile = (other * RING + back) * 4 + loc_ref[t, 0, a]
-    return jnp.dot(mixed, right[tile], preferred_element_type=jnp.float32).astype(jnp.bfloat16)
+    return lax.dot_general(
+        mixed, right[tile], (((1,), (1,)), ((), ())), preferred_element_type=jnp.float32
+    ).astype(jnp.bfloat16)
 
 
 def spot_of():
@@ -330,9 +332,8 @@
         jnp.broadcast_to(right_loc[:, 0][None, None], (STATES, 1, tiles)), "col", 0, 0, tiled=True
     )
     env_right, loc, _ = lax.optimization_barrier((env_right, loc, behind_x))
-    lane = lax.broadcasted_iota(jnp.int32, (1, 1, tile), 2)
-    right = jnp.swapaxes(env_right[0], 1, 2)
-    right = jnp.where(lane < right_size[:, None, None], right, 0).astype(jnp.bfloat16)
+    line = lax.broadcasted_iota(jnp.int32, (1, tile, 1), 1)
+    right = jnp.where(line < right_size[:, None, None], env_right[0], 0).astype(jnp.bfloat16)
     right = [right]
     for _ in range(RING - 1):
         right.append(hop(right[-1], "y"))

time: 137 us -> 136 us (level)
  local copies, waits for them, and re-layouts: 3.45 us -> 1.41 us
    optimization_barrier x1 -> x0, local copies, waits for them, and re-layouts: 2.04 us -> none  [per_device(): env_right, loc, _ = lax.optimization_barrier((env_right, loc, behind_x))]
    ppermute x5, starting transfers between devices: 5.79 us -> 4.19 us  [swap_cores(): return lax.ppermute(value, 'row', [(r, r ^ 1) for r in range(RING * CORES)])]
  transfers between devices with their start and end apart: 39 -> 39, of which waited for: 23 -> 22; matrix products, arithmetic and copies ran while one was open for 5% -> 4% of each run, Pallas kernels for 14% -> 14%
where the time goes in v7:
time: 136 us; the launch traced here: 135 us
  starting transfers between devices  52 us (38%)
  waiting for transfers between devices  50 us (37%)
  Pallas kernels  26.4 us (19%)
  other arithmetic  4.74 us (3%)
  local copies, waits for them, and re-layouts  1.41 us (1%)
    ppermute x33, waiting for transfers between devices, ring_send(): return lax.ppermute(value, ('row', 'col'), pairs)  48.2 us
    ppermute x33, starting transfers between devices, ring_send(): return lax.ppermute(value, ('row', 'col'), pairs)  43.2 us
    pallas_call x2, Pallas kernels, apply_terms(): pl.pallas_call(functools.partial(apply_kernel, chosen), out_shape=[out] *...  14.1 us
    pallas_call x2, Pallas kernels, left_parts(): pl.pallas_call(kernel, out_shape=pltpu.HBM(out, jnp.bfloat16), in_specs=[...  10.3 us
    all_to_all x1, starting transfers between devices, per_device(): lax.all_to_all(jnp.broadcast_to(right_loc[:, 0][None, None], (STATES, 1,...  4.65 us
    ppermute x5, starting transfers between devices, swap_cores(): return lax.ppermute(value, 'row', [(r, r ^ 1) for r in range(RING * CORES)])  4.19 us
  transfers between devices with their start and end apart: 39, of which 22 were waited for; matrix products, arithmetic and copies ran while one was open for 4% of the time, Pallas kernels for 14%

profile of v7, /device:TPU:0, one launch (start us, length us, event | category | flops | bytes accessed | tf_op | source)
XLA Modules:
  0.0 134.9 jit_solution(9804140593273940117)
XLA Ops:
  0.0 1.6 %collective-permute-start = (bf16[4,256,256]{2,1,0:T(8,128)(2,1)}, bf16[4,256,256]{2,1,0:T(8,128)(2,1)S(1)}, u32[]{:S(2)}, u32[]{:S(2)}) collective-permute-start(bf16[4,256,256]{2,1,0:T(8,128)(2,1)} %bitcast.16), channel_id=1, source_target_pairs={{0,1},{1,2},{2,3},{3,0},{4,5},{5,6},{6,7},{7,4},{8,9},{9,10},{10,1... | collective-permute-start | bytes 1572872 | tf_op jit(solution)/shard_map/ppermute | solution.py:50
  1.6 1.7 %collective-permute-start.1 = (bf16[4,256,256]{2,1,0:T(8,128)(2,1)}, bf16[4,256,256]{2,1,0:T(8,128)(2,1)S(1)}, u32[]{:S(2)}, u32[]{:S(2)}) collective-permute-start(bf16[4,256,256]{2,1,0:T(8,128)(2,1)} %bitcast.17), channel_id=1, source_target_pairs={{0,3},{1,0},{2,1},{3,2},{4,7},{5,4},{6,5},{7,6},{8,11},{9,8},{10,9... | collective-permute-start | bytes 1572872 | tf_op jit(solution)/shard_map/ppermute | solution.py:50
  3.2 2.0 %collective-permute-start.13 = (bf16[4,256,256]{2,1,0:T(8,128)(2,1)}, bf16[4,256,256]{2,1,0:T(8,128)(2,1)S(1)}, u32[]{:S(2)}, u32[]{:S(2)}) collective-permute-start(bf16[4,256,256]{2,1,0:T(8,128)(2,1)} %bitcast.18), channel_id=1, source_target_pairs={{0,4},{1,5},{2,6},{3,7},{4,8},{5,9},{6,10},{7,11},{8,12},{9,13},{1... | collective-permute-start | bytes 1572872 | tf_op jit(solution)/shard_map/ppermute | solution.py:50
  5.2 2.1 %collective-permute-start.14 = (bf16[4,256,256]{2,1,0:T(8,128)(2,1)}, bf16[4,256,256]{2,1,0:T(8,128)(2,1)S(1)}, u32[]{:S(2)}, u32[]{:S(2)}) collective-permute-start(bf16[4,256,256]{2,1,0:T(8,128)(2,1)} %bitcast.19), channel_id=1, source_target_pairs={{0,12},{1,13},{2,14},{3,15},{4,0},{5,1},{6,2},{7,3},{8,4},{9,5},{1... | collective-permute-start | bytes 1572872 | tf_op jit(solution)/shard_map/ppermute | solution.py:50
  7.4 1.3 broadcast_in_dim.35
  8.6 4.7 %all-to-all-start = ((s32[16,1,4]{2,1,0:T(1,128)}), s32[16,1,4]{2,1,0:T(1,128)S(1)}, u32[]{:S(2)}, u32[]{:S(2)}) async-start(s32[16,1,4]{2,1,0:T(1,128)} %broadcast_in_dim.35), calls=%async_computation | async-start | bytes 16384 | tf_op jit(solution)/shard_map/all_to_all | solution.py:331
  13.3 0.7 iota_compare_fusion
  14.0 0.7 collective-permute-done.first.refs_1_
  14.7 1.7 %collective-permute-start.9 = (bf16[4,256,256]{2,1,0:T(8,128)(2,1)S(1)}, bf16[4,256,256]{2,1,0:T(8,128)(2,1)}, u32[]{:S(2)}, u32[]{:S(2)}) collective-permute-start(bf16[4,256,256]{2,1,0:T(8,128)(2,1)S(1)} %collective-permute-done.first.refs_1_), channel_id=1, source_target_pairs={{0,1},{1,2},{2,3},{3,0},{4,5},{5,6},{6,7},{7,4},{8,9},{9,10},{10,1... | collective-permute-start | bytes 1572872 | tf_op jit(solution)/shard_map/ppermute | solution.py:50
  16.5 2.9 %collective-permute-done.13.first.refs_4_ = bf16[4,256,256]{2,1,0:T(8,128)(2,1)S(1)} collective-permute-done((bf16[4,256,256]{2,1,0:T(8,128)(2,1)}, bf16[4,256,256]{2,1,0:T(8,128)(2,1)S(1)}, u32[]{:S(2)}, u32[]{:S(2)}) %collective-permute-start.13) | collective-permute-done | bytes 524320 | tf_op jit(solution)/shard_map/ppermute | solution.py:50
  19.4 0.7 collective-permute-start.15
  20.1 0.6 all-to-all-done.loc_ref
  20.8 1.2 bitcast_select_fusion.refs_0_
  22.0 1.6 %collective-permute-start.2 = (bf16[4,256,256]{2,1,0:T(8,128)(2,1)S(1)}, bf16[4,256,256]{2,1,0:T(8,128)(2,1)}, u32[]{:S(2)}, u32[]{:S(2)}) collective-permute-start(bf16[4,256,256]{2,1,0:T(8,128)(2,1)S(1)} %bitcast_select_fusion.refs_0_), channel_id=1, source_target_pairs={{0,32},{1,33},{2,34},{3,35},{4,36},{5,37},{6,38},{7,39},{8,40},{9,... | collective-permute-start | bytes 1572872 | tf_op jit(solution)/shard_map/ppermute | solution.py:50
  23.7 1.3 collective-permute-start.5
  24.9 0.4 collective-permute-done.9.second.refs_2_
  25.3 1.0 join.2
  26.3 2.2 %collective-permute-start.10 = (bf16[3,4,256,128]{3,2,1,0:T(8,128)(2,1)S(1)}, bf16[3,4,256,128]{3,2,1,0:T(8,128)(2,1)}, u32[]{:S(2)}, u32[]{:S(2)}) collective-permute-start(bf16[3,4,256,128]{3,2,1,0:T(8,128)(2,1)S(1)} %join.2), channel_id=1, source_target_pairs={{0,4},{1,5},{2,6},{3,7},{4,8},{5,9},{6,10},{7,11},{8,12},{9,13},{1... | collective-permute-start | bytes 2359304 | tf_op jit(solution)/shard_map/ppermute | solution.py:50
  28.5 1.4 %collective-permute-done.15.second.refs_5_ = bf16[4,256,256]{2,1,0:T(8,128)(2,1)} collective-permute-done((bf16[4,256,256]{2,1,0:T(8,128)(2,1)S(1)}, bf16[4,256,256]{2,1,0:T(8,128)(2,1)}, u32[]{:S(2)}, u32[]{:S(2)}) %collective-permute-start.15) | collective-permute-done | bytes 524320 | tf_op jit(solution)/shard_map/ppermute | solution.py:50
  29.9 1.0 join.3
  31.1 1.5 %collective-permute-done.2.refs_1_ = bf16[4,256,256]{2,1,0:T(8,128)(2,1)} collective-permute-done((bf16[4,256,256]{2,1,0:T(8,128)(2,1)S(1)}, bf16[4,256,256]{2,1,0:T(8,128)(2,1)}, u32[]{:S(2)}, u32[]{:S(2)}) %collective-permute-start.2) | collective-permute-done | bytes 524320 | tf_op jit(solution)/shard_map/ppermute | solution.py:50
  32.6 0.4 collective-permute-start.3
  33.0 1.9 %collective-permute-start.11 = (bf16[3,4,256,128]{3,2,1,0:T(8,128)(2,1)S(1)}, bf16[3,4,256,128]{3,2,1,0:T(8,128)(2,1)S(1)}, u32[]{:S(2)}, u32[]{:S(2)}) collective-permute-start(bf16[3,4,256,128]{3,2,1,0:T(8,128)(2,1)S(1)} %join.2), channel_id=1, source_target_pairs={{0,12},{1,13},{2,14},{3,15},{4,0},{5,1},{6,2},{7,3},{8,4},{9,5},{1... | collective-permute-start | bytes 2359304 | tf_op jit(solution)/shard_map/ppermute | solution.py:50
  34.9 2.2 %collective-permute-start.17 = (bf16[3,4,256,128]{3,2,1,0:T(8,128)(2,1)S(1)}, bf16[3,4,256,128]{3,2,1,0:T(8,128)(2,1)S(1)}, u32[]{:S(2)}, u32[]{:S(2)}) collective-permute-start(bf16[3,4,256,128]{3,2,1,0:T(8,128)(2,1)S(1)} %join.3), channel_id=1, source_target_pairs={{0,3},{1,0},{2,1},{3,2},{4,7},{5,4},{6,5},{7,6},{8,11},{9,8},{10,9... | collective-permute-start | bytes 2359304 | tf_op jit(solution)/shard_map/ppermute | solution.py:50
  37.1 6.2 %collective-permute-done.3.refs_2_ = bf16[4,256,256]{2,1,0:T(8,128)(2,1)} collective-permute-done((bf16[4,256,256]{2,1,0:T(8,128)(2,1)}, bf16[4,256,256]{2,1,0:T(8,128)(2,1)}, u32[]{:S(2)}, u32[]{:S(2)}) %collective-permute-start.3) | collective-permute-done | bytes 524320 | tf_op jit(solution)/shard_map/ppermute | solution.py:50
  43.3 0.6 collective-permute-start.12
  43.9 5.3 %collective-permute-done.16.refs_2_.refs_11_ = bf16[3,4,256,128]{3,2,1,0:T(8,128)(2,1)} collective-permute-done((bf16[3,4,256,128]{3,2,1,0:T(8,128)(2,1)S(1)}, bf16[3,4,256,128]{3,2,1,0:T(8,128)(2,1)}, u32[]{:S(2)}, u32[]{:S(2)}) %collective-permute-start.16) | collective-permute-done | bytes 786464 | tf_op jit(solution)/shard_map/ppermute | solution.py:50
  49.2 0.7 collective-permute-start.6
  49.9 0.8 collective-permute-done.17.refs_3_.refs_12_
  50.7 2.2 %collective-permute-start.7 = (bf16[4,256,256]{2,1,0:T(8,128)(2,1)}, bf16[4,256,256]{2,1,0:T(8,128)(2,1)}, u32[]{:S(2)}, u32[]{:S(2)}) collective-permute-start(bf16[4,256,256]{2,1,0:T(8,128)(2,1)} %collective-permute-done.3.refs_2_), channel_id=1, source_target_pairs={{0,16},{16,0},{32,48},{48,32},{64,80},{80,64},{96,112},{112,96},{1... | collective-permute-start | bytes 1572872 | tf_op jit(solution)/shard_map/ppermute | solution.py:54
  52.9 1.1 collective-permute-done.4.refs_3_
  54.2 5.7 %left_parts.2.refs_14_ = bf16[7,4,256,256]{3,2,1,0:T(8,128)(2,1)} custom-call(s32[4,2]{1,0:T(4,128)S(1)} %copy.11.src_ref, bf16[4,2,256,256]{3,2,1,0:T(8,128)(2,1)S(1)} %bitcast.12, bf16[4,256,256]{2,1,0:T(8,128)(2,1)} %bitcast.20, bf16[4,256,256]{2,1,0:T(8,128)(2,1)} %copy-done.1, bf16[4,256,256]{2,1,0:T(8,128)(2,1)} %collective-permute-done.9.second.refs_2_, ...), custom_call_target="tpu_custom_call" | custom-call | flops 1879048192 | bytes 5242880 | tf_op jit(solution)/shard_map/left_parts/pallas_call | solution.py:145
  59.9 4.6 %left_parts.3.refs_15_ = bf16[4,4,256,256]{3,2,1,0:T(8,128)(2,1)} custom-call(s32[4,2]{1,0:T(4,128)S(1)} %copy.11.src_ref, bf16[4,2,256,256]{3,2,1,0:T(8,128)(2,1)S(1)} %bitcast.13, bf16[3,4,256,128]{3,2,1,0:T(8,128)(2,1)} %collective-permute-done.10.refs_0_.refs_8_, bf16[3,4,256,128]{3,2,1,0:T(8,128)(2,1)} %copy-done.6, ...), custom_call_target="tpu_custom_call" | custom-call | flops 1073741824 | bytes 5242880 | tf_op jit(solution)/shard_map/left_parts/pallas_call | solution.py:145
  64.6 6.9 %apply_terms.2 = (bf16[4,256,256]{2,1,0:T(8,128)(2,1)S(1)}, bf16[4,256,256]{2,1,0:T(8,128)(2,1)S(1)}, bf16[4,256,256]{2,1,0:T(8,128)(2,1)S(1)}, bf16[4,256,256]{...) custom-call(s32[4,2]{1,0:T(4,128)S(1)} %copy.11.src_ref, ...), custom_call_target="tpu_custom_call" | custom-call | flops 2684354560 | bytes 8388608 | tf_op jit(solution)/shard_map/apply_terms/pallas_call | solution.py:279
  71.5 0.6 collective-permute-start.19
  72.1 2.7 %collective-permute-start.20 = (bf16[4,256,256]{2,1,0:T(8,128)(2,1)S(1)}, bf16[4,256,256]{2,1,0:T(8,128)(2,1)S(1)}, u32[]{:S(2)}, u32[]{:S(2)}) collective-permute-start(bf16[4,256,256]{2,1,0:T(8,128)(2,1)S(1)} %get-tuple-element.44), channel_id=1, source_target_pairs={{0,12},{1,13},{2,14},{3,15},{4,0},{5,1},{6,2},{7,3},{8,4},{9,5},{1... | collective-permute-start | bytes 1572872 | tf_op jit(solution)/shard_map/ppermute | solution.py:50
  74.8 0.6 collective-permute-start.29
  75.4 2.7 %collective-permute-start.30 = (bf16[4,256,256]{2,1,0:T(8,128)(2,1)S(1)}, bf16[4,256,256]{2,1,0:T(8,128)(2,1)S(1)}, u32[]{:S(2)}, u32[]{:S(2)}) collective-permute-start(bf16[4,256,256]{2,1,0:T(8,128)(2,1)S(1)} %get-tuple-element.57), channel_id=1, source_target_pairs={{0,3},{1,0},{2,1},{3,2},{4,7},{5,4},{6,5},{7,6},{8,11},{9,8},{10,9... | collective-permute-start | bytes 1572872 | tf_op jit(solution)/shard_map/ppermute | solution.py:50
  78.0 1.2 collective-permute-done.22.token_ref
  79.2 7.2 %apply_terms.3 = (bf16[4,256,256]{2,1,0:T(8,128)(2,1)S(1)}, bf16[4,256,256]{2,1,0:T(8,128)(2,1)S(1)}, bf16[4,256,256]{2,1,0:T(8,128)(2,1)S(1)}, bf16[4,256,256]{...) custom-call(s32[4,2]{1,0:T(4,128)S(1)} %copy.11.src_ref, ...), custom_call_target="tpu_custom_call" | custom-call | flops 2684354560 | bytes 8388608 | tf_op jit(solution)/shard_map/apply_terms/pallas_call | solution.py:279
  86.4 0.8 collective-permute-start.23
  87.2 1.3 collective-permute-start.24
  88.5 1.1 collective-permute-start.32
  89.8 0.9 collective-permute-start.33
  90.7 1.1 collective-permute-start.21
  91.9 8.5 %collective-permute-done.23 = bf16[4,256,256]{2,1,0:T(8,128)(2,1)S(1)} collective-permute-done((bf16[4,256,256]{2,1,0:T(8,128)(2,1)S(1)}, bf16[4,256,256]{2,1,0:T(8,128)(2,1)S(1)}, u32[]{:S(2)}, u32[]{:S(2)}) %collective-permute-start.23) | collective-permute-done | bytes 524320 | tf_op jit(solution)/shard_map/ppermute | solution.py:50
  100.4 2.7 %collective-permute-done.24 = bf16[4,256,256]{2,1,0:T(8,128)(2,1)S(1)} collective-permute-done((bf16[4,256,256]{2,1,0:T(8,128)(2,1)S(1)}, bf16[4,256,256]{2,1,0:T(8,128)(2,1)S(1)}, u32[]{:S(2)}, u32[]{:S(2)}) %collective-permute-start.24) | collective-permute-done | bytes 524320 | tf_op jit(solution)/shard_map/ppermute | solution.py:50
  103.4 1.3 collective-permute-done.33
  104.8 1.2 collective-permute-start.34
  106.0 7.3 %collective-permute-done.21 = bf16[4,256,256]{2,1,0:T(8,128)(2,1)S(1)} collective-permute-done((bf16[4,256,256]{2,1,0:T(8,128)(2,1)S(1)}, bf16[4,256,256]{2,1,0:T(8,128)(2,1)S(1)}, u32[]{:S(2)}, u32[]{:S(2)}) %collective-permute-start.21) | collective-permute-done | bytes 524320 | tf_op jit(solution)/shard_map/ppermute | solution.py:50
  113.5 1.9 %collective-permute-done.31 = bf16[4,256,256]{2,1,0:T(8,128)(2,1)S(1)} collective-permute-done((bf16[4,256,256]{2,1,0:T(8,128)(2,1)S(1)}, bf16[4,256,256]{2,1,0:T(8,128)(2,1)S(1)}, u32[]{:S(2)}, u32[]{:S(2)}) %collective-permute-start.31) | collective-permute-done | bytes 524320 | tf_op jit(solution)/shard_map/ppermute | solution.py:50
  115.6 0.2 add_convert_fusion.20
  115.8 1.2 collective-permute-start.26
  117.0 1.2 collective-permute-start.27
  118.3 2.1 %collective-permute-start.28 = (bf16[2,256,256]{2,1,0:T(8,128)(2,1)S(1)}, bf16[2,256,256]{2,1,0:T(8,128)(2,1)S(1)}, u32[]{:S(2)}, u32[]{:S(2)}) collective-permute-start(bf16[2,256,256]{2,1,0:T(8,128)(2,1)S(1)} %pad_maximum_fusion.2), channel_id=1, source_target_pairs={{0,3},{1,0},{2,1},{3,2},{4,7},{5,4},{6,5},{7,6},{8,11},{9,8},{10,9... | collective-permute-start | bytes 786440 | tf_op jit(solution)/shard_map/ppermute | solution.py:50
  120.7 1.4 %collective-permute-start.35 = (bf16[2,256,256]{2,1,0:T(8,128)(2,1)S(1)}, bf16[2,256,256]{2,1,0:T(8,128)(2,1)S(1)}, u32[]{:S(2)}, u32[]{:S(2)}) collective-permute-start(bf16[2,256,256]{2,1,0:T(8,128)(2,1)S(1)} %pad_maximum_fusion.3), channel_id=1, source_target_pairs={{0,8},{1,9},{2,10},{3,11},{4,12},{5,13},{6,14},{7,15},{8,0},{9,1},... | collective-permute-start | bytes 786440 | tf_op jit(solution)/shard_map/ppermute | solution.py:50
  122.1 2.4 %collective-permute-start.36 = (bf16[2,256,256]{2,1,0:T(8,128)(2,1)S(1)}, bf16[2,256,256]{2,1,0:T(8,128)(2,1)S(1)}, u32[]{:S(2)}, u32[]{:S(2)}) collective-permute-start(bf16[2,256,256]{2,1,0:T(8,128)(2,1)S(1)} %pad_maximum_fusion.4), channel_id=1, source_target_pairs={{0,4},{1,5},{2,6},{3,7},{4,8},{5,9},{6,10},{7,11},{8,12},{9,13},{1... | collective-permute-start | bytes 786440 | tf_op jit(solution)/shard_map/ppermute | solution.py:50
  124.6 2.1 %collective-permute-done.26 = bf16[2,256,256]{2,1,0:T(8,128)(2,1)S(1)} collective-permute-done((bf16[2,256,256]{2,1,0:T(8,128)(2,1)S(1)}, bf16[2,256,256]{2,1,0:T(8,128)(2,1)S(1)}, u32[]{:S(2)}, u32[]{:S(2)}) %collective-permute-start.26) | collective-permute-done | bytes 262176 | tf_op jit(solution)/shard_map/ppermute | solution.py:50
  126.7 2.9 %collective-permute-start.37 = (bf16[2,256,256]{2,1,0:T(8,128)(2,1)S(1)}, bf16[2,256,256]{2,1,0:T(8,128)(2,1)S(1)}, u32[]{:S(2)}, u32[]{:S(2)}) collective-permute-start(bf16[2,256,256]{2,1,0:T(8,128)(2,1)S(1)} %pad_maximum_fusion.5), channel_id=1, source_target_pairs={{0,12},{1,13},{2,14},{3,15},{4,0},{5,1},{6,2},{7,3},{8,4},{9,5},{1... | collective-permute-start | bytes 786440 | tf_op jit(solution)/shard_map/ppermute | solution.py:50
  129.6 0.4 collective-permute-done.27
  130.2 0.5 collective-permute-done.35
  130.7 2.7 %collective-permute-done.36 = bf16[2,256,256]{2,1,0:T(8,128)(2,1)S(1)} collective-permute-done((bf16[2,256,256]{2,1,0:T(8,128)(2,1)S(1)}, bf16[2,256,256]{2,1,0:T(8,128)(2,1)S(1)}, u32[]{:S(2)}, u32[]{:S(2)}) %collective-permute-start.36) | collective-permute-done | bytes 262176 | tf_op jit(solution)/shard_map/ppermute | solution.py:50
  133.4 0.4 collective-permute-done.37
  133.9 1.0 fusion
  (67 shorter events, 2.0 us)
Async XLA Ops:
  0.0 54.0 %copy-start.10 = (s32[1,4,2]{1,2,0:T(2,128)S(1)}, s32[1,4,2]{1,2,0:T(2,128)}, u32[]{:S(2)}) copy-start(s32[1,4,2]{1,2,0:T(2,128)} %param.10) | copy-start | bytes 100
  0.0 54.2 %copy-start = (bf16[1,4,2,256,256]{4,3,2,1,0:T(8,128)(2,1)S(1)}, bf16[1,4,2,256,256]{4,3,2,1,0:T(8,128)(2,1)}, u32[]{:S(2)}) copy-start(bf16[1,4,2,256,256]{4,3,2,1,0:T(8,128)(2,1)} %param.9) | copy-start | bytes 3145732
  0.0 14.7 %collective-permute-start = (bf16[4,256,256]{2,1,0:T(8,128)(2,1)}, bf16[4,256,256]{2,1,0:T(8,128)(2,1)S(1)}, u32[]{:S(2)}, u32[]{:S(2)}) collective-permute-start(bf16[4,256,256]{2,1,0:T(8,128)(2,1)} %bitcast.16), channel_id=1, source_target_pairs={{0,1},{1,2},{2,3},{3,0},{4,5},{5,6},{6,7},{7,4},{8,9},{9,10},{10,1... | collective-permute-start | bytes 1572872 | tf_op jit(solution)/shard_map/ppermute | solution.py:50
  1.6 13.2 %collective-permute-start.1 = (bf16[4,256,256]{2,1,0:T(8,128)(2,1)}, bf16[4,256,256]{2,1,0:T(8,128)(2,1)S(1)}, u32[]{:S(2)}, u32[]{:S(2)}) collective-permute-start(bf16[4,256,256]{2,1,0:T(8,128)(2,1)} %bitcast.17), channel_id=1, source_target_pairs={{0,3},{1,0},{2,1},{3,2},{4,7},{5,4},{6,5},{7,6},{8,11},{9,8},{10,9... | collective-permute-start | bytes 1572872 | tf_op jit(solution)/shard_map/ppermute | solution.py:50
  3.2 16.1 %collective-permute-start.13 = (bf16[4,256,256]{2,1,0:T(8,128)(2,1)}, bf16[4,256,256]{2,1,0:T(8,128)(2,1)S(1)}, u32[]{:S(2)}, u32[]{:S(2)}) collective-permute-start(bf16[4,256,256]{2,1,0:T(8,128)(2,1)} %bitcast.18), channel_id=1, source_target_pairs={{0,4},{1,5},{2,6},{3,7},{4,8},{5,9},{6,10},{7,11},{8,12},{9,13},{1... | collective-permute-start | bytes 1572872 | tf_op jit(solution)/shard_map/ppermute | solution.py:50
  5.2 14.1 %collective-permute-start.14 = (bf16[4,256,256]{2,1,0:T(8,128)(2,1)}, bf16[4,256,256]{2,1,0:T(8,128)(2,1)S(1)}, u32[]{:S(2)}, u32[]{:S(2)}) collective-permute-start(bf16[4,256,256]{2,1,0:T(8,128)(2,1)} %bitcast.19), channel_id=1, source_target_pairs={{0,12},{1,13},{2,14},{3,15},{4,0},{5,1},{6,2},{7,3},{8,4},{9,5},{1... | collective-permute-start | bytes 1572872 | tf_op jit(solution)/shard_map/ppermute | solution.py:50
  8.6 12.1 %all-to-all-start = ((s32[16,1,4]{2,1,0:T(1,128)}), s32[16,1,4]{2,1,0:T(1,128)S(1)}, u32[]{:S(2)}, u32[]{:S(2)}) async-start(s32[16,1,4]{2,1,0:T(1,128)} %broadcast_in_dim.35), calls=%async_computation | async-start | bytes 16384 | tf_op jit(solution)/shard_map/all_to_all | solution.py:331
  14.7 39.4 %copy-start.1 = (bf16[4,256,256]{2,1,0:T(8,128)(2,1)}, bf16[4,256,256]{2,1,0:T(8,128)(2,1)S(1)}, u32[]{:S(2)}) copy-start(bf16[4,256,256]{2,1,0:T(8,128)(2,1)S(1)} %collective-permute-done.first.refs_1_) | copy-start | bytes 1572868
  14.7 39.4 %copy-start.2 = (bf16[4,256,256]{2,1,0:T(8,128)(2,1)}, bf16[4,256,256]{2,1,0:T(8,128)(2,1)S(1)}, u32[]{:S(2)}) copy-start(bf16[4,256,256]{2,1,0:T(8,128)(2,1)S(1)} %collective-permute-done.1.third.refs_3_) | copy-start | bytes 1572868
  14.7 10.6 %collective-permute-start.9 = (bf16[4,256,256]{2,1,0:T(8,128)(2,1)S(1)}, bf16[4,256,256]{2,1,0:T(8,128)(2,1)}, u32[]{:S(2)}, u32[]{:S(2)}) collective-permute-start(bf16[4,256,256]{2,1,0:T(8,128)(2,1)S(1)} %collective-permute-done.first.refs_1_), channel_id=1, source_target_pairs={{0,1},{1,2},{2,3},{3,0},{4,5},{5,6},{6,7},{7,4},{8,9},{9,10},{10,1... | collective-permute-start | bytes 1572872 | tf_op jit(solution)/shard_map/ppermute | solution.py:50
  19.4 34.8 %copy-start.3 = (bf16[4,256,256]{2,1,0:T(8,128)(2,1)}, bf16[4,256,256]{2,1,0:T(8,128)(2,1)S(1)}, u32[]{:S(2)}) copy-start(bf16[4,256,256]{2,1,0:T(8,128)(2,1)S(1)} %collective-permute-done.13.first.refs_4_) | copy-start | bytes 1572868
  19.4 34.8 %copy-start.4 = (bf16[4,256,256]{2,1,0:T(8,128)(2,1)}, bf16[4,256,256]{2,1,0:T(8,128)(2,1)S(1)}, u32[]{:S(2)}) copy-start(bf16[4,256,256]{2,1,0:T(8,128)(2,1)S(1)} %collective-permute-done.14.third.refs_6_) | copy-start | bytes 1572868
  19.4 10.6 %collective-permute-start.15 = (bf16[4,256,256]{2,1,0:T(8,128)(2,1)S(1)}, bf16[4,256,256]{2,1,0:T(8,128)(2,1)}, u32[]{:S(2)}, u32[]{:S(2)}) collective-permute-start(bf16[4,256,256]{2,1,0:T(8,128)(2,1)S(1)} %collective-permute-done.13.first.refs_4_), channel_id=1, source_target_pairs={{0,4},{1,5},{2,6},{3,7},{4,8},{5,9},{6,10},{7,11},{8,12},{9,13},{1... | collective-permute-start | bytes 1572872 | tf_op jit(solution)/shard_map/ppermute | solution.py:50
  22.0 32.0 %copy-start.8 = (bf16[4,256,256]{2,1,0:T(8,128)(2,1)}, bf16[4,256,256]{2,1,0:T(8,128)(2,1)S(1)}, u32[]{:S(2)}) copy-start(bf16[4,256,256]{2,1,0:T(8,128)(2,1)S(1)} %bitcast_select_fusion.refs_0_) | copy-start | bytes 1572868
  22.0 10.6 %collective-permute-start.2 = (bf16[4,256,256]{2,1,0:T(8,128)(2,1)S(1)}, bf16[4,256,256]{2,1,0:T(8,128)(2,1)}, u32[]{:S(2)}, u32[]{:S(2)}) collective-permute-start(bf16[4,256,256]{2,1,0:T(8,128)(2,1)S(1)} %bitcast_select_fusion.refs_0_), channel_id=1, source_target_pairs={{0,32},{1,33},{2,34},{3,35},{4,36},{5,37},{6,38},{7,39},{8,40},{9,... | collective-permute-start | bytes 1572872 | tf_op jit(solution)/shard_map/ppermute | solution.py:50
  23.7 11.2 %collective-permute-start.5 = (bf16[4,256,256]{2,1,0:T(8,128)(2,1)S(1)}, bf16[4,256,256]{2,1,0:T(8,128)(2,1)S(1)}, u32[]{:S(2)}, u32[]{:S(2)}) collective-permute-start(bf16[4,256,256]{2,1,0:T(8,128)(2,1)S(1)} %bitcast_select_fusion.refs_0_), channel_id=1, source_target_pairs={{0,16},{16,0},{32,48},{48,32},{64,80},{80,64},{96,112},{112,96},{1... | collective-permute-start | bytes 1572872 | tf_op jit(solution)/shard_map/ppermute | solution.py:54
  26.3 17.0 %collective-permute-start.10 = (bf16[3,4,256,128]{3,2,1,0:T(8,128)(2,1)S(1)}, bf16[3,4,256,128]{3,2,1,0:T(8,128)(2,1)}, u32[]{:S(2)}, u32[]{:S(2)}) collective-permute-start(bf16[3,4,256,128]{3,2,1,0:T(8,128)(2,1)S(1)} %join.2), channel_id=1, source_target_pairs={{0,4},{1,5},{2,6},{3,7},{4,8},{5,9},{6,10},{7,11},{8,12},{9,13},{1... | collective-permute-start | bytes 2359304 | tf_op jit(solution)/shard_map/ppermute | solution.py:50
  31.0 18.2 %collective-permute-start.16 = (bf16[3,4,256,128]{3,2,1,0:T(8,128)(2,1)S(1)}, bf16[3,4,256,128]{3,2,1,0:T(8,128)(2,1)}, u32[]{:S(2)}, u32[]{:S(2)}) collective-permute-start(bf16[3,4,256,128]{3,2,1,0:T(8,128)(2,1)S(1)} %join.3), channel_id=1, source_target_pairs={{0,1},{1,2},{2,3},{3,0},{4,5},{5,6},{6,7},{7,4},{8,9},{9,10},{10,1... | collective-permute-start | bytes 2359304 | tf_op jit(solution)/shard_map/ppermute | solution.py:50
  32.6 10.7 %collective-permute-start.3 = (bf16[4,256,256]{2,1,0:T(8,128)(2,1)}, bf16[4,256,256]{2,1,0:T(8,128)(2,1)}, u32[]{:S(2)}, u32[]{:S(2)}) collective-permute-start(bf16[4,256,256]{2,1,0:T(8,128)(2,1)} %collective-permute-done.2.refs_1_), channel_id=1, source_target_pairs={{0,32},{1,33},{2,34},{3,35},{4,36},{5,37},{6,38},{7,39},{8,40},{9,... | collective-permute-start | bytes 1572872 | tf_op jit(solution)/shard_map/ppermute | solution.py:50
  33.0 16.2 %collective-permute-start.11 = (bf16[3,4,256,128]{3,2,1,0:T(8,128)(2,1)S(1)}, bf16[3,4,256,128]{3,2,1,0:T(8,128)(2,1)S(1)}, u32[]{:S(2)}, u32[]{:S(2)}) collective-permute-start(bf16[3,4,256,128]{3,2,1,0:T(8,128)(2,1)S(1)} %join.2), channel_id=1, source_target_pairs={{0,12},{1,13},{2,14},{3,15},{4,0},{5,1},{6,2},{7,3},{8,4},{9,5},{1... | collective-permute-start | bytes 2359304 | tf_op jit(solution)/shard_map/ppermute | solution.py:50
  34.9 19.1 %copy-start.9 = (bf16[4,256,256]{2,1,0:T(8,128)(2,1)}, bf16[4,256,256]{2,1,0:T(8,128)(2,1)S(1)}, u32[]{:S(2)}) copy-start(bf16[4,256,256]{2,1,0:T(8,128)(2,1)S(1)} %collective-permute-done.5.refs_4_) | copy-start | bytes 1572868
  34.9 15.8 %collective-permute-start.17 = (bf16[3,4,256,128]{3,2,1,0:T(8,128)(2,1)S(1)}, bf16[3,4,256,128]{3,2,1,0:T(8,128)(2,1)S(1)}, u32[]{:S(2)}, u32[]{:S(2)}) collective-permute-start(bf16[3,4,256,128]{3,2,1,0:T(8,128)(2,1)S(1)} %join.3), channel_id=1, source_target_pairs={{0,3},{1,0},{2,1},{3,2},{4,7},{5,4},{6,5},{7,6},{8,11},{9,8},{10,9... | collective-permute-start | bytes 2359304 | tf_op jit(solution)/shard_map/ppermute | solution.py:50
  43.3 10.7 %collective-permute-start.4 = (bf16[4,256,256]{2,1,0:T(8,128)(2,1)}, bf16[4,256,256]{2,1,0:T(8,128)(2,1)}, u32[]{:S(2)}, u32[]{:S(2)}) collective-permute-start(bf16[4,256,256]{2,1,0:T(8,128)(2,1)} %collective-permute-done.3.refs_2_), channel_id=1, source_target_pairs={{0,32},{1,33},{2,34},{3,35},{4,36},{5,37},{6,38},{7,39},{8,40},{9,... | collective-permute-start | bytes 1572872 | tf_op jit(solution)/shard_map/ppermute | solution.py:50
  43.3 21.2 %collective-permute-start.12 = (bf16[3,4,256,128]{3,2,1,0:T(8,128)(2,1)}, bf16[3,4,256,128]{3,2,1,0:T(8,128)(2,1)}, u32[]{:S(2)}, u32[]{:S(2)}) collective-permute-start(bf16[3,4,256,128]{3,2,1,0:T(8,128)(2,1)} %collective-permute-done.10.refs_0_.refs_8_), channel_id=1, source_target_pairs={{0,4},{1,5},{2,6},{3,7},{4,8},{5,9},{6,10},{7,11},{8,12},{9,13},{1... | collective-permute-start | bytes 2359304 | tf_op jit(solution)/shard_map/ppermute | solution.py:50
  49.2 15.4 %collective-permute-start.18 = (bf16[3,4,256,128]{3,2,1,0:T(8,128)(2,1)}, bf16[3,4,256,128]{3,2,1,0:T(8,128)(2,1)}, u32[]{:S(2)}, u32[]{:S(2)}) collective-permute-start(bf16[3,4,256,128]{3,2,1,0:T(8,128)(2,1)} %collective-permute-done.16.refs_2_.refs_11_), channel_id=1, source_target_pairs={{0,1},{1,2},{2,3},{3,0},{4,5},{5,6},{6,7},{7,4},{8,9},{9,10},{10,1... | collective-permute-start | bytes 2359304 | tf_op jit(solution)/shard_map/ppermute | solution.py:50
  49.2 4.8 %copy-start.6 = (bf16[3,4,256,128]{3,2,1,0:T(8,128)(2,1)}, bf16[3,4,256,128]{3,2,1,0:T(8,128)(2,1)S(1)}, u32[]{:S(2)}) copy-start(bf16[3,4,256,128]{3,2,1,0:T(8,128)(2,1)S(1)} %collective-permute-done.11.refs_1_.refs_9_) | copy-start | bytes 2359300
  49.2 15.3 %collective-permute-start.6 = (bf16[4,256,256]{2,1,0:T(8,128)(2,1)}, bf16[4,256,256]{2,1,0:T(8,128)(2,1)}, u32[]{:S(2)}, u32[]{:S(2)}) collective-permute-start(bf16[4,256,256]{2,1,0:T(8,128)(2,1)} %collective-permute-done.2.refs_1_), channel_id=1, source_target_pairs={{0,16},{16,0},{32,48},{48,32},{64,80},{80,64},{96,112},{112,96},{1... | collective-permute-start | bytes 1572872 | tf_op jit(solution)/shard_map/ppermute | solution.py:54
  50.7 3.3 %copy-start.7 = (bf16[3,4,256,128]{3,2,1,0:T(8,128)(2,1)}, bf16[3,4,256,128]{3,2,1,0:T(8,128)(2,1)S(1)}, u32[]{:S(2)}) copy-start(bf16[3,4,256,128]{3,2,1,0:T(8,128)(2,1)S(1)} %collective-permute-done.17.refs_3_.refs_12_) | copy-start | bytes 2359300
  50.7 13.8 %collective-permute-start.7 = (bf16[4,256,256]{2,1,0:T(8,128)(2,1)}, bf16[4,256,256]{2,1,0:T(8,128)(2,1)}, u32[]{:S(2)}, u32[]{:S(2)}) collective-permute-start(bf16[4,256,256]{2,1,0:T(8,128)(2,1)} %collective-permute-done.3.refs_2_), channel_id=1, source_target_pairs={{0,16},{16,0},{32,48},{48,32},{64,80},{80,64},{96,112},{112,96},{1... | collective-permute-start | bytes 1572872 | tf_op jit(solution)/shard_map/ppermute | solution.py:54
  54.0 10.6 %collective-permute-start.8 = (bf16[4,256,256]{2,1,0:T(8,128)(2,1)}, bf16[4,256,256]{2,1,0:T(8,128)(2,1)}, u32[]{:S(2)}, u32[]{:S(2)}) collective-permute-start(bf16[4,256,256]{2,1,0:T(8,128)(2,1)} %collective-permute-done.4.refs_3_), channel_id=1, source_target_pairs={{0,16},{16,0},{32,48},{48,32},{64,80},{80,64},{96,112},{112,96},{1... | collective-permute-start | bytes 1572872 | tf_op jit(solution)/shard_map/ppermute | solution.py:54
  59.9 4.7 %copy-start.5 = (bf16[1,16,16]{2,1,0:T(8,128)(2,1)S(1)}, bf16[1,16,16]{2,1,0:T(8,128)(2,1)}, u32[]{:S(2)}) copy-start(bf16[1,16,16]{2,1,0:T(8,128)(2,1)} %two_site_ref.3) | copy-start | bytes 1540
  71.5 15.7 %collective-permute-start.19 = (bf16[4,256,256]{2,1,0:T(8,128)(2,1)S(1)}, bf16[4,256,256]{2,1,0:T(8,128)(2,1)S(1)}, u32[]{:S(2)}, u32[]{:S(2)}) collective-permute-start(bf16[4,256,256]{2,1,0:T(8,128)(2,1)S(1)} %get-tuple-element.43), channel_id=1, source_target_pairs={{0,4},{1,5},{2,6},{3,7},{4,8},{5,9},{6,10},{7,11},{8,12},{9,13},{1... | collective-permute-start | bytes 1572872 | tf_op jit(solution)/shard_map/ppermute | solution.py:50
  72.1 16.3 %collective-permute-start.20 = (bf16[4,256,256]{2,1,0:T(8,128)(2,1)S(1)}, bf16[4,256,256]{2,1,0:T(8,128)(2,1)S(1)}, u32[]{:S(2)}, u32[]{:S(2)}) collective-permute-start(bf16[4,256,256]{2,1,0:T(8,128)(2,1)S(1)} %get-tuple-element.44), channel_id=1, source_target_pairs={{0,12},{1,13},{2,14},{3,15},{4,0},{5,1},{6,2},{7,3},{8,4},{9,5},{1... | collective-permute-start | bytes 1572872 | tf_op jit(solution)/shard_map/ppermute | solution.py:50
  74.8 15.0 %collective-permute-start.29 = (bf16[4,256,256]{2,1,0:T(8,128)(2,1)S(1)}, bf16[4,256,256]{2,1,0:T(8,128)(2,1)S(1)}, u32[]{:S(2)}, u32[]{:S(2)}) collective-permute-start(bf16[4,256,256]{2,1,0:T(8,128)(2,1)S(1)} %get-tuple-element.56), channel_id=1, source_target_pairs={{0,1},{1,2},{2,3},{3,0},{4,5},{5,6},{6,7},{7,4},{8,9},{9,10},{10,1... | collective-permute-start | bytes 1572872 | tf_op jit(solution)/shard_map/ppermute | solution.py:50
  75.4 15.4 %collective-permute-start.30 = (bf16[4,256,256]{2,1,0:T(8,128)(2,1)S(1)}, bf16[4,256,256]{2,1,0:T(8,128)(2,1)S(1)}, u32[]{:S(2)}, u32[]{:S(2)}) collective-permute-start(bf16[4,256,256]{2,1,0:T(8,128)(2,1)S(1)} %get-tuple-element.57), channel_id=1, source_target_pairs={{0,3},{1,0},{2,1},{3,2},{4,7},{5,4},{6,5},{7,6},{8,11},{9,8},{10,9... | collective-permute-start | bytes 1572872 | tf_op jit(solution)/shard_map/ppermute | solution.py:50
  78.0 1.2 collective-permute-start.22
  86.4 14.1 %collective-permute-start.23 = (bf16[4,256,256]{2,1,0:T(8,128)(2,1)S(1)}, bf16[4,256,256]{2,1,0:T(8,128)(2,1)S(1)}, u32[]{:S(2)}, u32[]{:S(2)}) collective-permute-start(bf16[4,256,256]{2,1,0:T(8,128)(2,1)S(1)} %get-tuple-element.50), channel_id=1, source_target_pairs={{0,12},{1,13},{2,14},{3,15},{4,0},{5,1},{6,2},{7,3},{8,4},{9,5},{1... | collective-permute-start | bytes 1572872 | tf_op jit(solution)/shard_map/ppermute | solution.py:50
  87.2 16.0 %collective-permute-start.24 = (bf16[4,256,256]{2,1,0:T(8,128)(2,1)S(1)}, bf16[4,256,256]{2,1,0:T(8,128)(2,1)S(1)}, u32[]{:S(2)}, u32[]{:S(2)}) collective-permute-start(bf16[4,256,256]{2,1,0:T(8,128)(2,1)S(1)} %get-tuple-element.51), channel_id=1, source_target_pairs={{0,4},{1,5},{2,6},{3,7},{4,8},{5,9},{6,10},{7,11},{8,12},{9,13},{1... | collective-permute-start | bytes 1572872 | tf_op jit(solution)/shard_map/ppermute | solution.py:50
  88.5 14.9 %collective-permute-start.32 = (bf16[4,256,256]{2,1,0:T(8,128)(2,1)S(1)}, bf16[4,256,256]{2,1,0:T(8,128)(2,1)S(1)}, u32[]{:S(2)}, u32[]{:S(2)}) collective-permute-start(bf16[4,256,256]{2,1,0:T(8,128)(2,1)S(1)} %get-tuple-element.62), channel_id=1, source_target_pairs={{0,3},{1,0},{2,1},{3,2},{4,7},{5,4},{6,5},{7,6},{8,11},{9,8},{10,9... | collective-permute-start | bytes 1572872 | tf_op jit(solution)/shard_map/ppermute | solution.py:50
  89.8 14.9 %collective-permute-start.33 = (bf16[4,256,256]{2,1,0:T(8,128)(2,1)S(1)}, bf16[4,256,256]{2,1,0:T(8,128)(2,1)S(1)}, u32[]{:S(2)}, u32[]{:S(2)}) collective-permute-start(bf16[4,256,256]{2,1,0:T(8,128)(2,1)S(1)} %get-tuple-element.63), channel_id=1, source_target_pairs={{0,1},{1,2},{2,3},{3,0},{4,5},{5,6},{6,7},{7,4},{8,9},{9,10},{10,1... | collective-permute-start | bytes 1572872 | tf_op jit(solution)/shard_map/ppermute | solution.py:50
  90.7 22.6 %collective-permute-start.21 = (bf16[4,256,256]{2,1,0:T(8,128)(2,1)S(1)}, bf16[4,256,256]{2,1,0:T(8,128)(2,1)S(1)}, u32[]{:S(2)}, u32[]{:S(2)}) collective-permute-start(bf16[4,256,256]{2,1,0:T(8,128)(2,1)S(1)} %add_convert_fusion.3), channel_id=1, source_target_pairs={{0,4},{1,5},{2,6},{3,7},{4,8},{5,9},{6,10},{7,11},{8,12},{9,13},{1... | collective-permute-start | bytes 1572872 | tf_op jit(solution)/shard_map/ppermute | solution.py:50
  100.4 14.9 %collective-permute-start.31 = (bf16[4,256,256]{2,1,0:T(8,128)(2,1)S(1)}, bf16[4,256,256]{2,1,0:T(8,128)(2,1)S(1)}, u32[]{:S(2)}, u32[]{:S(2)}) collective-permute-start(bf16[4,256,256]{2,1,0:T(8,128)(2,1)S(1)} %add_convert_fusion.1), channel_id=1, source_target_pairs={{0,1},{1,2},{2,3},{3,0},{4,5},{5,6},{6,7},{7,4},{8,9},{9,10},{10,1... | collective-permute-start | bytes 1572872 | tf_op jit(solution)/shard_map/ppermute | solution.py:50
  103.3 12.3 %collective-permute-start.25 = (bf16[4,256,256]{2,1,0:T(8,128)(2,1)S(1)}, bf16[4,256,256]{2,1,0:T(8,128)(2,1)S(1)}, u32[]{:S(2)}, u32[]{:S(2)}) collective-permute-start(bf16[4,256,256]{2,1,0:T(8,128)(2,1)S(1)} %add_convert_fusion.2), channel_id=1, source_target_pairs={{0,12},{1,13},{2,14},{3,15},{4,0},{5,1},{6,2},{7,3},{8,4},{9,5},{1... | collective-permute-start | bytes 1572872 | tf_op jit(solution)/shard_map/ppermute | solution.py:50
  104.8 15.6 %collective-permute-start.34 = (bf16[4,256,256]{2,1,0:T(8,128)(2,1)S(1)}, bf16[4,256,256]{2,1,0:T(8,128)(2,1)S(1)}, u32[]{:S(2)}, u32[]{:S(2)}) collective-permute-start(bf16[4,256,256]{2,1,0:T(8,128)(2,1)S(1)} %add_convert_fusion), channel_id=1, source_target_pairs={{0,3},{1,0},{2,1},{3,2},{4,7},{5,4},{6,5},{7,6},{8,11},{9,8},{10,9... | collective-permute-start | bytes 1572872 | tf_op jit(solution)/shard_map/ppermute | solution.py:50
  115.6 14.0 %copy-start.11 = (s32[4]{0:T(128)S(1)}, s32[4]{0:T(128)}, u32[]{:S(2)}) copy-start(s32[4]{0:T(128)} %param.14) | copy-start | bytes 52
  115.8 10.8 %collective-permute-start.26 = (bf16[2,256,256]{2,1,0:T(8,128)(2,1)S(1)}, bf16[2,256,256]{2,1,0:T(8,128)(2,1)S(1)}, u32[]{:S(2)}, u32[]{:S(2)}) collective-permute-start(bf16[2,256,256]{2,1,0:T(8,128)(2,1)S(1)} %pad_maximum_fusion), channel_id=1, source_target_pairs={{0,2},{1,3},{2,0},{3,1},{4,6},{5,7},{6,4},{7,5},{8,10},{9,11},{10,... | collective-permute-start | bytes 786440 | tf_op jit(solution)/shard_map/ppermute | solution.py:50
  117.0 13.0 %collective-permute-start.27 = (bf16[2,256,256]{2,1,0:T(8,128)(2,1)S(1)}, bf16[2,256,256]{2,1,0:T(8,128)(2,1)S(1)}, u32[]{:S(2)}, u32[]{:S(2)}) collective-permute-start(bf16[2,256,256]{2,1,0:T(8,128)(2,1)S(1)} %pad_maximum_fusion.1), channel_id=1, source_target_pairs={{0,1},{1,2},{2,3},{3,0},{4,5},{5,6},{6,7},{7,4},{8,9},{9,10},{10,1... | collective-permute-start | bytes 786440 | tf_op jit(solution)/shard_map/ppermute | solution.py:50
  118.3 11.8 %collective-permute-start.28 = (bf16[2,256,256]{2,1,0:T(8,128)(2,1)S(1)}, bf16[2,256,256]{2,1,0:T(8,128)(2,1)S(1)}, u32[]{:S(2)}, u32[]{:S(2)}) collective-permute-start(bf16[2,256,256]{2,1,0:T(8,128)(2,1)S(1)} %pad_maximum_fusion.2), channel_id=1, source_target_pairs={{0,3},{1,0},{2,1},{3,2},{4,7},{5,4},{6,5},{7,6},{8,11},{9,8},{10,9... | collective-permute-start | bytes 786440 | tf_op jit(solution)/shard_map/ppermute | solution.py:50
  120.7 10.0 %collective-permute-start.35 = (bf16[2,256,256]{2,1,0:T(8,128)(2,1)S(1)}, bf16[2,256,256]{2,1,0:T(8,128)(2,1)S(1)}, u32[]{:S(2)}, u32[]{:S(2)}) collective-permute-start(bf16[2,256,256]{2,1,0:T(8,128)(2,1)S(1)} %pad_maximum_fusion.3), channel_id=1, source_target_pairs={{0,8},{1,9},{2,10},{3,11},{4,12},{5,13},{6,14},{7,15},{8,0},{9,1},... | collective-permute-start | bytes 786440 | tf_op jit(solution)/shard_map/ppermute | solution.py:50
  122.1 11.3 %collective-permute-start.36 = (bf16[2,256,256]{2,1,0:T(8,128)(2,1)S(1)}, bf16[2,256,256]{2,1,0:T(8,128)(2,1)S(1)}, u32[]{:S(2)}, u32[]{:S(2)}) collective-permute-start(bf16[2,256,256]{2,1,0:T(8,128)(2,1)S(1)} %pad_maximum_fusion.4), channel_id=1, source_target_pairs={{0,4},{1,5},{2,6},{3,7},{4,8},{5,9},{6,10},{7,11},{8,12},{9,13},{1... | collective-permute-start | bytes 786440 | tf_op jit(solution)/shard_map/ppermute | solution.py:50
  126.7 7.1 %collective-permute-start.37 = (bf16[2,256,256]{2,1,0:T(8,128)(2,1)S(1)}, bf16[2,256,256]{2,1,0:T(8,128)(2,1)S(1)}, u32[]{:S(2)}, u32[]{:S(2)}) collective-permute-start(bf16[2,256,256]{2,1,0:T(8,128)(2,1)S(1)} %pad_maximum_fusion.5), channel_id=1, source_target_pairs={{0,12},{1,13},{2,14},{3,15},{4,0},{5,1},{6,2},{7,3},{8,4},{9,5},{1... | collective-permute-start | bytes 786440 | tf_op jit(solution)/shard_map/ppermute | solution.py:50
